TPU v7x, 32 devices: a whole 2x2x4 slice. The times are simulated.
32 devices in a mesh: blk: 8 (over z, y), rep: 4 (over x, core).
Axes of the slice: x: 2, y: 2, z: 4, core: 2. Of those that a mesh axis runs over, the one named last changes fastest.
Arguments:
- point_xyz: float32 [3, 16384], P(None, ('blk', 'rep')), may hold values from -6 to 6
- point_attrs: float32 [5, 16384], P(None, ('blk', 'rep')), may hold values from -6 to 6
- scan_yaw: float32 [32], P(('blk', 'rep')), may hold values from -3.140625 to 3.140625
- scan_jitter: float32 [32, 3], P(('blk', 'rep')), may hold values from -0.5 to 0.5
- slot_counts: int32 [32, 8], P(('blk', 'rep')), may hold values from 0 to 64, as said below
- voxel_ids: int32 [16384], P(('blk', 'rep')), may hold values from 0 to 511
- point_weight: float32 [8, 96], replicated, may hold values from -2 to 2
- point_bias: float32 [96], replicated, may hold values from -3 to 3
- conv_one: bfloat16 [2592, 96], replicated, may hold values from -0.1875 to 0.1875
- conv_two: bfloat16 [2592, 128], replicated, may hold values from -0.1875 to 0.1875
- out_grad: bfloat16 [32, 64, 1024], P('rep', 'blk'), may hold values from -6 to 6
Outputs:
- block_out: bfloat16 [32, 64, 1024], P('rep', 'blk')
- attr_grad: float32 [5, 16384], P(None, ('blk', 'rep'))
- jitter_grad: float32 [32, 3], P(('blk', 'rep'))
- conv_one_grad: float32 [2592, 96], replicated
- conv_two_grad: float32 [2592, 128], replicated
Inputs may be any that keep to these rules, and one draw needn't show every extreme that they name: `slot_counts`: used slots out of 64; in every draw some voxel block receives 64 points from every scan of its slab. `voxel_ids`: voxel (x * 8 + y) * 8 + z inside the destination block; entries of unused slots are ignored.
All inputs are finite; a program needn't handle non-finite values.
Results may differ from a plain program's by a relative error of at most 0.006.
Values may be sent and summed in bfloat16 or wider, within the bound.
No kernel may reach another device: no remote copies, remote signals or barrier semaphores. Data moves between devices by JAX's collectives and lax.ppermute only.
A program may use at most 64 MiB of HBM per device.

v0:
```python
import jax
import jax.numpy as jnp
from jax import lax
from jax.sharding import PartitionSpec as P

SLOT_CAP = 64


def with_halo(cells, sides, width):
    for axis, dim in sides:
        count = lax.axis_size(axis)
        ends = count - 1
        head = lax.slice_in_dim(cells, 0, width, axis=dim)
        tail = lax.slice_in_dim(cells, cells.shape[dim] - width, cells.shape[dim], axis=dim)
        cells = jnp.concatenate(
            [
                lax.ppermute(tail, axis, [(i, (i + 1) % count) for i in range(ends)]),
                cells,
                lax.ppermute(head, axis, [((i + 1) % count, i) for i in range(ends)]),
            ],
            axis=dim,
        )
    return cells


def silu_slope(value):
    sigmoid_v = jax.nn.sigmoid(value)
    return sigmoid_v * (1.0 + value * (1.0 - sigmoid_v))


def point_layer(inputs, point_weight, point_bias):
    return (
        lax.dot_general(
            inputs, point_weight, (((0,), (0,)), ((), ())), precision=lax.Precision.HIGHEST
        )
        + point_bias
    )


def back_layer(grad_pre, point_weight):
    return lax.dot_general(
        point_weight, grad_pre, (((1,), (1,)), ((), ())), precision=lax.Precision.HIGHEST
    )


def with_faces(volume, channels):
    padded = with_halo(volume, (("blk", 1), ("rep", 0)), 1)
    shaped = padded.reshape(padded.shape[0], padded.shape[1], -1, channels)
    return jnp.pad(shaped, ((0, 0), (0, 0), (1, 1), (0, 0)))


def conv_apply(padded, weight, channels_in):
    kernel = weight.reshape(3, 3, 3, channels_in, weight.shape[1])
    result = lax.conv_general_dilated(
        padded[None],
        kernel,
        (1, 1, 1),
        "VALID",
        dimension_numbers=("NDHWC", "DHWIO", "NDHWC"),
        preferred_element_type=jnp.float32,
    )[0]
    return result.reshape(-1, weight.shape[1])


def kernel_grad(padded, partner, edge_len):
    channels_in = padded.shape[-1]
    channels_out = partner.shape[-1]
    source = jnp.transpose(padded, (3, 0, 1, 2))[..., None]
    target = partner.reshape(edge_len, edge_len, edge_len, 1, channels_out)
    result = lax.conv_general_dilated(
        source,
        target,
        (1, 1, 1),
        "VALID",
        dimension_numbers=("NDHWC", "DHWIO", "NDHWC"),
        preferred_element_type=jnp.float32,
    )
    return jnp.transpose(result, (1, 2, 3, 0, 4)).reshape(27 * channels_in, channels_out)


def flipped(weight, channels_in):
    taps = weight.reshape(3, 3, 3, channels_in, -1)[::-1, ::-1, ::-1]
    return jnp.swapaxes(taps, 3, 4).reshape(-1, channels_in)


def shards(
    point_xyz,
    point_attrs,
    scan_yaw,
    scan_jitter,
    slot_counts,
    voxel_ids,
    point_weight,
    point_bias,
    conv_one,
    conv_two,
    out_grad,
):
    owners = lax.axis_size("blk")
    edge_len = out_grad.shape[0]
    voxels = edge_len**3
    width_one = conv_one.shape[1]
    width_two = conv_two.shape[1]
    slot_index = lax.broadcasted_iota(jnp.int32, (owners, SLOT_CAP), 1)
    filled = slot_index < slot_counts[0][:, None]
    vox_sent = jnp.where(filled, voxel_ids.reshape(owners, SLOT_CAP), voxels)
    cos_yaw = jnp.cos(scan_yaw[0])
    sin_yaw = jnp.sin(scan_yaw[0])
    rotated_x = cos_yaw * point_xyz[0] - sin_yaw * point_xyz[1] + scan_jitter[0, 0]
    rotated_y = sin_yaw * point_xyz[0] + cos_yaw * point_xyz[1] + scan_jitter[0, 1]
    rotated_z = point_xyz[2] + scan_jitter[0, 2]
    inputs = jnp.concatenate([jnp.stack([rotated_x, rotated_y, rotated_z]), point_attrs], axis=0)
    pre_act = point_layer(inputs, point_weight, point_bias)
    local_feat = jax.nn.silu(pre_act).astype(jnp.bfloat16).reshape(owners, SLOT_CAP, width_one)
    incoming, vox_rows = (
        lax.all_to_all(local_feat, "blk", split_axis=0, concat_axis=0, tiled=True),
        lax.all_to_all(vox_sent, "blk", split_axis=0, concat_axis=0, tiled=True),
    )
    features = incoming.reshape(-1, width_one)
    vox_flat = vox_rows.reshape(-1)
    counts = jax.ops.segment_sum(jnp.ones_like(vox_flat), vox_flat, voxels + 1)[:voxels]
    divisor = jnp.maximum(counts, 1).astype(jnp.float32)
    totals = jax.ops.segment_sum(features.astype(jnp.float32), vox_flat, voxels + 1)[:voxels]
    pooled = lax.optimization_barrier((totals / divisor[:, None]).astype(jnp.bfloat16))
    occupied = (counts > 0).astype(jnp.float32)[:, None]
    pooled_pad = with_faces(pooled.reshape(edge_len, edge_len, -1), width_one)
    act_one = conv_apply(pooled_pad, conv_one, width_one)
    hidden = (occupied * jax.nn.silu(act_one)).astype(jnp.bfloat16)
    hidden_pad = with_faces(hidden.reshape(edge_len, edge_len, -1), width_one)
    out_two = conv_apply(hidden_pad, conv_two, width_one)
    block_out = (occupied * out_two).astype(jnp.bfloat16).reshape(edge_len, edge_len, -1)
    grad_two = jnp.where(
        occupied > 0, out_grad.reshape(voxels, width_two), jnp.zeros((), jnp.bfloat16)
    )
    grad_two_pad = with_faces(grad_two.reshape(edge_len, edge_len, -1), width_two)
    grad_hidden = conv_apply(grad_two_pad, flipped(conv_two, width_one), width_two)
    part_two = kernel_grad(hidden_pad, grad_two, edge_len)
    grad_act = (occupied * grad_hidden * silu_slope(act_one)).astype(jnp.bfloat16)
    grad_act_pad = with_faces(grad_act.reshape(edge_len, edge_len, -1), width_one)
    grad_pooled = conv_apply(grad_act_pad, flipped(conv_one, width_one), width_one)
    part_one = kernel_grad(pooled_pad, grad_act, edge_len)
    one_total, two_total = lax.psum((part_one, part_two), ("blk", "rep"))
    grad_ext = jnp.concatenate([grad_pooled, jnp.zeros((1, width_one), jnp.float32)], axis=0)
    count_ext = jnp.concatenate([divisor, jnp.ones((1,), jnp.float32)])
    grad_feat = grad_ext[vox_flat] / count_ext[vox_flat][:, None]
    returned = lax.all_to_all(
        grad_feat.reshape(owners, SLOT_CAP, width_one),
        "blk",
        split_axis=0,
        concat_axis=0,
        tiled=True,
    )
    grad_pre = returned.reshape(-1, width_one) * silu_slope(pre_act)
    grad_inputs = back_layer(grad_pre, point_weight)
    attr_grad = grad_inputs[3:]
    jitter_grad = jnp.sum(grad_inputs[:3], axis=1)[None, :]
    return (block_out, attr_grad, jitter_grad, one_total, two_total)


def solution(mesh):
    in_specs = (
        P(None, ("blk", "rep")),
        P(None, ("blk", "rep")),
        P(("blk", "rep")),
        P(("blk", "rep"), None),
        P(("blk", "rep"), None),
        P(("blk", "rep")),
        P(),
        P(),
        P(),
        P(),
        P("rep", "blk", None),
    )
    out_specs = (P("rep", "blk", None), P(None, ("blk", "rep")), P(("blk", "rep"), None), P(), P())
    return jax.shard_map(shards, mesh=mesh, in_specs=in_specs, out_specs=out_specs, check_vma=False)
```

profile of v0, /device:TPU:0, one launch (start us, length us, event | category | flops | bytes accessed | tf_op | source)
XLA Modules:
  0.0 269.3 jit_solution(3016571241570396834)
XLA Ops:
  7.2 0.9 reshape.249
  8.0 1.3 compare_select_fusion
  9.4 7.3 %all-to-all-start = ((s32[8,1,64]{2,1,0:T(1,128)}), s32[8,1,64]{2,1,0:T(1,128)S(1)}, u32[]{:S(2)}, u32[]{:S(2)}) async-start(s32[8,1,64]{2,1,0:T(1,128)} %compare_select_fusion), calls=%async_computation | async-start | bytes 8192 | tf_op jit(solution)/shard_map/all_to_all | solution.py:117
  17.5 1.4 fusion.41
  18.8 2.8 %subtract_add_fusion = (f32[1,512]{1,0:T(1,128)S(1)}, f32[1,512]{1,0:T(1,128)S(1)}, f32[1,512]{1,0:T(1,128)S(1)}) fusion(f32[3,512]{1,0:T(4,128)} %param.11, f32[]{:T(128)} %bitcast.4, f32[]{:T(128)} %bitcast.3, f32[]{:T(128)} %bitcast.2, f32[]{:T(128)} %bitcast.5, f32[]{:T(128)} %bitcast.6), kind=kLoop, calls=%fused_computation.81 | loop fusion | flops 4608 | bytes 12308 | tf_op jit(solution)/shard_map/add | solution.py:109
  21.6 1.8 multiply_convert_fusion.3
  23.4 0.8 copy.39
  24.2 0.3 copy.40
  24.5 6.0 %all-to-all-start.1 = ((bf16[8,64,96]{2,1,0:T(8,128)(2,1)}), bf16[8,64,96]{2,1,0:T(8,128)(2,1)S(1)}, u32[]{:S(2)}, u32[]{:S(2)}) async-start(bf16[8,64,96]{2,1,0:T(8,128)(2,1)} %bitcast.7), calls=%async_computation.1 | async-start | bytes 262144 | tf_op jit(solution)/shard_map/all_to_all | solution.py:116
  30.6 0.5 broadcast.171
  31.1 0.7 reduce.15
  31.9 4.1 %scatter_custom_fusion = s32[513]{0:T(1024)S(1)} fusion(s32[512]{0:T(512)S(1)} %reshape.282, s32[512]{0:T(512)S(1)} %broadcast.146, s32[]{:T(128)} %constant.8.clone.1), kind=kCustom, calls=%fused_computation.82 | custom fusion | flops 512 | bytes 2056 | tf_op jit(solution)/shard_map/scatter-add | solution.py:121
  36.3 0.1 bitcast_select_fusion
  36.5 3.9 %collective-permute-start.8 = (bf16[8,1,1024]{2,1,0:T(2,128)(2,1)S(1)}, bf16[8,1,1024]{2,1,0:T(2,128)(2,1)S(1)}, u32[]{:S(2)}, u32[]{:S(2)}) collective-permute-start(bf16[8,1,1024]{2,1,0:T(2,128)(2,1)S(1)} %get-tuple-element.21), channel_id=1, source_target_pairs={{0,4},{4,8},{8,12},{12,16},{16,20},{20,24},{24,28},{1,5},{5,9},{9,... | collective-permute-start | bytes 49160 | tf_op jit(solution)/shard_map/ppermute | solution.py:17
  40.3 1.3 collective-permute-start.9
  41.7 0.3 collective-permute-done.8
  41.9 4.2 %collective-permute-done.9 = bf16[8,1,1024]{2,1,0:T(2,128)(2,1)S(1)} collective-permute-done((bf16[8,1,1024]{2,1,0:T(2,128)(2,1)S(1)}, bf16[8,1,1024]{2,1,0:T(2,128)(2,1)S(1)}, u32[]{:S(2)}, u32[]{:S(2)}) %collective-permute-start.9) | collective-permute-done | bytes 16416 | tf_op jit(solution)/shard_map/ppermute | solution.py:19
  46.2 1.3 collective-permute-start.10
  47.5 1.3 collective-permute-start.11
  48.8 0.7 copy.38
  49.5 2.3 gather_fusion.1
  51.8 0.7 div.43
  53.0 3.0 %scatter_custom_fusion.1 = f32[513,96]{1,0:T(8,128)S(1)} fusion(s32[512]{0:T(512)S(1)} %reshape.282, bf16[512,96]{1,0:T(8,128)(2,1)S(1)} %bitcast.68, f32[]{:T(128)} %constant.11.clone.1), kind=kCustom, calls=%fused_computation.28 | custom fusion | flops 98304 | bytes 328068 | tf_op jit(solution)/shard_map/scatter-add | solution.py:123
  56.0 0.1 fusion.11
  56.3 4.3 %collective-permute-start = (bf16[8,1,768]{2,1,0:T(2,128)(2,1)S(1)}, bf16[8,1,768]{2,1,0:T(2,128)(2,1)S(1)}, u32[]{:S(2)}, u32[]{:S(2)}) collective-permute-start(bf16[8,1,768]{2,1,0:T(2,128)(2,1)S(1)} %get-tuple-element.27), channel_id=1, source_target_pairs={{0,4},{4,8},{8,12},{12,16},{16,20},{20,24},{24,28},{1,5},{5,9},{9,... | collective-permute-start | bytes 36872 | tf_op jit(solution)/shard_map/ppermute | solution.py:17
  60.6 1.3 collective-permute-start.1
  62.1 4.2 %collective-permute-done.1 = bf16[8,1,768]{2,1,0:T(2,128)(2,1)S(1)} collective-permute-done((bf16[8,1,768]{2,1,0:T(2,128)(2,1)S(1)}, bf16[8,1,768]{2,1,0:T(2,128)(2,1)S(1)}, u32[]{:S(2)}, u32[]{:S(2)}) %collective-permute-start.1) | collective-permute-done | bytes 12320 | tf_op jit(solution)/shard_map/ppermute | solution.py:19
  66.4 3.6 %collective-permute-start.2 = (bf16[1,10,768]{2,1,0:T(8,128)(2,1)S(1)}, bf16[1,10,768]{2,1,0:T(8,128)(2,1)S(1)}, u32[]{:S(2)}, u32[]{:S(2)}) collective-permute-start(bf16[1,10,768]{2,1,0:T(8,128)(2,1)S(1)} %get-tuple-element.19), channel_id=1, source_target_pairs={{0,1},{1,2},{2,3},{4,5},{5,6},{6,7},{8,9},{9,10},{10,11},{12,13},{... | collective-permute-start | bytes 46088 | tf_op jit(solution)/shard_map/ppermute | solution.py:17
  70.0 1.5 collective-permute-start.3
  71.5 0.5 broadcast.172
  72.0 4.0 %fusion.43 = (f32[8,8,8,96]{3,2,1,0:T(8,128)S(1)}, f32[1,8,8,8,96]{4,0,3,2,1:T(1,128)S(1)}) fusion(f32[]{:T(128)} %broadcast.172, bf16[3,3,3,96,128]{4,3,2,1,0:T(8,128)(2,1)S(1)} %bitcast.61, bf16[1,10,10,10,128]{4,3,2,1,0:T(8,128)(2,1)S(1)} %pad_bitcast_fusion.5), kind=kOutput, calls=%fused_computation.94 | convolution fusion | flops 339738624 | bytes 1312772 | tf_op jit(solution)/shard_map/conv_general_dilated | solution.py:54
  76.3 0.3 reshape.252
  76.6 0.1 pad_bitcast_fusion.2
  76.7 4.2 %fusion.42 = (f32[8,8,8,96]{3,2,1,0:T(8,128)S(1)}, f32[1,8,8,8,96]{4,0,3,2,1:T(1,128)S(1)}) fusion(f32[]{:T(128)} %broadcast.172, bf16[3,3,3,96,96]{4,3,2,1,0:T(8,128)(2,1)S(1)} %bitcast.66, bf16[1,10,10,10,96]{4,3,2,1,0:T(8,128)(2,1)S(1)} %get-tuple-element.12), kind=kOutput, calls=%fused_computation.93 | convolution fusion | flops 254803968 | bytes 1082884 | tf_op jit(solution)/shard_map/conv_general_dilated | solution.py:54
  81.2 3.1 %collective-permute-start.12 = (bf16[8,1,768]{2,1,0:T(2,128)(2,1)S(1)}, bf16[8,1,768]{2,1,0:T(2,128)(2,1)S(1)}, u32[]{:S(2)}, u32[]{:S(2)}) collective-permute-start(bf16[8,1,768]{2,1,0:T(2,128)(2,1)S(1)} %get-tuple-element.23), channel_id=1, source_target_pairs={{0,4},{4,8},{8,12},{12,16},{16,20},{20,24},{24,28},{1,5},{5,9},{9,... | collective-permute-start | bytes 36872 | tf_op jit(solution)/shard_map/ppermute | solution.py:17
  84.4 1.3 collective-permute-start.13
  85.7 4.5 %collective-permute-start.4 = (bf16[8,1,768]{2,1,0:T(2,128)(2,1)S(1)}, bf16[8,1,768]{2,1,0:T(2,128)(2,1)S(1)}, u32[]{:S(2)}, u32[]{:S(2)}) collective-permute-start(bf16[8,1,768]{2,1,0:T(2,128)(2,1)S(1)} %get-tuple-element.25), channel_id=1, source_target_pairs={{0,4},{4,8},{8,12},{12,16},{16,20},{20,24},{24,28},{1,5},{5,9},{9,... | collective-permute-start | bytes 36872 | tf_op jit(solution)/shard_map/ppermute | solution.py:17
  90.3 1.3 collective-permute-start.5
  91.6 0.1 multiply_convert_fusion
  91.7 3.6 %fusion.2 = f32[3,3,3,96,96]{4,3,2,1,0:T(8,128)S(1)} fusion(bf16[96,10,10,10,1]{0,3,4,2,1:T(8,128)(2,1)S(1)} %get-tuple-element.11, bf16[8,8,8,1,96]{4,2,1,0,3:T(8,128)(2,1)S(1)} %multiply_convert_fusion), kind=kOutput, calls=%fused_computation.10 | convolution fusion | flops 254803968 | bytes 1285632 | tf_op jit(solution)/shard_map/transpose | solution.py:78
  95.3 1.4 copy.49
  96.7 4.9 %collective-permute-start.14 = (bf16[1,10,768]{2,1,0:T(8,128)(2,1)S(1)}, bf16[1,10,768]{2,1,0:T(8,128)(2,1)S(1)}, u32[]{:S(2)}, u32[]{:S(2)}) collective-permute-start(bf16[1,10,768]{2,1,0:T(8,128)(2,1)S(1)} %get-tuple-element.15), channel_id=1, source_target_pairs={{0,1},{1,2},{2,3},{4,5},{5,6},{6,7},{8,9},{9,10},{10,11},{12,13},{... | collective-permute-start | bytes 46088 | tf_op jit(solution)/shard_map/ppermute | solution.py:17
  101.6 1.3 collective-permute-start.15
  102.9 5.1 %collective-permute-start.6 = (bf16[1,10,768]{2,1,0:T(8,128)(2,1)S(1)}, bf16[1,10,768]{2,1,0:T(8,128)(2,1)S(1)}, u32[]{:S(2)}, u32[]{:S(2)}) collective-permute-start(bf16[1,10,768]{2,1,0:T(8,128)(2,1)S(1)} %get-tuple-element.17), channel_id=1, source_target_pairs={{0,1},{1,2},{2,3},{4,5},{5,6},{6,7},{8,9},{9,10},{10,11},{12,13},{... | collective-permute-start | bytes 46088 | tf_op jit(solution)/shard_map/ppermute | solution.py:17
  108.1 1.5 collective-permute-start.7
  109.7 0.3 reshape.257
  110.0 2.4 collective-permute-done.7
  112.5 0.3 reshape.254
  112.9 0.1 pad_bitcast_fusion
  113.0 4.9 %fusion = f32[3,3,3,96,128]{4,3,2,1,0:T(8,128)} fusion(bf16[96,10,10,10,1]{0,3,4,2,1:T(8,128)(2,1)S(1)} %get-tuple-element.9, pred[8,8,8]{2,1,0:T(8,128)(4,1)S(1)} %broadcast_compare_fusion, bf16[8,8,8,1,128]{4,1,2,0,3:T(8,128)(2,1)S(1)} %bitcast.72), kind=kOutput, calls=%fused_computation.8 | convolution fusion | flops 339804160 | bytes 1650688 | tf_op jit(solution)/shard_map/transpose | solution.py:78
  118.0 1.1 copy-done.3
  119.0 5.5 %fusion.4 = f32[1,8,8,8,96]{4,0,3,2,1:T(1,128)S(1)} fusion(bf16[3,3,3,96,96]{4,3,2,1,0:T(8,128)(2,1)S(1)} %bitcast.67, bf16[1,10,10,10,96]{4,3,2,1,0:T(8,128)(2,1)S(1)} %pad_bitcast_fusion.4), kind=kOutput, calls=%fused_computation.12 | convolution fusion | flops 254803968 | bytes 886272 | tf_op jit(solution)/shard_map/conv_general_dilated | solution.py:54
  124.5 1.0 gather_fusion
  125.6 0.9 broadcast_divide_fusion
  126.5 6.2 %all-to-all-start.2 = ((f32[8,64,96]{2,1,0:T(8,128)}), f32[8,64,96]{2,1,0:T(8,128)S(1)}, u32[]{:S(2)}, u32[]{:S(2)}) async-start(f32[8,64,96]{2,1,0:T(8,128)} %broadcast_divide_fusion), calls=%async_computation.2 | async-start | bytes 524288 | tf_op jit(solution)/shard_map/all_to_all | solution.py:146
  132.6 3.4 %convolution_reduce_fusion = f32[8,8,8,128]{3,2,1,0:T(8,128)S(1)} fusion(bf16[3,3,3,96,128]{4,3,2,1,0:T(8,128)(2,1)S(1)} %bitcast.60, bf16[1,10,10,10,96]{4,3,2,1,0:T(8,128)(2,1)S(1)} %get-tuple-element.10), kind=kOutput, calls=%fused_computation.4 | convolution fusion | flops 339738624 | bytes 1117696 | tf_op jit(solution)/shard_map/conv_general_dilated | solution.py:54
  136.1 0.8 fusion.14
  136.9 6.8 %all-to-all-done.2 = f32[8,64,96]{2,1,0:T(8,128)S(1)} async-done(((f32[8,64,96]{2,1,0:T(8,128)}), f32[8,64,96]{2,1,0:T(8,128)S(1)}, u32[]{:S(2)}, u32[]{:S(2)}) %all-to-all-start.2) | async-done | bytes 196640 | tf_op jit(solution)/shard_map/all_to_all | solution.py:146
  143.9 0.3 convolution_bitcast_fusion
  144.2 0.6 slice.119
  144.8 0.6 slice_reduce_fusion
  145.4 113.6 %all-reduce.8.cloned.1.call-done = (f32[2592,96]{0,1:T(8,128)}, f32[2592,128]{1,0:T(8,128)}) async-done(((f32[2592,96]{0,1:T(8,128)}, f32[2592,128]{1,0:T(8,128)}), (f32[2592,96]{0,1:T(8,128)}, f32[2592,128]{1,0:T(8,128)})) %all-reduce.8.cloned.1.call-update) | async-done | bytes 2322448 | tf_op jit(solution)/shard_map/psum | solution.py:142
  259.0 2.3 copy.77
  261.4 1.1 copy.78
  (74 shorter events, 2.6 us)
Async XLA Ops:
  7.2 64.4 %copy-start = (bf16[2592,128]{1,0:T(8,128)(2,1)S(1)}, bf16[2592,128]{1,0:T(8,128)(2,1)}, u32[]{:S(2)}) copy-start(bf16[2592,128]{1,0:T(8,128)(2,1)} %param.20) | copy-start | bytes 1990660
  7.2 17.0 %copy-start.4 = (bf16[2592,96]{0,1:T(8,128)(2,1)S(1)}, bf16[2592,96]{0,1:T(8,128)(2,1)}, u32[]{:S(2)}) copy-start(bf16[2592,96]{0,1:T(8,128)(2,1)} %param.19) | copy-start | bytes 1492996
  9.4 15.2 %all-to-all-start = ((s32[8,1,64]{2,1,0:T(1,128)}), s32[8,1,64]{2,1,0:T(1,128)S(1)}, u32[]{:S(2)}, u32[]{:S(2)}) async-start(s32[8,1,64]{2,1,0:T(1,128)} %compare_select_fusion), calls=%async_computation | async-start | bytes 8192 | tf_op jit(solution)/shard_map/all_to_all | solution.py:117
  21.6 14.7 %copy-start.5 = (bf16[8,8,1024]{2,1,0:T(8,128)(2,1)S(1)}, bf16[8,8,1024]{2,1,0:T(8,128)(2,1)}, u32[]{:S(2)}) copy-start(bf16[8,8,1024]{2,1,0:T(8,128)(2,1)} %param.21) | copy-start | bytes 393220
  24.5 52.2 %copy-start.2 = (bf16[2592,96]{1,0:T(8,128)(2,1)}, bf16[2592,96]{1,0:T(8,128)(2,1)S(1)}, u32[]{:S(2)}) copy-start(bf16[2592,96]{1,0:T(8,128)(2,1)S(1)} %copy.40) | copy-start | bytes 1492996
  24.5 28.5 %all-to-all-start.1 = ((bf16[8,64,96]{2,1,0:T(8,128)(2,1)}), bf16[8,64,96]{2,1,0:T(8,128)(2,1)S(1)}, u32[]{:S(2)}, u32[]{:S(2)}) async-start(bf16[8,64,96]{2,1,0:T(8,128)(2,1)} %bitcast.7), calls=%async_computation.1 | async-start | bytes 262144 | tf_op jit(solution)/shard_map/all_to_all | solution.py:116
  30.5 228.5 %all-reduce.8.cloned.1.call-start = ((), (), s32[]{:S(2)}) async-start(), calls=%async_computation.3 | async-start | bytes 4718592 | tf_op jit(solution)/shard_map/psum | solution.py:142
  36.5 5.5 %collective-permute-start.8 = (bf16[8,1,1024]{2,1,0:T(2,128)(2,1)S(1)}, bf16[8,1,1024]{2,1,0:T(2,128)(2,1)S(1)}, u32[]{:S(2)}, u32[]{:S(2)}) collective-permute-start(bf16[8,1,1024]{2,1,0:T(2,128)(2,1)S(1)} %get-tuple-element.21), channel_id=1, source_target_pairs={{0,4},{4,8},{8,12},{12,16},{16,20},{20,24},{24,28},{1,5},{5,9},{9,... | collective-permute-start | bytes 49160 | tf_op jit(solution)/shard_map/ppermute | solution.py:17
  40.3 5.8 %collective-permute-start.9 = (bf16[8,1,1024]{2,1,0:T(2,128)(2,1)S(1)}, bf16[8,1,1024]{2,1,0:T(2,128)(2,1)S(1)}, u32[]{:S(2)}, u32[]{:S(2)}) collective-permute-start(bf16[8,1,1024]{2,1,0:T(2,128)(2,1)S(1)} %get-tuple-element.22), channel_id=1, source_target_pairs={{4,0},{8,4},{12,8},{16,12},{20,16},{24,20},{28,24},{5,1},{9,5},{13... | collective-permute-start | bytes 49160 | tf_op jit(solution)/shard_map/ppermute | solution.py:19
  41.7 10.8 %copy-start.8 = (s32[1024]{0:T(1024)}, s32[1024]{0:T(1024)S(1)}, u32[]{:S(2)}) copy-start(s32[1024]{0:T(1024)S(1)} %pad_clamp_fusion) | copy-start | bytes 12292
  46.2 6.5 %collective-permute-start.10 = (bf16[1,10,1024]{2,1,0:T(8,128)(2,1)S(1)}, bf16[1,10,1024]{2,1,0:T(8,128)(2,1)S(1)}, u32[]{:S(2)}, u32[]{:S(2)}) collective-permute-start(bf16[1,10,1024]{2,1,0:T(8,128)(2,1)S(1)} %get-tuple-element.13), channel_id=1, source_target_pairs={{0,1},{1,2},{2,3},{4,5},{5,6},{6,7},{8,9},{9,10},{10,11},{12,13},{... | collective-permute-start | bytes 61448 | tf_op jit(solution)/shard_map/ppermute | solution.py:17
  47.5 5.2 %collective-permute-start.11 = (bf16[1,10,1024]{2,1,0:T(8,128)(2,1)S(1)}, bf16[1,10,1024]{2,1,0:T(8,128)(2,1)S(1)}, u32[]{:S(2)}, u32[]{:S(2)}) collective-permute-start(bf16[1,10,1024]{2,1,0:T(8,128)(2,1)S(1)} %get-tuple-element.14), channel_id=1, source_target_pairs={{1,0},{2,1},{3,2},{5,4},{6,5},{7,6},{9,8},{10,9},{11,10},{13,12},{... | collective-permute-start | bytes 61448 | tf_op jit(solution)/shard_map/ppermute | solution.py:19
  56.3 5.8 %collective-permute-start = (bf16[8,1,768]{2,1,0:T(2,128)(2,1)S(1)}, bf16[8,1,768]{2,1,0:T(2,128)(2,1)S(1)}, u32[]{:S(2)}, u32[]{:S(2)}) collective-permute-start(bf16[8,1,768]{2,1,0:T(2,128)(2,1)S(1)} %get-tuple-element.27), channel_id=1, source_target_pairs={{0,4},{4,8},{8,12},{12,16},{16,20},{20,24},{24,28},{1,5},{5,9},{9,... | collective-permute-start | bytes 36872 | tf_op jit(solution)/shard_map/ppermute | solution.py:17
  60.6 5.7 %collective-permute-start.1 = (bf16[8,1,768]{2,1,0:T(2,128)(2,1)S(1)}, bf16[8,1,768]{2,1,0:T(2,128)(2,1)S(1)}, u32[]{:S(2)}, u32[]{:S(2)}) collective-permute-start(bf16[8,1,768]{2,1,0:T(2,128)(2,1)S(1)} %get-tuple-element.28), channel_id=1, source_target_pairs={{4,0},{8,4},{12,8},{16,12},{20,16},{24,20},{28,24},{5,1},{9,5},{13... | collective-permute-start | bytes 36872 | tf_op jit(solution)/shard_map/ppermute | solution.py:19
  66.4 9.8 %collective-permute-start.2 = (bf16[1,10,768]{2,1,0:T(8,128)(2,1)S(1)}, bf16[1,10,768]{2,1,0:T(8,128)(2,1)S(1)}, u32[]{:S(2)}, u32[]{:S(2)}) collective-permute-start(bf16[1,10,768]{2,1,0:T(8,128)(2,1)S(1)} %get-tuple-element.19), channel_id=1, source_target_pairs={{0,1},{1,2},{2,3},{4,5},{5,6},{6,7},{8,9},{9,10},{10,11},{12,13},{... | collective-permute-start | bytes 46088 | tf_op jit(solution)/shard_map/ppermute | solution.py:17
  70.0 6.2 %collective-permute-start.3 = (bf16[1,10,768]{2,1,0:T(8,128)(2,1)S(1)}, bf16[1,10,768]{2,1,0:T(8,128)(2,1)S(1)}, u32[]{:S(2)}, u32[]{:S(2)}) collective-permute-start(bf16[1,10,768]{2,1,0:T(8,128)(2,1)S(1)} %get-tuple-element.20), channel_id=1, source_target_pairs={{1,0},{2,1},{3,2},{5,4},{6,5},{7,6},{9,8},{10,9},{11,10},{13,12},{... | collective-permute-start | bytes 46088 | tf_op jit(solution)/shard_map/ppermute | solution.py:19
  81.2 15.5 %collective-permute-start.12 = (bf16[8,1,768]{2,1,0:T(2,128)(2,1)S(1)}, bf16[8,1,768]{2,1,0:T(2,128)(2,1)S(1)}, u32[]{:S(2)}, u32[]{:S(2)}) collective-permute-start(bf16[8,1,768]{2,1,0:T(2,128)(2,1)S(1)} %get-tuple-element.23), channel_id=1, source_target_pairs={{0,4},{4,8},{8,12},{12,16},{16,20},{20,24},{24,28},{1,5},{5,9},{9,... | collective-permute-start | bytes 36872 | tf_op jit(solution)/shard_map/ppermute | solution.py:17
  84.4 12.3 %collective-permute-start.13 = (bf16[8,1,768]{2,1,0:T(2,128)(2,1)S(1)}, bf16[8,1,768]{2,1,0:T(2,128)(2,1)S(1)}, u32[]{:S(2)}, u32[]{:S(2)}) collective-permute-start(bf16[8,1,768]{2,1,0:T(2,128)(2,1)S(1)} %get-tuple-element.24), channel_id=1, source_target_pairs={{4,0},{8,4},{12,8},{16,12},{20,16},{24,20},{28,24},{5,1},{9,5},{13... | collective-permute-start | bytes 36872 | tf_op jit(solution)/shard_map/ppermute | solution.py:19
  85.7 17.2 %collective-permute-start.4 = (bf16[8,1,768]{2,1,0:T(2,128)(2,1)S(1)}, bf16[8,1,768]{2,1,0:T(2,128)(2,1)S(1)}, u32[]{:S(2)}, u32[]{:S(2)}) collective-permute-start(bf16[8,1,768]{2,1,0:T(2,128)(2,1)S(1)} %get-tuple-element.25), channel_id=1, source_target_pairs={{0,4},{4,8},{8,12},{12,16},{16,20},{20,24},{24,28},{1,5},{5,9},{9,... | collective-permute-start | bytes 36872 | tf_op jit(solution)/shard_map/ppermute | solution.py:17
  90.3 12.6 %collective-permute-start.5 = (bf16[8,1,768]{2,1,0:T(2,128)(2,1)S(1)}, bf16[8,1,768]{2,1,0:T(2,128)(2,1)S(1)}, u32[]{:S(2)}, u32[]{:S(2)}) collective-permute-start(bf16[8,1,768]{2,1,0:T(2,128)(2,1)S(1)} %get-tuple-element.26), channel_id=1, source_target_pairs={{4,0},{8,4},{12,8},{16,12},{20,16},{24,20},{28,24},{5,1},{9,5},{13... | collective-permute-start | bytes 36872 | tf_op jit(solution)/shard_map/ppermute | solution.py:19
  96.7 12.9 %collective-permute-start.14 = (bf16[1,10,768]{2,1,0:T(8,128)(2,1)S(1)}, bf16[1,10,768]{2,1,0:T(8,128)(2,1)S(1)}, u32[]{:S(2)}, u32[]{:S(2)}) collective-permute-start(bf16[1,10,768]{2,1,0:T(8,128)(2,1)S(1)} %get-tuple-element.15), channel_id=1, source_target_pairs={{0,1},{1,2},{2,3},{4,5},{5,6},{6,7},{8,9},{9,10},{10,11},{12,13},{... | collective-permute-start | bytes 46088 | tf_op jit(solution)/shard_map/ppermute | solution.py:17
  101.6 8.0 %collective-permute-start.15 = (bf16[1,10,768]{2,1,0:T(8,128)(2,1)S(1)}, bf16[1,10,768]{2,1,0:T(8,128)(2,1)S(1)}, u32[]{:S(2)}, u32[]{:S(2)}) collective-permute-start(bf16[1,10,768]{2,1,0:T(8,128)(2,1)S(1)} %get-tuple-element.16), channel_id=1, source_target_pairs={{1,0},{2,1},{3,2},{5,4},{6,5},{7,6},{9,8},{10,9},{11,10},{13,12},{... | collective-permute-start | bytes 46088 | tf_op jit(solution)/shard_map/ppermute | solution.py:19
  102.9 7.0 %collective-permute-start.6 = (bf16[1,10,768]{2,1,0:T(8,128)(2,1)S(1)}, bf16[1,10,768]{2,1,0:T(8,128)(2,1)S(1)}, u32[]{:S(2)}, u32[]{:S(2)}) collective-permute-start(bf16[1,10,768]{2,1,0:T(8,128)(2,1)S(1)} %get-tuple-element.17), channel_id=1, source_target_pairs={{0,1},{1,2},{2,3},{4,5},{5,6},{6,7},{8,9},{9,10},{10,11},{12,13},{... | collective-permute-start | bytes 46088 | tf_op jit(solution)/shard_map/ppermute | solution.py:17
  108.1 4.3 %collective-permute-start.7 = (bf16[1,10,768]{2,1,0:T(8,128)(2,1)S(1)}, bf16[1,10,768]{2,1,0:T(8,128)(2,1)S(1)}, u32[]{:S(2)}, u32[]{:S(2)}) collective-permute-start(bf16[1,10,768]{2,1,0:T(8,128)(2,1)S(1)} %get-tuple-element.18), channel_id=1, source_target_pairs={{1,0},{2,1},{3,2},{5,4},{6,5},{7,6},{9,8},{10,9},{11,10},{13,12},{... | collective-permute-start | bytes 46088 | tf_op jit(solution)/shard_map/ppermute | solution.py:19
  117.9 1.1 copy-start.3
  119.0 5.5 %copy-start.9 = (s32[1024]{0:T(1024)S(1)}, s32[1024]{0:T(1024)}, u32[]{:S(2)}) copy-start(s32[1024]{0:T(1024)} %copy-done.8) | copy-start | bytes 12292
  124.5 1.1 copy-start.7
  126.5 17.3 %all-to-all-start.2 = ((f32[8,64,96]{2,1,0:T(8,128)}), f32[8,64,96]{2,1,0:T(8,128)S(1)}, u32[]{:S(2)}, u32[]{:S(2)}) async-start(f32[8,64,96]{2,1,0:T(8,128)} %broadcast_divide_fusion), calls=%async_computation.2 | async-start | bytes 524288 | tf_op jit(solution)/shard_map/all_to_all | solution.py:146
  132.6 3.5 %copy-start.6 = (f32[8,8,8]{1,2,0:T(8,128)S(1)}, f32[8,8,8]{1,2,0:T(8,128)}, u32[]{:S(2)}) copy-start(f32[8,8,8]{1,2,0:T(8,128)} %copy.38) | copy-start | bytes 6148
  136.0 7.8 %copy-start.10 = (f32[8,96]{1,0:T(8,128)S(1)}, f32[8,96]{1,0:T(8,128)}, u32[]{:S(2)}) copy-start(f32[8,96]{1,0:T(8,128)} %param.17) | copy-start | bytes 9220
  136.1 7.8 %copy-start.11 = (f32[512,96]{0,1:T(8,128)S(1)}, f32[512,96]{0,1:T(8,128)}, u32[]{:S(2)}) copy-start(f32[512,96]{0,1:T(8,128)} %get-tuple-element.36) | copy-start | bytes 589828
  259.0 2.4 copy-start.1
Sparse Core Ops, SparseCore 0:
  118.1 140.8 all-reduce.7
where the time goes:
time: 270 us; the launch traced here: 269 us
  waiting for transfers between devices  132 us (49%)
  starting transfers between devices  61.1 us (23%)
  matrix products  27.6 us (10%)
  local copies, waits for them, and re-layouts  18.2 us (7%)
  between operations  15.5 us (6%)
  other arithmetic  15.2 us (6%)
    psum x1, waiting for transfers between devices, shards(): one_total, two_total = lax.psum((part_one, part_two), ('blk', 'rep'))  114 us
    ppermute x8, starting transfers between devices, with_halo(): lax.ppermute(tail, axis, [(i, (i + 1) % count) for i in range(ends)])  30.8 us
    conv_general_dilated x4, matrix products, conv_apply(): lax.conv_general_dilated(padded[None], kernel, (1, 1, 1), 'VALID', dimens...  17 us
    ppermute x8, waiting for transfers between devices, with_halo(): lax.ppermute(head, axis, [((i + 1) % count, i) for i in range(ends)])  10.9 us
    ppermute x8, starting transfers between devices, with_halo(): lax.ppermute(head, axis, [((i + 1) % count, i) for i in range(ends)])  10.7 us
    transpose x2, matrix products, kernel_grad(): jnp.transpose(result, (1, 2, 3, 0, 4))  8.46 us
    all_to_all x1, starting transfers between devices, shards(): lax.all_to_all(vox_sent, 'blk', split_axis=0, concat_axis=0, tiled=True)  7.31 us
    all_to_all x1, waiting for transfers between devices, shards(): lax.all_to_all(grad_feat.reshape(owners, SLOT_CAP, width_one), 'blk', spl...  6.8 us
  transfers between devices with their start and end apart: 20, of which 7 were waited for; matrix products, arithmetic and copies ran while one was open for 15% of the time, Pallas kernels for 0%

commit v1 on v0

--- a/solution.py
+++ b/solution.py
@@ -81,6 +81,41 @@
 def flipped(weight, channels_in):
     taps = weight.reshape(3, 3, 3, channels_in, -1)[::-1, ::-1, ::-1]
     return jnp.swapaxes(taps, 3, 4).reshape(-1, channels_in)
+
+
+def exchange_orders(count):
+    bits = [1 << k for k in range(count.bit_length() - 1)]
+    rest = bits[1:]
+    other = []
+    for k in range(0, len(rest), 2):
+        other.extend(rest[k : k + 2][::-1])
+    return bits, bits[:1] + other
+
+
+def reduce_everywhere(total, axes):
+    count = 1
+    for axis in axes:
+        count *= lax.axis_size(axis)
+    index = lax.axis_index(axes)
+    even, odd = exchange_orders(count)
+    steps = []
+    for mask_even, mask_odd in zip(even, odd):
+        pairs = [(i, i ^ (mask_odd if i & 1 else mask_even)) for i in range(count)]
+        mask = jnp.where((index & 1) == 1, mask_odd, mask_even)
+        steps.append((pairs, ((index & mask) != 0).astype(jnp.int32)))
+    for pairs, upper in steps:
+        halves = total.reshape(2, total.shape[0] // 2, total.shape[1])
+        sent = lax.dynamic_index_in_dim(halves, 1 - upper, 0, keepdims=False)
+        kept = lax.dynamic_index_in_dim(halves, upper, 0, keepdims=False)
+        received = lax.ppermute(sent.astype(jnp.bfloat16), axes, pairs)
+        total = kept + received.astype(jnp.float32)
+    whole = total.astype(jnp.bfloat16)
+    for pairs, upper in steps[::-1]:
+        received = lax.ppermute(whole, axes, pairs)
+        first = jnp.where(upper == 1, received, whole)
+        second = jnp.where(upper == 1, whole, received)
+        whole = jnp.concatenate([first, second], axis=0)
+    return whole
 
 
 def shards(
@@ -139,7 +174,15 @@
     grad_act_pad = with_faces(grad_act.reshape(edge_len, edge_len, -1), width_one)
     grad_pooled = conv_apply(grad_act_pad, flipped(conv_one, width_one), width_one)
     part_one = kernel_grad(pooled_pad, grad_act, edge_len)
-    one_total, two_total = lax.psum((part_one, part_two), ("blk", "rep"))
+    rows = part_one.shape[0]
+    unit = 8 * owners * lax.axis_size("rep")
+    stacked = jnp.concatenate(
+        [part_two, jnp.pad(part_one, ((0, 0), (0, width_two - width_one)))], axis=0
+    )
+    stacked = jnp.pad(stacked, ((0, -2 * rows % unit), (0, 0)))
+    summed = reduce_everywhere(stacked, ("blk", "rep")).astype(jnp.float32)
+    two_total = summed[:rows]
+    one_total = summed[rows : 2 * rows, :width_one]
     grad_ext = jnp.concatenate([grad_pooled, jnp.zeros((1, width_one), jnp.float32)], axis=0)
     count_ext = jnp.concatenate([divisor, jnp.ones((1,), jnp.float32)])
     grad_feat = grad_ext[vox_flat] / count_ext[vox_flat][:, None]

time: 270 us -> 176 us (0.65)
  waiting for transfers between devices: 132 us -> 27.7 us
  starting transfers between devices: 61.1 us -> 79.6 us
  between operations: 15.5 us -> 2.29 us
  other arithmetic: 15.2 us -> 21.5 us
    psum x1 -> x0, waiting for transfers between devices: 114 us -> none  [shards(): one_total, two_total = lax.psum((part_one, part_two), ('blk', 'rep'))]
    ppermute x0 -> x10, starting transfers between devices: none -> 19.4 us  [the longest x5 12 us: reduce_everywhere(): received = lax.ppermute(sent.astype(jnp.bfloat16), axes, pairs)]
    ppermute x0 -> x10, waiting for transfers between devices: none -> 17.8 us  [the longest x5 14.8 us: reduce_everywhere(): received = lax.ppermute(sent.astype(jnp.bfloat16), axes, pairs)]
    ppermute x8, waiting for transfers between devices: 10.9 us -> 0.02 us  [with_halo(): lax.ppermute(head, axis, [((i + 1) % count, i) for i in range(ends)])]
    all_to_all x1, waiting for transfers between devices: 6.8 us -> 3.73 us  [shards(): lax.all_to_all(grad_feat.reshape(owners, SLOT_CAP, width_one), 'blk', spl...]
    ppermute x8, waiting for transfers between devices: 0.35 us -> 3.27 us  [with_halo(): lax.ppermute(tail, axis, [(i, (i + 1) % count) for i in range(ends)])]
  transfers between devices with their start and end apart: 20 -> 29, of which waited for: 7 -> 11; matrix products, arithmetic and copies ran while one was open for 15% -> 19% of each run, Pallas kernels for 0% -> 0%
where the time goes in v1:
time: 176 us; the launch traced here: 175 us
  starting transfers between devices  79.6 us (45%)
  waiting for transfers between devices  27.7 us (16%)
  matrix products  27.5 us (16%)
  other arithmetic  21.5 us (12%)
  local copies, waits for them, and re-layouts  16.3 us (9%)
  between operations  2.29 us (1%)
    ppermute x8, starting transfers between devices, with_halo(): lax.ppermute(tail, axis, [(i, (i + 1) % count) for i in range(ends)])  32.2 us
    conv_general_dilated x4, matrix products, conv_apply(): lax.conv_general_dilated(padded[None], kernel, (1, 1, 1), 'VALID', dimens...  17.1 us
    ppermute x5, waiting for transfers between devices, reduce_everywhere(): received = lax.ppermute(sent.astype(jnp.bfloat16), axes, pairs)  14.8 us
    ppermute x5, starting transfers between devices, reduce_everywhere(): received = lax.ppermute(sent.astype(jnp.bfloat16), axes, pairs)  12 us
    ppermute x8, starting transfers between devices, with_halo(): lax.ppermute(head, axis, [((i + 1) % count, i) for i in range(ends)])  10.3 us
    transpose x2, matrix products, kernel_grad(): jnp.transpose(result, (1, 2, 3, 0, 4))  7.41 us
    ppermute x5, starting transfers between devices, reduce_everywhere(): received = lax.ppermute(whole, axes, pairs)  7.4 us
    all_to_all x1, starting transfers between devices, shards(): lax.all_to_all(vox_sent, 'blk', split_axis=0, concat_axis=0, tiled=True)  7.31 us
  transfers between devices with their start and end apart: 29, of which 11 were waited for; matrix products, arithmetic and copies ran while one was open for 19% of the time, Pallas kernels for 0%

profile of v1, /device:TPU:0, one launch (start us, length us, event | category | flops | bytes accessed | tf_op | source)
XLA Modules:
  0.0 175.0 jit_solution(5849232746696199313)
XLA Ops:
  0.7 0.9 reshape.269
  1.5 1.3 compare_select_fusion
  2.8 7.3 %all-to-all-start = ((s32[8,1,64]{2,1,0:T(1,128)}), s32[8,1,64]{2,1,0:T(1,128)S(1)}, u32[]{:S(2)}, u32[]{:S(2)}) async-start(s32[8,1,64]{2,1,0:T(1,128)} %compare_select_fusion), calls=%async_computation | async-start | bytes 8192 | tf_op jit(solution)/shard_map/all_to_all | solution.py:152
  11.0 1.4 fusion.48
  12.3 2.8 %subtract_add_fusion = (f32[1,512]{1,0:T(1,128)S(1)}, f32[1,512]{1,0:T(1,128)S(1)}, f32[1,512]{1,0:T(1,128)S(1)}) fusion(f32[3,512]{1,0:T(4,128)} %param.11, f32[]{:T(128)} %bitcast.4, f32[]{:T(128)} %bitcast.3, f32[]{:T(128)} %bitcast.2, f32[]{:T(128)} %bitcast.5, f32[]{:T(128)} %bitcast.6), kind=kLoop, calls=%fused_computation.116 | loop fusion | flops 4608 | bytes 12308 | tf_op jit(solution)/shard_map/add | solution.py:144
  15.1 1.5 all-to-all-done
  17.8 4.1 %scatter_custom_fusion = s32[513]{0:T(1024)S(1)} fusion(s32[512]{0:T(512)S(1)} %reshape.307, s32[512]{0:T(512)S(1)} %broadcast.150, s32[]{:T(128)} %constant.64.clone.1), kind=kCustom, calls=%fused_computation.117 | custom fusion | flops 512 | bytes 2056 | tf_op jit(solution)/shard_map/scatter-add | solution.py:156
  22.1 1.0 bitcast_select_fusion
  23.2 1.3 collective-permute-start.9
  24.5 4.5 %collective-permute-start.8 = (bf16[8,1,1024]{2,1,0:T(2,128)(2,1)S(1)}, bf16[8,1,1024]{2,1,0:T(2,128)(2,1)S(1)}, u32[]{:S(2)}, u32[]{:S(2)}) collective-permute-start(bf16[8,1,1024]{2,1,0:T(2,128)(2,1)S(1)} %get-tuple-element.42), channel_id=1, source_target_pairs={{0,4},{4,8},{8,12},{12,16},{16,20},{20,24},{24,28},{1,5},{5,9},{9,... | collective-permute-start | bytes 49160 | tf_op jit(solution)/shard_map/ppermute | solution.py:17
  29.1 1.8 %multiply_convert_fusion.3 = (bf16[512,96]{0,1:T(8,128)(2,1)S(1)}, f32[512,96]{0,1:T(8,128)}) fusion(f32[96]{0:T(128)} %param.18, f32[8,96]{1,0:T(8,128)} %param.17, f32[5,512]{1,0:T(8,128)} %param.12, f32[1,512]{1,0:T(1,128)S(1)} %get-tuple-element.54, f32[1,512]{1,0:T(1,128)S(1)} %get-tuple-element.53, f32[1,512]{1,0:T(1,128)S(1)} %get-tuple-element.52), kind=kOutput, calls=%fused_computation.66 | convolution fusion | flops 5025792 | bytes 314752 | tf_op jit(solution)/shard_map/dot_general | solution.py:33
  30.9 0.8 copy.39
  31.6 4.5 %all-to-all-start.1 = ((bf16[8,64,96]{2,1,0:T(8,128)(2,1)}), bf16[8,64,96]{2,1,0:T(8,128)(2,1)S(1)}, u32[]{:S(2)}, u32[]{:S(2)}) async-start(bf16[8,64,96]{2,1,0:T(8,128)(2,1)} %bitcast.7), calls=%async_computation.1 | async-start | bytes 262144 | tf_op jit(solution)/shard_map/all_to_all | solution.py:151
  36.6 1.3 collective-permute-start.11
  37.9 3.0 %collective-permute-start.10 = (bf16[1,10,1024]{2,1,0:T(8,128)(2,1)S(1)}, bf16[1,10,1024]{2,1,0:T(8,128)(2,1)S(1)}, u32[]{:S(2)}, u32[]{:S(2)}) collective-permute-start(bf16[1,10,1024]{2,1,0:T(8,128)(2,1)S(1)} %get-tuple-element.32), channel_id=1, source_target_pairs={{0,1},{1,2},{2,3},{4,5},{5,6},{6,7},{8,9},{9,10},{10,11},{12,13},{... | collective-permute-start | bytes 61448 | tf_op jit(solution)/shard_map/ppermute | solution.py:17
  42.1 1.4 all-to-all-done.1
  43.5 3.2 %scatter_custom_fusion.1 = f32[513,96]{1,0:T(8,128)S(1)} fusion(s32[512]{0:T(512)S(1)} %reshape.307, bf16[512,96]{1,0:T(8,128)(2,1)S(1)} %bitcast.105, f32[]{:T(128)} %constant.67.clone.1), kind=kCustom, calls=%fused_computation.47 | custom fusion | flops 98304 | bytes 328068 | tf_op jit(solution)/shard_map/scatter-add | solution.py:158
  47.1 1.3 collective-permute-start.1
  48.4 4.5 %collective-permute-start = (bf16[8,1,768]{2,1,0:T(2,128)(2,1)S(1)}, bf16[8,1,768]{2,1,0:T(2,128)(2,1)S(1)}, u32[]{:S(2)}, u32[]{:S(2)}) collective-permute-start(bf16[8,1,768]{2,1,0:T(2,128)(2,1)S(1)} %get-tuple-element.48), channel_id=1, source_target_pairs={{0,4},{4,8},{8,12},{12,16},{16,20},{20,24},{24,28},{1,5},{5,9},{9,... | collective-permute-start | bytes 36872 | tf_op jit(solution)/shard_map/ppermute | solution.py:17
  53.1 1.4 collective-permute-done
  54.5 1.3 collective-permute-start.3
  55.8 3.2 %collective-permute-start.2 = (bf16[1,10,768]{2,1,0:T(8,128)(2,1)S(1)}, bf16[1,10,768]{2,1,0:T(8,128)(2,1)S(1)}, u32[]{:S(2)}, u32[]{:S(2)}) collective-permute-start(bf16[1,10,768]{2,1,0:T(8,128)(2,1)S(1)} %get-tuple-element.40), channel_id=1, source_target_pairs={{0,1},{1,2},{2,3},{4,5},{5,6},{6,7},{8,9},{9,10},{10,11},{12,13},{... | collective-permute-start | bytes 46088 | tf_op jit(solution)/shard_map/ppermute | solution.py:17
  59.5 4.0 %fusion.50 = (f32[8,8,8,96]{3,2,1,0:T(8,128)S(1)}, f32[1,8,8,8,96]{4,0,3,2,1:T(1,128)S(1)}) fusion(f32[]{:T(128)} %broadcast.180, bf16[3,3,3,96,128]{4,3,2,1,0:T(8,128)(2,1)S(1)} %bitcast.88, bf16[1,10,10,10,128]{4,3,2,1,0:T(8,128)(2,1)S(1)} %pad_bitcast_fusion.5), kind=kOutput, calls=%fused_computation.129 | convolution fusion | flops 339738624 | bytes 1312772 | tf_op jit(solution)/shard_map/conv_general_dilated | solution.py:54
  64.2 4.1 %fusion.49 = (f32[8,8,8,96]{3,2,1,0:T(8,128)S(1)}, f32[1,8,8,8,96]{4,0,3,2,1:T(1,128)S(1)}) fusion(f32[]{:T(128)} %broadcast.180, bf16[3,3,3,96,96]{4,3,2,1,0:T(8,128)(2,1)S(1)} %bitcast.101, bf16[1,10,10,10,96]{4,3,2,1,0:T(8,128)(2,1)S(1)} %get-tuple-element.31), kind=kOutput, calls=%fused_computation.128 | convolution fusion | flops 254803968 | bytes 1082884 | tf_op jit(solution)/shard_map/conv_general_dilated | solution.py:54
  68.5 0.7 multiply_convert_fusion.1
  69.3 1.3 collective-permute-start.5
  70.6 4.8 %collective-permute-start.4 = (bf16[8,1,768]{2,1,0:T(2,128)(2,1)S(1)}, bf16[8,1,768]{2,1,0:T(2,128)(2,1)S(1)}, u32[]{:S(2)}, u32[]{:S(2)}) collective-permute-start(bf16[8,1,768]{2,1,0:T(2,128)(2,1)S(1)} %get-tuple-element.46), channel_id=1, source_target_pairs={{0,4},{4,8},{8,12},{12,16},{16,20},{20,24},{24,28},{1,5},{5,9},{9,... | collective-permute-start | bytes 36872 | tf_op jit(solution)/shard_map/ppermute | solution.py:17
  75.6 1.3 collective-permute-done.4
  76.9 1.3 collective-permute-start.7
  78.2 4.2 %collective-permute-start.6 = (bf16[1,10,768]{2,1,0:T(8,128)(2,1)S(1)}, bf16[1,10,768]{2,1,0:T(8,128)(2,1)S(1)}, u32[]{:S(2)}, u32[]{:S(2)}) collective-permute-start(bf16[1,10,768]{2,1,0:T(8,128)(2,1)S(1)} %get-tuple-element.38), channel_id=1, source_target_pairs={{0,1},{1,2},{2,3},{4,5},{5,6},{6,7},{8,9},{9,10},{10,11},{12,13},{... | collective-permute-start | bytes 46088 | tf_op jit(solution)/shard_map/ppermute | solution.py:17
  82.5 3.6 %fusion.2 = f32[3,3,3,96,96]{4,3,2,1,0:T(8,128)S(1)} fusion(bf16[96,10,10,10,1]{0,3,4,2,1:T(8,128)(2,1)S(1)} %get-tuple-element.30, bf16[8,8,8,1,96]{4,2,1,0,3:T(8,128)(2,1)S(1)} %multiply_convert_fusion), kind=kOutput, calls=%fused_computation.21 | convolution fusion | flops 254803968 | bytes 1285632 | tf_op jit(solution)/shard_map/transpose | solution.py:78
  86.4 0.9 pad_bitcast_fusion
  87.3 3.9 %fusion.4 = f32[3,3,3,96,128]{4,3,2,1,0:T(8,128)S(1)} fusion(bf16[96,10,10,10,1]{0,3,4,2,1:T(8,128)(2,1)S(1)} %get-tuple-element.28, pred[8,8,8]{2,1,0:T(8,128)(4,1)S(1)} %broadcast_compare_fusion, bf16[8,8,8,1,128]{4,1,2,0,3:T(8,128)(2,1)S(1)} %bitcast.109), kind=kOutput, calls=%fused_computation.23 | convolution fusion | flops 339804160 | bytes 1650688 | tf_op jit(solution)/shard_map/transpose | solution.py:78
  91.5 0.9 fusion
  92.5 1.7 collective-permute-start.16
  94.2 2.1 %collective-permute-done.16 = bf16[2688,128]{1,0:T(8,128)(2,1)} collective-permute-done((bf16[2688,128]{1,0:T(8,128)(2,1)}, bf16[2688,128]{1,0:T(8,128)(2,1)}, u32[]{:S(2)}, u32[]{:S(2)}) %collective-permute-start.16) | collective-permute-done | bytes 688160 | tf_op jit(solution)/shard_map/ppermute | solution.py:110
  96.3 1.3 bitcast_add_fusion
  97.6 1.1 copy-done.1
  99.2 6.8 %collective-permute-done.17 = bf16[1344,128]{1,0:T(8,128)(2,1)S(1)} collective-permute-done((bf16[1344,128]{1,0:T(8,128)(2,1)S(1)}, bf16[1344,128]{1,0:T(8,128)(2,1)S(1)}, u32[]{:S(2)}, u32[]{:S(2)}) %collective-permute-start.17) | collective-permute-done | bytes 344096 | tf_op jit(solution)/shard_map/ppermute | solution.py:110
  106.0 1.2 bitcast_add_fusion.1
  107.3 3.3 %collective-permute-start.18 = (bf16[672,128]{1,0:T(8,128)(2,1)S(1)}, bf16[672,128]{1,0:T(8,128)(2,1)S(1)}, u32[]{:S(2)}, u32[]{:S(2)}) collective-permute-start(bf16[672,128]{1,0:T(8,128)(2,1)S(1)} %fusion.25), channel_id=1, source_target_pairs={{0,4},{1,3},{2,6},{3,1},{4,0},{5,7},{6,2},{7,5},{8,12},{9,11},{10,... | collective-permute-start | bytes 516104 | tf_op jit(solution)/shard_map/ppermute | solution.py:110
  110.6 3.4 %collective-permute-done.18 = bf16[672,128]{1,0:T(8,128)(2,1)S(1)} collective-permute-done((bf16[672,128]{1,0:T(8,128)(2,1)S(1)}, bf16[672,128]{1,0:T(8,128)(2,1)S(1)}, u32[]{:S(2)}, u32[]{:S(2)}) %collective-permute-start.18) | collective-permute-done | bytes 172064 | tf_op jit(solution)/shard_map/ppermute | solution.py:110
  114.0 3.5 %collective-permute-start.19 = (bf16[336,128]{1,0:T(8,128)(2,1)S(1)}, bf16[336,128]{1,0:T(8,128)(2,1)S(1)}, u32[]{:S(2)}, u32[]{:S(2)}) collective-permute-start(bf16[336,128]{1,0:T(8,128)(2,1)S(1)} %fusion.29), channel_id=1, source_target_pairs={{0,8},{1,17},{2,10},{3,19},{4,12},{5,21},{6,14},{7,23},{8,0},{9,25... | collective-permute-start | bytes 258056 | tf_op jit(solution)/shard_map/ppermute | solution.py:110
  117.5 2.5 %collective-permute-done.19 = bf16[336,128]{1,0:T(8,128)(2,1)S(1)} collective-permute-done((bf16[336,128]{1,0:T(8,128)(2,1)S(1)}, bf16[336,128]{1,0:T(8,128)(2,1)S(1)}, u32[]{:S(2)}, u32[]{:S(2)}) %collective-permute-start.19) | collective-permute-done | bytes 86048 | tf_op jit(solution)/shard_map/ppermute | solution.py:110
  120.0 3.0 %collective-permute-start.20 = (bf16[168,128]{1,0:T(8,128)(2,1)S(1)}, bf16[168,128]{1,0:T(8,128)(2,1)S(1)}, u32[]{:S(2)}, u32[]{:S(2)}) collective-permute-start(bf16[168,128]{1,0:T(8,128)(2,1)S(1)} %fusion.31), channel_id=1, source_target_pairs={{0,16},{1,9},{2,18},{3,11},{4,20},{5,13},{6,22},{7,15},{8,24},{9,1... | collective-permute-start | bytes 129032 | tf_op jit(solution)/shard_map/ppermute | solution.py:110
  123.2 2.3 %gather_fusion.1 = f32[512]{0:T(512)S(1)} fusion(f32[513]{0:T(1024)S(1)} %pad_maximum_fusion.21, s32[1024]{0:T(1024)S(1)} %pad_clamp_fusion), kind=kCustom, calls=%fused_computation.1 | custom fusion | bytes 6144 | tf_op jit(solution)/shard_map/gather | solution.py:188
  125.6 2.6 %collective-permute-start.21 = (bf16[168,128]{1,0:T(8,128)(2,1)S(1)}, bf16[168,128]{1,0:T(8,128)(2,1)S(1)}, u32[]{:S(2)}, u32[]{:S(2)}) collective-permute-start(bf16[168,128]{1,0:T(8,128)(2,1)S(1)} %fusion.30), channel_id=1, source_target_pairs={{0,16},{1,9},{2,18},{3,11},{4,20},{5,13},{6,22},{7,15},{8,24},{9,1... | collective-permute-start | bytes 129032 | tf_op jit(solution)/shard_map/ppermute | solution.py:114
  128.2 1.3 collective-permute-start.13
  129.5 4.5 %collective-permute-start.12 = (bf16[8,1,768]{2,1,0:T(2,128)(2,1)S(1)}, bf16[8,1,768]{2,1,0:T(2,128)(2,1)S(1)}, u32[]{:S(2)}, u32[]{:S(2)}) collective-permute-start(bf16[8,1,768]{2,1,0:T(2,128)(2,1)S(1)} %get-tuple-element.44), channel_id=1, source_target_pairs={{0,4},{4,8},{8,12},{12,16},{16,20},{20,24},{24,28},{1,5},{5,9},{9,... | collective-permute-start | bytes 36872 | tf_op jit(solution)/shard_map/ppermute | solution.py:17
  134.1 2.1 %collective-permute-start.22 = (bf16[336,128]{1,0:T(8,128)(2,1)S(1)}, bf16[336,128]{1,0:T(8,128)(2,1)S(1)}, u32[]{:S(2)}, u32[]{:S(2)}) collective-permute-start(bf16[336,128]{1,0:T(8,128)(2,1)S(1)} %pad_maximum_fusion.8), channel_id=1, source_target_pairs={{0,8},{1,17},{2,10},{3,19},{4,12},{5,21},{6,14},{7,23},{8,0},{9,25... | collective-permute-start | bytes 258056 | tf_op jit(solution)/shard_map/ppermute | solution.py:114
  136.2 1.3 collective-permute-start.15
  137.5 3.3 %collective-permute-start.14 = (bf16[1,10,768]{2,1,0:T(8,128)(2,1)S(1)}, bf16[1,10,768]{2,1,0:T(8,128)(2,1)S(1)}, u32[]{:S(2)}, u32[]{:S(2)}) collective-permute-start(bf16[1,10,768]{2,1,0:T(8,128)(2,1)S(1)} %get-tuple-element.36), channel_id=1, source_target_pairs={{0,1},{1,2},{2,3},{4,5},{5,6},{6,7},{8,9},{9,10},{10,11},{12,13},{... | collective-permute-start | bytes 46088 | tf_op jit(solution)/shard_map/ppermute | solution.py:17
  140.9 2.0 %collective-permute-start.23 = (bf16[672,128]{1,0:T(8,128)(2,1)S(1)}, bf16[672,128]{1,0:T(8,128)(2,1)S(1)}, u32[]{:S(2)}, u32[]{:S(2)}) collective-permute-start(bf16[672,128]{1,0:T(8,128)(2,1)S(1)} %pad_maximum_fusion.7), channel_id=1, source_target_pairs={{0,4},{1,3},{2,6},{3,1},{4,0},{5,7},{6,2},{7,5},{8,12},{9,11},{10,... | collective-permute-start | bytes 516104 | tf_op jit(solution)/shard_map/ppermute | solution.py:114
  143.4 3.0 %collective-permute-done.23 = bf16[672,128]{1,0:T(8,128)(2,1)S(1)} collective-permute-done((bf16[672,128]{1,0:T(8,128)(2,1)S(1)}, bf16[672,128]{1,0:T(8,128)(2,1)S(1)}, u32[]{:S(2)}, u32[]{:S(2)}) %collective-permute-start.23) | collective-permute-done | bytes 172064 | tf_op jit(solution)/shard_map/ppermute | solution.py:114
  147.2 5.5 %fusion.6 = f32[1,8,8,8,96]{4,0,3,2,1:T(1,128)S(1)} fusion(bf16[3,3,3,96,96]{4,3,2,1,0:T(8,128)(2,1)S(1)} %bitcast.102, bf16[1,10,10,10,96]{4,3,2,1,0:T(8,128)(2,1)S(1)} %pad_bitcast_fusion.4), kind=kOutput, calls=%fused_computation.25 | convolution fusion | flops 254803968 | bytes 886272 | tf_op jit(solution)/shard_map/conv_general_dilated | solution.py:54
  152.7 1.0 gather_fusion
  153.8 0.8 broadcast_divide_fusion
  154.6 5.8 %all-to-all-start.2 = ((f32[8,64,96]{2,1,0:T(8,128)}), f32[8,64,96]{2,1,0:T(8,128)S(1)}, u32[]{:S(2)}, u32[]{:S(2)}) async-start(f32[8,64,96]{2,1,0:T(8,128)} %broadcast_divide_fusion), calls=%async_computation.2 | async-start | bytes 524288 | tf_op jit(solution)/shard_map/all_to_all | solution.py:189
  161.5 3.4 %convolution_reduce_fusion = f32[8,8,8,128]{3,2,1,0:T(8,128)S(1)} fusion(bf16[3,3,3,96,128]{4,3,2,1,0:T(8,128)(2,1)S(1)} %bitcast.87, bf16[1,10,10,10,96]{4,3,2,1,0:T(8,128)(2,1)S(1)} %copy-done.8), kind=kOutput, calls=%fused_computation.8 | convolution fusion | flops 339738624 | bytes 1117696 | tf_op jit(solution)/shard_map/conv_general_dilated | solution.py:54
  165.0 0.8 fusion.17
  165.8 3.7 %all-to-all-done.2 = f32[8,64,96]{2,1,0:T(8,128)S(1)} async-done(((f32[8,64,96]{2,1,0:T(8,128)}), f32[8,64,96]{2,1,0:T(8,128)S(1)}, u32[]{:S(2)}, u32[]{:S(2)}) %all-to-all-start.2) | async-done | bytes 196640 | tf_op jit(solution)/shard_map/all_to_all | solution.py:189
  169.6 1.2 convolution_bitcast_fusion
  172.5 1.1 fusion.1
  173.6 1.4 copy.51
  (118 shorter events, 10.6 us)
Async XLA Ops:
  0.6 58.4 %copy-start = (bf16[2592,128]{1,0:T(8,128)(2,1)S(1)}, bf16[2592,128]{1,0:T(8,128)(2,1)}, u32[]{:S(2)}) copy-start(bf16[2592,128]{1,0:T(8,128)(2,1)} %param.20) | copy-start | bytes 1990660
  0.6 35.5 %copy-start.7 = (bf16[2592,96]{0,1:T(8,128)(2,1)S(1)}, bf16[2592,96]{0,1:T(8,128)(2,1)}, u32[]{:S(2)}) copy-start(bf16[2592,96]{0,1:T(8,128)(2,1)} %param.19) | copy-start | bytes 1492996
  2.8 13.7 %all-to-all-start = ((s32[8,1,64]{2,1,0:T(1,128)}), s32[8,1,64]{2,1,0:T(1,128)S(1)}, u32[]{:S(2)}, u32[]{:S(2)}) async-start(s32[8,1,64]{2,1,0:T(1,128)} %compare_select_fusion), calls=%async_computation | async-start | bytes 8192 | tf_op jit(solution)/shard_map/all_to_all | solution.py:152
  16.6 5.4 %copy-start.10 = (s32[8,1,64]{2,1,0:T(1,128)}, s32[8,1,64]{2,1,0:T(1,128)S(1)}, u32[]{:S(2)}) copy-start(s32[8,1,64]{2,1,0:T(1,128)S(1)} %all-to-all-done) | copy-start | bytes 6148
  22.0 53.4 %copy-start.3 = (f32[8,8,8]{2,1,0:T(8,128)}, f32[8,8,8]{2,1,0:T(8,128)S(1)}, u32[]{:S(2)}) copy-start(f32[8,8,8]{2,1,0:T(8,128)S(1)} %reshape.287) | copy-start | bytes 6148
  23.2 13.3 %collective-permute-start.9 = (bf16[8,1,1024]{2,1,0:T(2,128)(2,1)S(1)}, bf16[8,1,1024]{2,1,0:T(2,128)(2,1)S(1)}, u32[]{:S(2)}, u32[]{:S(2)}) collective-permute-start(bf16[8,1,1024]{2,1,0:T(2,128)(2,1)S(1)} %get-tuple-element.43), channel_id=1, source_target_pairs={{4,0},{8,4},{12,8},{16,12},{20,16},{24,20},{28,24},{5,1},{9,5},{13... | collective-permute-start | bytes 49160 | tf_op jit(solution)/shard_map/ppermute | solution.py:19
  24.5 12.0 %collective-permute-start.8 = (bf16[8,1,1024]{2,1,0:T(2,128)(2,1)S(1)}, bf16[8,1,1024]{2,1,0:T(2,128)(2,1)S(1)}, u32[]{:S(2)}, u32[]{:S(2)}) collective-permute-start(bf16[8,1,1024]{2,1,0:T(2,128)(2,1)S(1)} %get-tuple-element.42), channel_id=1, source_target_pairs={{0,4},{4,8},{8,12},{12,16},{16,20},{20,24},{24,28},{1,5},{5,9},{9,... | collective-permute-start | bytes 49160 | tf_op jit(solution)/shard_map/ppermute | solution.py:17
  31.6 11.9 %all-to-all-start.1 = ((bf16[8,64,96]{2,1,0:T(8,128)(2,1)}), bf16[8,64,96]{2,1,0:T(8,128)(2,1)S(1)}, u32[]{:S(2)}, u32[]{:S(2)}) async-start(bf16[8,64,96]{2,1,0:T(8,128)(2,1)} %bitcast.7), calls=%async_computation.1 | async-start | bytes 262144 | tf_op jit(solution)/shard_map/all_to_all | solution.py:151
  36.5 27.7 %copy-start.5 = (bf16[2592,96]{1,0:T(8,128)(2,1)}, bf16[2592,96]{1,0:T(8,128)(2,1)S(1)}, u32[]{:S(2)}) copy-start(bf16[2592,96]{1,0:T(8,128)(2,1)S(1)} %copy.40) | copy-start | bytes 1492996
  36.6 4.6 %collective-permute-start.11 = (bf16[1,10,1024]{2,1,0:T(8,128)(2,1)S(1)}, bf16[1,10,1024]{2,1,0:T(8,128)(2,1)S(1)}, u32[]{:S(2)}, u32[]{:S(2)}) collective-permute-start(bf16[1,10,1024]{2,1,0:T(8,128)(2,1)S(1)} %get-tuple-element.33), channel_id=1, source_target_pairs={{1,0},{2,1},{3,2},{5,4},{6,5},{7,6},{9,8},{10,9},{11,10},{13,12},{... | collective-permute-start | bytes 61448 | tf_op jit(solution)/shard_map/ppermute | solution.py:19
  37.9 3.9 %collective-permute-start.10 = (bf16[1,10,1024]{2,1,0:T(8,128)(2,1)S(1)}, bf16[1,10,1024]{2,1,0:T(8,128)(2,1)S(1)}, u32[]{:S(2)}, u32[]{:S(2)}) collective-permute-start(bf16[1,10,1024]{2,1,0:T(8,128)(2,1)S(1)} %get-tuple-element.32), channel_id=1, source_target_pairs={{0,1},{1,2},{2,3},{4,5},{5,6},{6,7},{8,9},{9,10},{10,11},{12,13},{... | collective-permute-start | bytes 61448 | tf_op jit(solution)/shard_map/ppermute | solution.py:17
  41.0 6.1 %copy-start.12 = (f32[512]{0:T(512)}, f32[512]{0:T(512)S(1)}, u32[]{:S(2)}) copy-start(f32[512]{0:T(512)S(1)} %maximum_convert_fusion.1) | copy-start | bytes 6148
  47.1 6.0 %collective-permute-start.1 = (bf16[8,1,768]{2,1,0:T(2,128)(2,1)S(1)}, bf16[8,1,768]{2,1,0:T(2,128)(2,1)S(1)}, u32[]{:S(2)}, u32[]{:S(2)}) collective-permute-start(bf16[8,1,768]{2,1,0:T(2,128)(2,1)S(1)} %get-tuple-element.49), channel_id=1, source_target_pairs={{4,0},{8,4},{12,8},{16,12},{20,16},{24,20},{28,24},{5,1},{9,5},{13... | collective-permute-start | bytes 36872 | tf_op jit(solution)/shard_map/ppermute | solution.py:19
  48.4 6.1 %collective-permute-start = (bf16[8,1,768]{2,1,0:T(2,128)(2,1)S(1)}, bf16[8,1,768]{2,1,0:T(2,128)(2,1)S(1)}, u32[]{:S(2)}, u32[]{:S(2)}) collective-permute-start(bf16[8,1,768]{2,1,0:T(2,128)(2,1)S(1)} %get-tuple-element.48), channel_id=1, source_target_pairs={{0,4},{4,8},{8,12},{12,16},{16,20},{20,24},{24,28},{1,5},{5,9},{9,... | collective-permute-start | bytes 36872 | tf_op jit(solution)/shard_map/ppermute | solution.py:17
  54.5 9.2 %collective-permute-start.3 = (bf16[1,10,768]{2,1,0:T(8,128)(2,1)S(1)}, bf16[1,10,768]{2,1,0:T(8,128)(2,1)S(1)}, u32[]{:S(2)}, u32[]{:S(2)}) collective-permute-start(bf16[1,10,768]{2,1,0:T(8,128)(2,1)S(1)} %get-tuple-element.41), channel_id=1, source_target_pairs={{1,0},{2,1},{3,2},{5,4},{6,5},{7,6},{9,8},{10,9},{11,10},{13,12},{... | collective-permute-start | bytes 46088 | tf_op jit(solution)/shard_map/ppermute | solution.py:19
  55.8 7.9 %collective-permute-start.2 = (bf16[1,10,768]{2,1,0:T(8,128)(2,1)S(1)}, bf16[1,10,768]{2,1,0:T(8,128)(2,1)S(1)}, u32[]{:S(2)}, u32[]{:S(2)}) collective-permute-start(bf16[1,10,768]{2,1,0:T(8,128)(2,1)S(1)} %get-tuple-element.40), channel_id=1, source_target_pairs={{0,1},{1,2},{2,3},{4,5},{5,6},{6,7},{8,9},{9,10},{10,11},{12,13},{... | collective-permute-start | bytes 46088 | tf_op jit(solution)/shard_map/ppermute | solution.py:17
  69.3 6.3 %collective-permute-start.5 = (bf16[8,1,768]{2,1,0:T(2,128)(2,1)S(1)}, bf16[8,1,768]{2,1,0:T(2,128)(2,1)S(1)}, u32[]{:S(2)}, u32[]{:S(2)}) collective-permute-start(bf16[8,1,768]{2,1,0:T(2,128)(2,1)S(1)} %get-tuple-element.47), channel_id=1, source_target_pairs={{4,0},{8,4},{12,8},{16,12},{20,16},{24,20},{28,24},{5,1},{9,5},{13... | collective-permute-start | bytes 36872 | tf_op jit(solution)/shard_map/ppermute | solution.py:19
  70.6 6.4 %collective-permute-start.4 = (bf16[8,1,768]{2,1,0:T(2,128)(2,1)S(1)}, bf16[8,1,768]{2,1,0:T(2,128)(2,1)S(1)}, u32[]{:S(2)}, u32[]{:S(2)}) collective-permute-start(bf16[8,1,768]{2,1,0:T(2,128)(2,1)S(1)} %get-tuple-element.46), channel_id=1, source_target_pairs={{0,4},{4,8},{8,12},{12,16},{16,20},{20,24},{24,28},{1,5},{5,9},{9,... | collective-permute-start | bytes 36872 | tf_op jit(solution)/shard_map/ppermute | solution.py:17
  76.9 9.1 %collective-permute-start.7 = (bf16[1,10,768]{2,1,0:T(8,128)(2,1)S(1)}, bf16[1,10,768]{2,1,0:T(8,128)(2,1)S(1)}, u32[]{:S(2)}, u32[]{:S(2)}) collective-permute-start(bf16[1,10,768]{2,1,0:T(8,128)(2,1)S(1)} %get-tuple-element.39), channel_id=1, source_target_pairs={{1,0},{2,1},{3,2},{5,4},{6,5},{7,6},{9,8},{10,9},{11,10},{13,12},{... | collective-permute-start | bytes 46088 | tf_op jit(solution)/shard_map/ppermute | solution.py:19
  78.2 7.8 %collective-permute-start.6 = (bf16[1,10,768]{2,1,0:T(8,128)(2,1)S(1)}, bf16[1,10,768]{2,1,0:T(8,128)(2,1)S(1)}, u32[]{:S(2)}, u32[]{:S(2)}) collective-permute-start(bf16[1,10,768]{2,1,0:T(8,128)(2,1)S(1)} %get-tuple-element.38), channel_id=1, source_target_pairs={{0,1},{1,2},{2,3},{4,5},{5,6},{6,7},{8,9},{9,10},{10,11},{12,13},{... | collective-permute-start | bytes 46088 | tf_op jit(solution)/shard_map/ppermute | solution.py:17
  86.0 1.3 copy-start.9
  92.5 3.9 %collective-permute-start.16 = (bf16[2688,128]{1,0:T(8,128)(2,1)}, bf16[2688,128]{1,0:T(8,128)(2,1)}, u32[]{:S(2)}, u32[]{:S(2)}) collective-permute-start(bf16[2688,128]{1,0:T(8,128)(2,1)} %fusion), channel_id=1, source_target_pairs={{0,1},{1,0},{2,3},{3,2},{4,5},{5,4},{6,7},{7,6},{8,9},{9,8},{10,11... | collective-permute-start | bytes 2064392 | tf_op jit(solution)/shard_map/ppermute | solution.py:110
  94.2 5.0 %copy-start.11 = (s32[8,1,64]{2,1,0:T(1,128)S(1)}, s32[8,1,64]{2,1,0:T(1,128)}, u32[]{:S(2)}) copy-start(s32[8,1,64]{2,1,0:T(1,128)} %copy-done.10) | copy-start | bytes 6148
  97.6 1.1 copy-start.1
  98.7 7.3 %collective-permute-start.17 = (bf16[1344,128]{1,0:T(8,128)(2,1)S(1)}, bf16[1344,128]{1,0:T(8,128)(2,1)S(1)}, u32[]{:S(2)}, u32[]{:S(2)}) collective-permute-start(bf16[1344,128]{1,0:T(8,128)(2,1)S(1)} %fusion.13), channel_id=1, source_target_pairs={{0,2},{1,5},{2,0},{3,7},{4,6},{5,1},{6,4},{7,3},{8,10},{9,13},{10,... | collective-permute-start | bytes 1032200 | tf_op jit(solution)/shard_map/ppermute | solution.py:110
  107.2 15.8 %copy-start.13 = (f32[512]{0:T(512)S(1)}, f32[512]{0:T(512)}, u32[]{:S(2)}) copy-start(f32[512]{0:T(512)} %copy-done.12) | copy-start | bytes 6148
  107.2 15.8 %copy-start.4 = (f32[8,8,8]{2,1,0:T(8,128)S(1)}, f32[8,8,8]{2,1,0:T(8,128)}, u32[]{:S(2)}) copy-start(f32[8,8,8]{2,1,0:T(8,128)} %copy-done.3) | copy-start | bytes 6148
  107.3 6.7 %collective-permute-start.18 = (bf16[672,128]{1,0:T(8,128)(2,1)S(1)}, bf16[672,128]{1,0:T(8,128)(2,1)S(1)}, u32[]{:S(2)}, u32[]{:S(2)}) collective-permute-start(bf16[672,128]{1,0:T(8,128)(2,1)S(1)} %fusion.25), channel_id=1, source_target_pairs={{0,4},{1,3},{2,6},{3,1},{4,0},{5,7},{6,2},{7,5},{8,12},{9,11},{10,... | collective-permute-start | bytes 516104 | tf_op jit(solution)/shard_map/ppermute | solution.py:110
  114.0 6.0 %collective-permute-start.19 = (bf16[336,128]{1,0:T(8,128)(2,1)S(1)}, bf16[336,128]{1,0:T(8,128)(2,1)S(1)}, u32[]{:S(2)}, u32[]{:S(2)}) collective-permute-start(bf16[336,128]{1,0:T(8,128)(2,1)S(1)} %fusion.29), channel_id=1, source_target_pairs={{0,8},{1,17},{2,10},{3,19},{4,12},{5,21},{6,14},{7,23},{8,0},{9,25... | collective-permute-start | bytes 258056 | tf_op jit(solution)/shard_map/ppermute | solution.py:110
  117.5 10.6 %copy-start.2 = (bf16[8,8,768]{2,1,0:T(8,128)(2,1)S(1)}, bf16[8,8,768]{2,1,0:T(8,128)(2,1)}, u32[]{:S(2)}) copy-start(bf16[8,8,768]{2,1,0:T(8,128)(2,1)} %get-tuple-element.24) | copy-start | bytes 294916
  120.0 5.5 %collective-permute-start.20 = (bf16[168,128]{1,0:T(8,128)(2,1)S(1)}, bf16[168,128]{1,0:T(8,128)(2,1)S(1)}, u32[]{:S(2)}, u32[]{:S(2)}) collective-permute-start(bf16[168,128]{1,0:T(8,128)(2,1)S(1)} %fusion.31), channel_id=1, source_target_pairs={{0,16},{1,9},{2,18},{3,11},{4,20},{5,13},{6,22},{7,15},{8,24},{9,1... | collective-permute-start | bytes 129032 | tf_op jit(solution)/shard_map/ppermute | solution.py:110
  125.6 8.5 %collective-permute-start.21 = (bf16[168,128]{1,0:T(8,128)(2,1)S(1)}, bf16[168,128]{1,0:T(8,128)(2,1)S(1)}, u32[]{:S(2)}, u32[]{:S(2)}) collective-permute-start(bf16[168,128]{1,0:T(8,128)(2,1)S(1)} %fusion.30), channel_id=1, source_target_pairs={{0,16},{1,9},{2,18},{3,11},{4,20},{5,13},{6,22},{7,15},{8,24},{9,1... | collective-permute-start | bytes 129032 | tf_op jit(solution)/shard_map/ppermute | solution.py:114
  128.2 8.0 %collective-permute-start.13 = (bf16[8,1,768]{2,1,0:T(2,128)(2,1)S(1)}, bf16[8,1,768]{2,1,0:T(2,128)(2,1)S(1)}, u32[]{:S(2)}, u32[]{:S(2)}) collective-permute-start(bf16[8,1,768]{2,1,0:T(2,128)(2,1)S(1)} %get-tuple-element.45), channel_id=1, source_target_pairs={{4,0},{8,4},{12,8},{16,12},{20,16},{24,20},{28,24},{5,1},{9,5},{13... | collective-permute-start | bytes 36872 | tf_op jit(solution)/shard_map/ppermute | solution.py:19
  129.5 6.7 %collective-permute-start.12 = (bf16[8,1,768]{2,1,0:T(2,128)(2,1)S(1)}, bf16[8,1,768]{2,1,0:T(2,128)(2,1)S(1)}, u32[]{:S(2)}, u32[]{:S(2)}) collective-permute-start(bf16[8,1,768]{2,1,0:T(2,128)(2,1)S(1)} %get-tuple-element.44), channel_id=1, source_target_pairs={{0,4},{4,8},{8,12},{12,16},{16,20},{20,24},{24,28},{1,5},{5,9},{9,... | collective-permute-start | bytes 36872 | tf_op jit(solution)/shard_map/ppermute | solution.py:17
  134.1 6.7 %collective-permute-start.22 = (bf16[336,128]{1,0:T(8,128)(2,1)S(1)}, bf16[336,128]{1,0:T(8,128)(2,1)S(1)}, u32[]{:S(2)}, u32[]{:S(2)}) collective-permute-start(bf16[336,128]{1,0:T(8,128)(2,1)S(1)} %pad_maximum_fusion.8), channel_id=1, source_target_pairs={{0,8},{1,17},{2,10},{3,19},{4,12},{5,21},{6,14},{7,23},{8,0},{9,25... | collective-permute-start | bytes 258056 | tf_op jit(solution)/shard_map/ppermute | solution.py:114
  136.2 6.7 %collective-permute-start.15 = (bf16[1,10,768]{2,1,0:T(8,128)(2,1)S(1)}, bf16[1,10,768]{2,1,0:T(8,128)(2,1)S(1)}, u32[]{:S(2)}, u32[]{:S(2)}) collective-permute-start(bf16[1,10,768]{2,1,0:T(8,128)(2,1)S(1)} %get-tuple-element.37), channel_id=1, source_target_pairs={{1,0},{2,1},{3,2},{5,4},{6,5},{7,6},{9,8},{10,9},{11,10},{13,12},{... | collective-permute-start | bytes 46088 | tf_op jit(solution)/shard_map/ppermute | solution.py:19
  137.5 5.4 %collective-permute-start.14 = (bf16[1,10,768]{2,1,0:T(8,128)(2,1)S(1)}, bf16[1,10,768]{2,1,0:T(8,128)(2,1)S(1)}, u32[]{:S(2)}, u32[]{:S(2)}) collective-permute-start(bf16[1,10,768]{2,1,0:T(8,128)(2,1)S(1)} %get-tuple-element.36), channel_id=1, source_target_pairs={{0,1},{1,2},{2,3},{4,5},{5,6},{6,7},{8,9},{9,10},{10,11},{12,13},{... | collective-permute-start | bytes 46088 | tf_op jit(solution)/shard_map/ppermute | solution.py:17
  140.9 6.3 %copy-start.6 = (bf16[2592,96]{1,0:T(8,128)(2,1)S(1)}, bf16[2592,96]{1,0:T(8,128)(2,1)}, u32[]{:S(2)}) copy-start(bf16[2592,96]{1,0:T(8,128)(2,1)} %copy-done.5) | copy-start | bytes 1492996
  140.9 5.5 %collective-permute-start.23 = (bf16[672,128]{1,0:T(8,128)(2,1)S(1)}, bf16[672,128]{1,0:T(8,128)(2,1)S(1)}, u32[]{:S(2)}, u32[]{:S(2)}) collective-permute-start(bf16[672,128]{1,0:T(8,128)(2,1)S(1)} %pad_maximum_fusion.7), channel_id=1, source_target_pairs={{0,4},{1,3},{2,6},{3,1},{4,0},{5,7},{6,2},{7,5},{8,12},{9,11},{10,... | collective-permute-start | bytes 516104 | tf_op jit(solution)/shard_map/ppermute | solution.py:114
  146.5 14.0 %collective-permute-start.24 = (bf16[1344,128]{1,0:T(8,128)(2,1)S(1)}, bf16[1344,128]{1,0:T(8,128)(2,1)S(1)}, u32[]{:S(2)}, u32[]{:S(2)}) collective-permute-start(bf16[1344,128]{1,0:T(8,128)(2,1)S(1)} %pad_maximum_fusion.2), channel_id=1, source_target_pairs={{0,2},{1,5},{2,0},{3,7},{4,6},{5,1},{6,4},{7,3},{8,10},{9,13},{10,... | collective-permute-start | bytes 1032200 | tf_op jit(solution)/shard_map/ppermute | solution.py:114
  154.6 14.9 %all-to-all-start.2 = ((f32[8,64,96]{2,1,0:T(8,128)}), f32[8,64,96]{2,1,0:T(8,128)S(1)}, u32[]{:S(2)}, u32[]{:S(2)}) async-start(f32[8,64,96]{2,1,0:T(8,128)} %broadcast_divide_fusion), calls=%async_computation.2 | async-start | bytes 524288 | tf_op jit(solution)/shard_map/all_to_all | solution.py:189
  160.5 1.0 copy-start.8
  160.7 11.4 %collective-permute-start.25 = (bf16[2688,128]{1,0:T(8,128)(2,1)S(1)}, bf16[2688,128]{1,0:T(8,128)(2,1)S(1)}, u32[]{:S(2)}, u32[]{:S(2)}) collective-permute-start(bf16[2688,128]{1,0:T(8,128)(2,1)S(1)} %pad_maximum_fusion), channel_id=1, source_target_pairs={{0,1},{1,0},{2,3},{3,2},{4,5},{5,4},{6,7},{7,6},{8,9},{9,8},{10,11... | collective-permute-start | bytes 2064392 | tf_op jit(solution)/shard_map/ppermute | solution.py:114
  164.9 4.7 %copy-start.14 = (f32[8,96]{1,0:T(8,128)S(1)}, f32[8,96]{1,0:T(8,128)}, u32[]{:S(2)}) copy-start(f32[8,96]{1,0:T(8,128)} %param.17) | copy-start | bytes 9220

commit v2 on v1

v2 whole, which is shorter than its diff:
```python
import functools

import jax
import jax.numpy as jnp
from jax import lax
from jax.experimental import pallas as pl
from jax.experimental.pallas import tpu as pltpu
from jax.sharding import PartitionSpec as P

SLOT_CAP = 64
LANES = 128
TAPS = 27
GROUP = 8


def with_halo(cells, sides, width):
    for axis, dim in sides:
        count = lax.axis_size(axis)
        ends = count - 1
        head = lax.slice_in_dim(cells, 0, width, axis=dim)
        tail = lax.slice_in_dim(cells, cells.shape[dim] - width, cells.shape[dim], axis=dim)
        cells = jnp.concatenate(
            [
                lax.ppermute(tail, axis, [(i, (i + 1) % count) for i in range(ends)]),
                cells,
                lax.ppermute(head, axis, [((i + 1) % count, i) for i in range(ends)]),
            ],
            axis=dim,
        )
    return cells


def exchange_orders(count):
    bits = [1 << k for k in range(count.bit_length() - 1)]
    rest = bits[1:]
    other = []
    for k in range(0, len(rest), 2):
        other.extend(rest[k : k + 2][::-1])
    return bits, bits[:1] + other


def reduce_everywhere(total, axes):
    count = 1
    for axis in axes:
        count *= lax.axis_size(axis)
    index = lax.axis_index(axes)
    even, odd = exchange_orders(count)
    steps = []
    for mask_even, mask_odd in zip(even, odd):
        pairs = [(i, i ^ (mask_odd if i & 1 else mask_even)) for i in range(count)]
        mask = jnp.where((index & 1) == 1, mask_odd, mask_even)
        steps.append((pairs, ((index & mask) != 0).astype(jnp.int32)))
    for pairs, upper in steps:
        halves = total.reshape(2, total.shape[0] // 2, total.shape[1])
        sent = lax.dynamic_index_in_dim(halves, 1 - upper, 0, keepdims=False)
        kept = lax.dynamic_index_in_dim(halves, upper, 0, keepdims=False)
        received = lax.ppermute(sent.astype(jnp.bfloat16), axes, pairs)
        total = kept + received.astype(jnp.float32)
    whole = total.astype(jnp.bfloat16)
    for pairs, upper in steps[::-1]:
        received = lax.ppermute(whole, axes, pairs)
        first = jnp.where(upper == 1, received, whole)
        second = jnp.where(upper == 1, whole, received)
        whole = jnp.concatenate([first, second], axis=0)
    return whole


def silu_slope(value):
    sigmoid_v = jax.nn.sigmoid(value)
    return sigmoid_v * (1.0 + value * (1.0 - sigmoid_v))


def iota(shape, axis):
    return lax.broadcasted_iota(jnp.int32, shape, axis)


def pack_kernel(blocks, slabs, counts_ref, yaw_ref, jitter_ref, xyz_ref, attr_ref, vox_ref, sent_ref):
    cos_yaw = jnp.cos(yaw_ref[...])
    sin_yaw = jnp.sin(yaw_ref[...])
    x, y, z = (xyz_ref[k : k + 1, :] for k in range(3))
    jitter = jitter_ref[...]
    rotated_x = cos_yaw * x - sin_yaw * y + jitter[:, 0:1]
    rotated_y = sin_yaw * x + cos_yaw * y + jitter[:, 1:2]
    rotated_z = z + jitter[:, 2:3]
    values = jnp.concatenate([rotated_x, rotated_y, rotated_z, attr_ref[...]], axis=0)
    slot = iota((1, SLOT_CAP), 1)
    named = []
    for block in range(blocks):
        piece = vox_ref[:, block * SLOT_CAP : (block + 1) * SLOT_CAP]
        named.append(jnp.where(slot < counts_ref[0, block], piece + 1, 0).astype(jnp.float32))
    none = jnp.zeros((1, SLOT_CAP), jnp.float32)
    named = [none] + named + [none]
    blank = jnp.zeros((8, SLOT_CAP), jnp.float32)
    wide = jnp.concatenate([blank, values, blank], axis=1)
    for block in range(blocks):
        window = wide[:, block * SLOT_CAP : (block + 3) * SLOT_CAP]
        voxels = jnp.concatenate(named[block : block + 3] + [jnp.zeros((5, SLOT_CAP), jnp.float32)], axis=0)
        message = jnp.concatenate([window, voxels], axis=1)
        for slab in range(slabs):
            sent_ref[block * slabs + slab] = message


def fill_copies(copies, value):
    depth, rows, _ = value.shape
    cube = value.reshape(depth * rows // 8, 8, LANES)
    place = iota(cube.shape, 1)
    below = jnp.where(place == 0, 0.0, pltpu.roll(cube, 1, 1))
    above = jnp.where(place == 7, 0.0, pltpu.roll(cube, 7, 1))
    odd_rows = (rows - 8) // 16 * 16
    for s, moved in enumerate((below, cube, above)):
        moved = moved.reshape(depth, rows, LANES)
        copies[s, 0] = moved.astype(jnp.bfloat16)
        copies[s, 1, :, :odd_rows, :] = moved[:, 8 : 8 + odd_rows, :].astype(jnp.bfloat16)


def window(copies, tap, depth, rows, base=0):
    ix, iy, s = tap // 9 + base, tap // 3 % 3 + base, tap % 3
    start = iy // 2 * 16
    part = copies[s, iy % 2, ix : ix + depth, start : start + rows, :]
    return part.reshape(depth * rows, LANES)


def conv_forward(copies, weight_ref, width, depth, rows):
    total = None
    for tap in range(0, TAPS, 2):
        taps = [t for t in (tap, tap + 1) if t < TAPS]
        left = jnp.concatenate([window(copies, t, depth, rows) for t in taps], axis=1)
        right = jnp.concatenate(
            [weight_ref[t * width : t * width + LANES, :] for t in taps], axis=0
        )
        part = jnp.dot(left, right, preferred_element_type=jnp.float32)
        total = part if total is None else total + part
    return total


def conv_back(copies, weight_ref, width, depth, rows):
    total = None
    for tap in range(0, TAPS, 2):
        taps = [t for t in (tap, tap + 1) if t < TAPS]
        left = jnp.concatenate([window(copies, t, depth, rows) for t in taps], axis=1)
        right = jnp.concatenate(
            [weight_ref[(TAPS - 1 - t) * width : (TAPS - t) * width, :] for t in taps], axis=1
        )
        part = lax.dot_general(
            left, right, (((1,), (1,)), ((), ())), preferred_element_type=jnp.float32
        )
        total = part if total is None else total + part
    return total


def kernel_grad(copies, base, partner, width, edge, out_ref, offset):
    turned = partner.astype(jnp.float32).T.astype(jnp.bfloat16)
    for tap in range(0, TAPS, 2):
        taps = [t for t in (tap, tap + 1) if t < TAPS]
        right = jnp.concatenate([window(copies, t, edge, edge * 8, base) for t in taps], axis=1)
        part = jnp.dot(turned, right, preferred_element_type=jnp.float32)
        for k, t in enumerate(taps):
            block = part[:, k * LANES : (k + 1) * LANES].T
            out_ref[offset + t * width : offset + (t + 1) * width, :] = block[:width]


def layer_t(values, weight_t, bias_t):
    total = bias_t
    for k in range(values.shape[0]):
        total = total + weight_t[:, k : k + 1] * values[k : k + 1, :]
    return total


def widen(value):
    return jnp.concatenate(
        [value, jnp.zeros((value.shape[0], LANES - value.shape[1]), value.dtype)], axis=1
    )


def forward_kernel(
    blocks, slabs, edge, width,
    where_ref, got_ref, og_ref, w1_ref, w2_ref, wt_ref, bias_ref,
    grads_ref, hidden_ref, ga_ref, inverse_ref,
    pool_ref, occ_ref, pc_ref, gc_ref,
):
    here = where_ref[0]
    near = edge + 4
    weight_t = wt_ref[...]
    bias_t = bias_ref[...]
    scans = min(blocks, GROUP)
    lanes = scans * SLOT_CAP
    ones = (iota((LANES - width, lanes), 0) == 0).astype(jnp.bfloat16)
    lane = iota((1, LANES), 1)
    for sx in (-1, 0, 1):
        slab = jnp.clip(here + sx, 0, slabs - 1)
        exists = jnp.logical_and(here + sx >= 0, here + sx < slabs)
        for sy in (-1, 0, 1):
            xs = edge if sx == 0 else 2
            ys = edge if sy == 0 else 2
            cells = xs * ys * edge
            row = iota((cells, 1), 0)
            x0 = edge - 2 if sx < 0 else 0
            y0 = edge - 2 if sy < 0 else 0
            voxel = (row // (ys * edge) + x0) * edge * edge + y0 * edge + row % (ys * edge)
            voxel = (voxel + 1).astype(jnp.float32)
            total = jnp.zeros((cells, LANES), jnp.float32)
            for first in range(0, blocks, scans):
                low = (sy + 1) * SLOT_CAP
                got = [got_ref[first + k, slab] for k in range(scans)]
                values = jnp.concatenate([g[:, low : low + SLOT_CAP] for g in got], axis=1)
                names = jnp.concatenate(
                    [g[sy + 1 : sy + 2, 3 * SLOT_CAP :] for g in got], axis=1
                )
                names = jnp.where(exists, names, 0.0)
                pre = layer_t(values, weight_t, bias_t)
                feat = (pre * jax.nn.sigmoid(pre)).astype(jnp.bfloat16)
                feat = jnp.concatenate([feat, ones], axis=0)
                chosen = (voxel == names).astype(jnp.bfloat16)
                total = total + lax.dot_general(
                    chosen, feat, (((1,), (1,)), ((), ())), preferred_element_type=jnp.float32
                )
            count = total[:, width : width + 1]
            divisor = jnp.maximum(count, 1.0)
            pooled = jnp.where(lane < width, total / divisor, 0.0)
            occupied = jnp.broadcast_to((count > 0).astype(jnp.float32), (cells, LANES))
            gx = 0 if sx < 0 else (2 if sx == 0 else edge + 2)
            gy = 0 if sy < 0 else (2 if sy == 0 else edge + 2)
            at = (slice(gx, gx + xs), slice(gy * edge, (gy + ys) * edge))
            pool_ref[at] = pooled.reshape(xs, ys * edge, LANES)
            occ_ref[at] = occupied.reshape(xs, ys * edge, LANES)
            if sx == 0 and sy == 0:
                inverse_ref[...] = jnp.broadcast_to(1.0 / divisor, (cells, LANES))
    fill_copies(pc_ref, pool_ref[...])
    one = edge + 2
    act = conv_forward(pc_ref, w1_ref, width, one, one * edge)
    occ_one = occ_ref[1 : one + 1, edge : edge + one * edge, :].reshape(-1, LANES)
    keep = act.shape[1]
    sigmoid_v = jax.nn.sigmoid(act)
    hidden = occ_one[:, :keep] * (act * sigmoid_v)
    slope = sigmoid_v * (1.0 + act * (1.0 - sigmoid_v))
    fill_copies(hidden_ref, hidden.reshape(one, one * edge, LANES))
    occ = occ_ref[...]
    for z in range(edge):
        pool_ref[:, pl.ds(z, near, stride=edge), :] = og_ref[
            :, :, z * LANES : (z + 1) * LANES
        ].astype(jnp.float32)
    grad_two = jnp.where(occ > 0, pool_ref[...], 0.0)
    fill_copies(gc_ref, grad_two)
    own = grad_two[2 : edge + 2, 2 * edge : (edge + 2) * edge, :].reshape(-1, LANES)
    kernel_grad(hidden_ref, 0, own, width, edge, grads_ref, 0)
    grad_hidden = widen(conv_back(gc_ref, w2_ref, width, one, one * edge))
    grad_act = occ_one * grad_hidden * slope
    fill_copies(ga_ref, grad_act.reshape(one, one * edge, LANES))
    own = ga_ref[1, 1, 1 : edge + 1, : edge * edge, :].reshape(-1, LANES)
    kernel_grad(pc_ref, 1, own, width, edge, grads_ref, TAPS * width)
    used = 2 * TAPS * width
    grads_ref[used:, :] = jnp.zeros((grads_ref.shape[0] - used, LANES), jnp.float32)


def backward_kernel(
    blocks, slabs, edge, width,
    where_ref, got_ref, hidden_ref, ga_ref, inverse_ref, occ_ref, w1_ref, w2_ref, wt_ref, weight_ref, bias_ref,
    block_ref, ret_ref,
    out_ref,
):
    out_ref[...] = conv_forward(hidden_ref, w2_ref, width, edge, edge * edge)
    for z in range(edge):
        at = pl.ds(z, edge * edge, stride=edge)
        block_ref[:, z * LANES : (z + 1) * LANES] = (occ_ref[at, :] * out_ref[at, :]).astype(
            jnp.bfloat16
        )
    grad_pooled = widen(conv_back(ga_ref, w1_ref, width, edge, edge * edge))
    turned = (grad_pooled * inverse_ref[...]).T
    high = turned.astype(jnp.bfloat16)
    low = (turned - high.astype(jnp.float32)).astype(jnp.bfloat16)
    turned = jnp.concatenate([high, low], axis=0)
    here = where_ref[0]
    scans = min(blocks, GROUP)
    voxel = (iota((edge**3, 1), 0) + 1).astype(jnp.float32)
    for first in range(0, blocks, scans):
        got = [got_ref[first + k, here] for k in range(scans)]
        values = jnp.concatenate([g[:, SLOT_CAP : 2 * SLOT_CAP] for g in got], axis=1)
        names = jnp.concatenate([g[1:2, 3 * SLOT_CAP :] for g in got], axis=1)
        pre = layer_t(values, wt_ref[...], bias_ref[...])
        chosen = (voxel == names).astype(jnp.bfloat16)
        both = jnp.dot(turned, chosen, preferred_element_type=jnp.float32)
        grad_pre = (both[:width] + both[LANES : LANES + width]) * silu_slope(pre)
        back = jnp.dot(
            weight_ref[...], grad_pre,
            precision=lax.Precision.HIGHEST, preferred_element_type=jnp.float32,
        )
        for k in range(scans):
            ret_ref[first + k] = back[:, k * SLOT_CAP : (k + 1) * SLOT_CAP]


def vmem(count):
    return [pl.BlockSpec(memory_space=pltpu.VMEM)] * count


def smem():
    return [pl.BlockSpec(memory_space=pltpu.SMEM)]


PARAMS = pltpu.CompilerParams(vmem_limit_bytes=56 * 1024 * 1024)


def shards(
    point_xyz,
    point_attrs,
    scan_yaw,
    scan_jitter,
    slot_counts,
    voxel_ids,
    point_weight,
    point_bias,
    conv_one,
    conv_two,
    out_grad,
):
    blocks = lax.axis_size("blk")
    slabs = lax.axis_size("rep")
    edge = out_grad.shape[0]
    width = conv_one.shape[1]
    here = lax.axis_index("rep").astype(jnp.int32).reshape(1)
    sent = pl.pallas_call(
        functools.partial(pack_kernel, blocks, slabs),
        out_shape=jax.ShapeDtypeStruct((blocks * slabs, 8, 4 * SLOT_CAP), jnp.float32),
        in_specs=smem() + vmem(5),
        out_specs=vmem(1)[0],
        compiler_params=PARAMS,
    )(slot_counts, scan_yaw.reshape(1, 1), scan_jitter, point_xyz, point_attrs, voxel_ids.reshape(1, -1))
    got = lax.all_to_all(sent, ("blk", "rep"), split_axis=0, concat_axis=0, tiled=True)
    got = got.reshape(blocks, slabs, 8, 4 * SLOT_CAP)
    og_wide = with_halo(out_grad, (("blk", 1), ("rep", 0)), 2)
    taps_rows = conv_one.shape[0]
    w1 = jnp.pad(conv_one, ((0, 32), (0, LANES - width)))
    w2 = jnp.pad(conv_two, ((0, 32), (0, 0)))
    weight_t = point_weight.T
    bias_t = point_bias.reshape(-1, 1)
    unit = 8 * blocks * slabs
    rows = 2 * taps_rows + -2 * taps_rows % unit
    near, one = edge + 4, edge + 2
    cells = edge**3
    bf16, f32 = jnp.bfloat16, jnp.float32
    grads, hidden, grad_act, inverse, occ = pl.pallas_call(
        functools.partial(forward_outer, blocks, slabs, edge, width),
        out_shape=(
            jax.ShapeDtypeStruct((rows, LANES), f32),
            jax.ShapeDtypeStruct((3, 2, one, one * edge, LANES), bf16),
            jax.ShapeDtypeStruct((3, 2, one, one * edge, LANES), bf16),
            jax.ShapeDtypeStruct((cells, LANES), f32),
            jax.ShapeDtypeStruct((cells, LANES), f32),
        ),
        in_specs=smem() + vmem(6),
        out_specs=tuple(vmem(5)),
        scratch_shapes=[
            pltpu.VMEM((near, near * edge, LANES), f32),
            pltpu.VMEM((near, near * edge, LANES), f32),
            pltpu.VMEM((3, 2, near, near * edge, LANES), bf16),
            pltpu.VMEM((3, 2, near, near * edge, LANES), bf16),
        ],
        compiler_params=PARAMS,
    )(here, got, og_wide, w1, w2, weight_t, bias_t)
    block_out, back = pl.pallas_call(
        functools.partial(backward_kernel, blocks, slabs, edge, width),
        out_shape=(
            jax.ShapeDtypeStruct((edge * edge, edge * LANES), bf16),
            jax.ShapeDtypeStruct((blocks, 8, SLOT_CAP), f32),
        ),
        in_specs=smem() + vmem(10),
        out_specs=tuple(vmem(2)),
        scratch_shapes=[pltpu.VMEM((cells, LANES), f32)],
        compiler_params=PARAMS,
    )(here, got, hidden, grad_act, inverse, occ, w1, w2, weight_t, point_weight, bias_t)
    summed = reduce_everywhere(grads, ("blk", "rep")).astype(f32)
    two_total = summed[:taps_rows]
    one_total = summed[taps_rows : 2 * taps_rows, :width]
    returned = lax.all_to_all(back, "blk", split_axis=0, concat_axis=0, tiled=True)
    grad_inputs = jnp.transpose(returned, (1, 0, 2)).reshape(8, -1)
    attr_grad = grad_inputs[3:]
    jitter_grad = jnp.sum(grad_inputs[:3], axis=1)[None, :]
    return (block_out.reshape(edge, edge, -1), attr_grad, jitter_grad, one_total, two_total)


def forward_outer(blocks, slabs, edge, width, *refs):
    occ_out = refs[11]
    rest = refs[:11] + refs[12:]
    forward_kernel(blocks, slabs, edge, width, *rest)
    occ_ref = rest[12]
    occ_out[...] = occ_ref[2 : edge + 2, 2 * edge : (edge + 2) * edge, :].reshape(-1, LANES)


def solution(mesh):
    in_specs = (
        P(None, ("blk", "rep")),
        P(None, ("blk", "rep")),
        P(("blk", "rep")),
        P(("blk", "rep"), None),
        P(("blk", "rep"), None),
        P(("blk", "rep")),
        P(),
        P(),
        P(),
        P(),
        P("rep", "blk", None),
    )
    out_specs = (P("rep", "blk", None), P(None, ("blk", "rep")), P(("blk", "rep"), None), P(), P())
    return jax.shard_map(shards, mesh=mesh, in_specs=in_specs, out_specs=out_specs, check_vma=False)
```

time: 176 us -> 124 us (0.70)
  starting transfers between devices: 79.6 us -> 41 us
  matrix products: 27.5 us -> 0 us
  Pallas kernels: 0 us -> 19.8 us
  waiting for transfers between devices: 27.7 us -> 43 us
  other arithmetic: 21.5 us -> 6.51 us
  local copies, waits for them, and re-layouts: 16.3 us -> 11 us
    ppermute x8 -> x2, starting transfers between devices: 32.2 us -> 7.71 us  [with_halo(): lax.ppermute(tail, axis, [(i, (i + 1) % count) for i in range(ends)])]
    pallas_call x0 -> x3, Pallas kernels: none -> 19.8 us  [the longest x1 12.5 us: shards(): pl.pallas_call(functools.partial(forward_outer, blocks, slabs, edge, widt...]
    conv_general_dilated x4 -> x0, matrix products: 17.1 us -> none  [conv_apply(): lax.conv_general_dilated(padded[None], kernel, (1, 1, 1), 'VALID', dimens...]
    ppermute x5, waiting for transfers between devices: 3 us -> 18.6 us  [reduce_everywhere(): received = lax.ppermute(whole, axes, pairs)]
    ppermute x8 -> x2, starting transfers between devices: 10.3 us -> 2.58 us  [with_halo(): lax.ppermute(head, axis, [((i + 1) % count, i) for i in range(ends)])]
    transpose x2 -> x0, matrix products: 7.41 us -> none  [kernel_grad(): jnp.transpose(result, (1, 2, 3, 0, 4))]
    scatter-add x2 -> x0, other arithmetic: 7.32 us -> none  [the longest x1 4.09 us: shards(): jax.ops.segment_sum(jnp.ones_like(vox_flat), vox_flat, voxels + 1)[:voxels]]
    all_to_all x3 -> x2, starting transfers between devices: 17.7 us -> 13.1 us  [the longest x1 7.33 us: shards(): lax.all_to_all(sent, ('blk', 'rep'), split_axis=0, concat_axis=0, tiled=T...]
  transfers between devices with their start and end apart: 29 -> 16, of which waited for: 11 -> 11; matrix products, arithmetic and copies ran while one was open for 19% -> 8% of each run, Pallas kernels for 0% -> 5%
where the time goes in v2:
time: 124 us; the launch traced here: 123 us
  waiting for transfers between devices  43 us (35%)
  starting transfers between devices  41 us (33%)
  Pallas kernels  19.8 us (16%)
  local copies, waits for them, and re-layouts  11 us (9%)
  other arithmetic  6.51 us (5%)
  between operations  1.6 us (1%)
    ppermute x5, waiting for transfers between devices, reduce_everywhere(): received = lax.ppermute(whole, axes, pairs)  18.6 us
    ppermute x5, waiting for transfers between devices, reduce_everywhere(): received = lax.ppermute(sent.astype(jnp.bfloat16), axes, pairs)  16.2 us
    pallas_call x1, Pallas kernels, shards(): pl.pallas_call(functools.partial(forward_outer, blocks, slabs, edge, widt...  12.5 us
    ppermute x5, starting transfers between devices, reduce_everywhere(): received = lax.ppermute(sent.astype(jnp.bfloat16), axes, pairs)  11.5 us
    ppermute x2, starting transfers between devices, with_halo(): lax.ppermute(tail, axis, [(i, (i + 1) % count) for i in range(ends)])  7.71 us
    all_to_all x1, starting transfers between devices, shards(): lax.all_to_all(sent, ('blk', 'rep'), split_axis=0, concat_axis=0, tiled=T...  7.33 us
    all_to_all x1, waiting for transfers between devices, shards(): lax.all_to_all(back, 'blk', split_axis=0, concat_axis=0, tiled=True)  6.58 us
    ppermute x5, starting transfers between devices, reduce_everywhere(): received = lax.ppermute(whole, axes, pairs)  6.06 us
  transfers between devices with their start and end apart: 16, of which 11 were waited for; matrix products, arithmetic and copies ran while one was open for 8% of the time, Pallas kernels for 5%

profile of v2, /device:TPU:0, one launch (start us, length us, event | category | flops | bytes accessed | tf_op | source)
XLA Modules:
  0.0 123.0 jit_solution(12201077393116440667)
XLA Ops:
  1.3 1.8 %shard_map.146 = f32[32,8,256]{2,1,0:T(8,128)} custom-call(s32[1,8]{1,0:T(1,128)} %counts_ref.1, f32[1,1]{1,0:T(1,128)} %bitcast.36.yaw_ref, f32[1,3]{1,0:T(1,128)} %jitter_ref.1, f32[3,512]{1,0:T(4,128)} %xyz_ref.1, f32[5,512]{1,0:T(8,128)} %attr_ref.1, s32[1,512]{1,0:T(1,128)} %bitcast.53), custom_call_target="tpu_custom_call" | custom-call | tf_op jit(solution)/shard_map/pallas_call | solution.py:320
  3.1 7.3 %all-to-all-start = ((f32[32,8,256]{2,1,0:T(8,128)}), f32[32,8,256]{2,1,0:T(8,128)S(1)}, u32[]{:S(2)}, u32[]{:S(2)}) async-start(f32[32,8,256]{2,1,0:T(8,128)} %shard_map.146), calls=%async_computation | async-start | bytes 524288 | tf_op jit(solution)/shard_map/all_to_all | solution.py:327
  10.5 1.0 fusion.7
  11.5 1.3 %collective-permute-start.1 = (bf16[8,2,1024]{2,1,0:T(2,128)(2,1)S(1)}, bf16[8,2,1024]{2,1,0:T(2,128)(2,1)S(1)}, u32[]{:S(2)}, u32[]{:S(2)}) collective-permute-start(bf16[8,2,1024]{2,1,0:T(2,128)(2,1)S(1)} %get-tuple-element.40), channel_id=1, source_target_pairs={{4,0},{8,4},{12,8},{16,12},{20,16},{24,20},{28,24},{5,1},{9,5},{13... | collective-permute-start | bytes 98312 | tf_op jit(solution)/shard_map/ppermute | solution.py:26
  12.8 0.0 copy-start.2
  12.8 4.7 %collective-permute-start = (bf16[8,2,1024]{2,1,0:T(2,128)(2,1)S(1)}, bf16[8,2,1024]{2,1,0:T(2,128)(2,1)S(1)}, u32[]{:S(2)}, u32[]{:S(2)}) collective-permute-start(bf16[8,2,1024]{2,1,0:T(2,128)(2,1)S(1)} %get-tuple-element.39), channel_id=1, source_target_pairs={{0,4},{4,8},{8,12},{12,16},{16,20},{20,24},{24,28},{1,5},{5,9},{9,... | collective-permute-start | bytes 98312 | tf_op jit(solution)/shard_map/ppermute | solution.py:24
  17.5 0.0 collective-permute-done.1
  17.5 1.6 %collective-permute-done = bf16[8,2,1024]{2,1,0:T(2,128)(2,1)S(1)} collective-permute-done((bf16[8,2,1024]{2,1,0:T(2,128)(2,1)S(1)}, bf16[8,2,1024]{2,1,0:T(2,128)(2,1)S(1)}, u32[]{:S(2)}, u32[]{:S(2)}) %collective-permute-start) | collective-permute-done | bytes 32800 | tf_op jit(solution)/shard_map/ppermute | solution.py:24
  19.1 0.8 pad_maximum_fusion.8
  19.9 1.3 %collective-permute-start.3 = (bf16[2,12,1024]{2,1,0:T(8,128)(2,1)S(1)}, bf16[2,12,1024]{2,1,0:T(8,128)(2,1)S(1)}, u32[]{:S(2)}, u32[]{:S(2)}) collective-permute-start(bf16[2,12,1024]{2,1,0:T(8,128)(2,1)S(1)} %get-tuple-element.36), channel_id=1, source_target_pairs={{1,0},{2,1},{3,2},{5,4},{6,5},{7,6},{9,8},{10,9},{11,10},{13,12},{... | collective-permute-start | bytes 147464 | tf_op jit(solution)/shard_map/ppermute | solution.py:26
  21.2 3.0 %collective-permute-start.2 = (bf16[2,12,1024]{2,1,0:T(8,128)(2,1)S(1)}, bf16[2,12,1024]{2,1,0:T(8,128)(2,1)S(1)}, u32[]{:S(2)}, u32[]{:S(2)}) collective-permute-start(bf16[2,12,1024]{2,1,0:T(8,128)(2,1)S(1)} %get-tuple-element.35), channel_id=1, source_target_pairs={{0,1},{1,2},{2,3},{4,5},{5,6},{6,7},{8,9},{9,10},{10,11},{12,13},{... | collective-permute-start | bytes 147464 | tf_op jit(solution)/shard_map/ppermute | solution.py:24
  24.3 0.0 copy-done.3
  24.3 0.3 copy.21
  24.6 0.0 copy-start.4
  24.6 0.0 copy-start.5
  24.6 0.0 copy-start.1
  24.6 1.0 pad.8.refs_3_.w1_ref
  25.6 0.9 pad.9.refs_4_.w2_ref
  26.5 0.7 copy.22
  27.2 0.7 copy.23.refs_6_.bias_ref
  27.9 0.0 collective-permute-done.3
  27.9 0.0 collective-permute-done.2
  27.9 0.9 pad_maximum_fusion.2.refs_2_
  28.8 0.0 all-to-all-done
  28.8 0.7 copy-done
  29.6 12.5 %shard_map.147 = (f32[5376,128]{1,0:T(8,128)}, bf16[3,2,10,80,128]{4,3,2,1,0:T(8,128)(2,1)}, bf16[3,2,10,80,128]{4,3,2,1,0:T(8,128)(2,1)}, f32[512,128]{1,0:T(8,128)}, f32[512,128]{1,0:T(8,128)}) custom-call(s32[1]{0:T(128)} %bitcast.refs_0_.where_ref, f32[8,4,8,256]{3,2,1,0:T(8,128)} %bitcast.39, bf16[12,12,1024]{2,1,0:T(8,128)(2,1)} %pad_maximum_fusion.2.refs_2_, ...), custom_call_target="tpu_custom_call" | custom-call | tf_op jit(solution)/shard_map/pallas_call | solution.py:340
  42.0 1.4 %fusion = bf16[2688,128]{1,0:T(8,128)(2,1)S(1)} fusion(f32[2,2688,128]{2,1,0:T(8,128)} %bitcast.43, s32[]{:T(128)S(6)} %select_n.119), kind=kLoop, calls=%fused_computation.2 | loop fusion | bytes 1376260 | tf_op jit(solution)/shard_map/convert_element_type | solution.py:57
  43.5 1.5 %collective-permute-start.4 = (bf16[2688,128]{1,0:T(8,128)(2,1)S(1)}, bf16[2688,128]{1,0:T(8,128)(2,1)S(1)}, u32[]{:S(2)}, u32[]{:S(2)}) collective-permute-start(bf16[2688,128]{1,0:T(8,128)(2,1)S(1)} %fusion), channel_id=1, source_target_pairs={{0,1},{1,0},{2,3},{3,2},{4,5},{5,4},{6,7},{7,6},{8,9},{9,8},{10,11... | collective-permute-start | bytes 2064392 | tf_op jit(solution)/shard_map/ppermute | solution.py:57
  44.9 1.8 %collective-permute-done.4 = bf16[2688,128]{1,0:T(8,128)(2,1)S(1)} collective-permute-done((bf16[2688,128]{1,0:T(8,128)(2,1)S(1)}, bf16[2688,128]{1,0:T(8,128)(2,1)S(1)}, u32[]{:S(2)}, u32[]{:S(2)}) %collective-permute-start.4) | collective-permute-done | bytes 688160 | tf_op jit(solution)/shard_map/ppermute | solution.py:57
  46.7 1.5 %bitcast_add_fusion = f32[2688,128]{1,0:T(8,128)S(1)} fusion(bf16[2688,128]{1,0:T(8,128)(2,1)S(1)} %collective-permute-done.4, f32[2,2688,128]{2,1,0:T(8,128)} %bitcast.44, s32[]{:T(128)S(6)} %select_n.118), kind=kLoop, calls=%fused_computation | loop fusion | flops 688128 | bytes 3440644 | tf_op jit(solution)/shard_map/add | solution.py:58
  48.2 0.8 collective-permute-start.5
  49.0 6.5 %collective-permute-done.5 = bf16[1344,128]{1,0:T(8,128)(2,1)S(1)} collective-permute-done((bf16[1344,128]{1,0:T(8,128)(2,1)S(1)}, bf16[1344,128]{1,0:T(8,128)(2,1)S(1)}, u32[]{:S(2)}, u32[]{:S(2)}) %collective-permute-start.5) | collective-permute-done | bytes 344096 | tf_op jit(solution)/shard_map/ppermute | solution.py:57
  55.5 0.1 bitcast_add_fusion.1
  55.6 2.5 %collective-permute-start.6 = (bf16[672,128]{1,0:T(8,128)(2,1)S(1)}, bf16[672,128]{1,0:T(8,128)(2,1)S(1)}, u32[]{:S(2)}, u32[]{:S(2)}) collective-permute-start(bf16[672,128]{1,0:T(8,128)(2,1)S(1)} %fusion.3), channel_id=1, source_target_pairs={{0,4},{1,3},{2,6},{3,1},{4,0},{5,7},{6,2},{7,5},{8,12},{9,11},{10,... | collective-permute-start | bytes 516104 | tf_op jit(solution)/shard_map/ppermute | solution.py:57
  58.1 3.4 %collective-permute-done.6 = bf16[672,128]{1,0:T(8,128)(2,1)S(1)} collective-permute-done((bf16[672,128]{1,0:T(8,128)(2,1)S(1)}, bf16[672,128]{1,0:T(8,128)(2,1)S(1)}, u32[]{:S(2)}, u32[]{:S(2)}) %collective-permute-start.6) | collective-permute-done | bytes 172064 | tf_op jit(solution)/shard_map/ppermute | solution.py:57
  61.5 3.8 %collective-permute-start.7 = (bf16[336,128]{1,0:T(8,128)(2,1)S(1)}, bf16[336,128]{1,0:T(8,128)(2,1)S(1)}, u32[]{:S(2)}, u32[]{:S(2)}) collective-permute-start(bf16[336,128]{1,0:T(8,128)(2,1)S(1)} %fusion.4), channel_id=1, source_target_pairs={{0,8},{1,17},{2,10},{3,19},{4,12},{5,21},{6,14},{7,23},{8,0},{9,25... | collective-permute-start | bytes 258056 | tf_op jit(solution)/shard_map/ppermute | solution.py:57
  65.3 2.5 %collective-permute-done.7 = bf16[336,128]{1,0:T(8,128)(2,1)S(1)} collective-permute-done((bf16[336,128]{1,0:T(8,128)(2,1)S(1)}, bf16[336,128]{1,0:T(8,128)(2,1)S(1)}, u32[]{:S(2)}, u32[]{:S(2)}) %collective-permute-start.7) | collective-permute-done | bytes 86048 | tf_op jit(solution)/shard_map/ppermute | solution.py:57
  67.8 3.0 %collective-permute-start.8 = (bf16[168,128]{1,0:T(8,128)(2,1)S(1)}, bf16[168,128]{1,0:T(8,128)(2,1)S(1)}, u32[]{:S(2)}, u32[]{:S(2)}) collective-permute-start(bf16[168,128]{1,0:T(8,128)(2,1)S(1)} %fusion.6), channel_id=1, source_target_pairs={{0,16},{1,9},{2,18},{3,11},{4,20},{5,13},{6,22},{7,15},{8,24},{9,1... | collective-permute-start | bytes 129032 | tf_op jit(solution)/shard_map/ppermute | solution.py:57
  70.8 2.1 %collective-permute-done.8 = bf16[168,128]{1,0:T(8,128)(2,1)S(1)} collective-permute-done((bf16[168,128]{1,0:T(8,128)(2,1)S(1)}, bf16[168,128]{1,0:T(8,128)(2,1)S(1)}, u32[]{:S(2)}, u32[]{:S(2)}) %collective-permute-start.8) | collective-permute-done | bytes 43040 | tf_op jit(solution)/shard_map/ppermute | solution.py:57
  72.9 3.1 %collective-permute-start.9 = (bf16[168,128]{1,0:T(8,128)(2,1)S(1)}, bf16[168,128]{1,0:T(8,128)(2,1)S(1)}, u32[]{:S(2)}, u32[]{:S(2)}) collective-permute-start(bf16[168,128]{1,0:T(8,128)(2,1)S(1)} %fusion.5), channel_id=1, source_target_pairs={{0,16},{1,9},{2,18},{3,11},{4,20},{5,13},{6,22},{7,15},{8,24},{9,1... | collective-permute-start | bytes 129032 | tf_op jit(solution)/shard_map/ppermute | solution.py:61
  76.0 2.4 %collective-permute-done.9 = bf16[168,128]{1,0:T(8,128)(2,1)S(1)} collective-permute-done((bf16[168,128]{1,0:T(8,128)(2,1)S(1)}, bf16[168,128]{1,0:T(8,128)(2,1)S(1)}, u32[]{:S(2)}, u32[]{:S(2)}) %collective-permute-start.9) | collective-permute-done | bytes 43040 | tf_op jit(solution)/shard_map/ppermute | solution.py:61
  78.4 2.0 %collective-permute-start.10 = (bf16[336,128]{1,0:T(8,128)(2,1)S(1)}, bf16[336,128]{1,0:T(8,128)(2,1)S(1)}, u32[]{:S(2)}, u32[]{:S(2)}) collective-permute-start(bf16[336,128]{1,0:T(8,128)(2,1)S(1)} %pad_maximum_fusion.5), channel_id=1, source_target_pairs={{0,8},{1,17},{2,10},{3,19},{4,12},{5,21},{6,14},{7,23},{8,0},{9,25... | collective-permute-start | bytes 258056 | tf_op jit(solution)/shard_map/ppermute | solution.py:61
  80.4 2.5 %collective-permute-done.10 = bf16[336,128]{1,0:T(8,128)(2,1)S(1)} collective-permute-done((bf16[336,128]{1,0:T(8,128)(2,1)S(1)}, bf16[336,128]{1,0:T(8,128)(2,1)S(1)}, u32[]{:S(2)}, u32[]{:S(2)}) %collective-permute-start.10) | collective-permute-done | bytes 86048 | tf_op jit(solution)/shard_map/ppermute | solution.py:61
  83.0 0.4 collective-permute-start.11
  83.4 7.0 %collective-permute-done.11 = bf16[672,128]{1,0:T(8,128)(2,1)S(1)} collective-permute-done((bf16[672,128]{1,0:T(8,128)(2,1)S(1)}, bf16[672,128]{1,0:T(8,128)(2,1)S(1)}, u32[]{:S(2)}, u32[]{:S(2)}) %collective-permute-start.11) | collective-permute-done | bytes 172064 | tf_op jit(solution)/shard_map/ppermute | solution.py:61
  90.3 0.1 broadcast_select_fusion.5
  90.4 0.6 collective-permute-start.12
  91.0 6.7 %collective-permute-done.12 = bf16[1344,128]{1,0:T(8,128)(2,1)S(1)} collective-permute-done((bf16[1344,128]{1,0:T(8,128)(2,1)S(1)}, bf16[1344,128]{1,0:T(8,128)(2,1)S(1)}, u32[]{:S(2)}, u32[]{:S(2)}) %collective-permute-start.12) | collective-permute-done | bytes 344096 | tf_op jit(solution)/shard_map/ppermute | solution.py:61
  97.8 0.2 broadcast_select_fusion.3
  98.0 0.1 collective-permute-start.13
  98.1 5.5 %shard_map.148 = (bf16[64,1024]{1,0:T(8,128)(2,1)}, f32[8,8,64]{2,1,0:T(8,128)}) custom-call(s32[1]{0:T(128)} %bitcast.refs_0_.where_ref, f32[8,4,8,256]{3,2,1,0:T(8,128)} %bitcast.40, bf16[3,2,10,80,128]{4,3,2,1,0:T(8,128)(2,1)} %get-tuple-element.12.hidden_ref, bf16[3,2,10,80,128]{4,3,2,1,0:T(8,128)(2,1)} %get-tuple-element.13.ga_ref, ...), custom_call_target="tpu_custom_call" | custom-call | tf_op jit(solution)/shard_map/pallas_call | solution.py:359
  103.6 1.4 %reshape.62 = f32[8,1,512]{2,1,0:T(1,128)} reshape(f32[8,8,64]{2,1,0:T(8,128)} %get-tuple-element.17) | data formatting | bytes 32768
  105.1 5.8 %all-to-all-start.1 = ((f32[8,1,512]{2,1,0:T(1,128)}), f32[8,1,512]{2,1,0:T(1,128)S(1)}, u32[]{:S(2)}, u32[]{:S(2)}) async-start(f32[8,1,512]{2,1,0:T(1,128)} %reshape.62), calls=%async_computation.1 | async-start | bytes 32768 | tf_op jit(solution)/shard_map/all_to_all | solution.py:373
  110.9 6.6 %all-to-all-done.1 = f32[8,1,512]{2,1,0:T(1,128)S(1)} async-done(((f32[8,1,512]{2,1,0:T(1,128)}), f32[8,1,512]{2,1,0:T(1,128)S(1)}, u32[]{:S(2)}, u32[]{:S(2)}) %all-to-all-start.1) | async-done | bytes 16416 | tf_op jit(solution)/shard_map/all_to_all | solution.py:373
  117.4 0.5 broadcast.4
  118.0 0.7 reduce.1
  118.6 0.1 reshape.63
  118.7 0.7 slice.33
  119.4 0.6 slice_reduce_fusion
  120.0 0.0 collective-permute-done.13
  120.1 0.3 broadcast_select_fusion.1
  120.3 0.1 maximum_convert_fusion
  120.4 1.1 fusion.1
  121.6 1.4 %copy.26 = f32[2592,96]{0,1:T(8,128)} copy(f32[2592,96]{1,0:T(8,128)S(1)} %maximum_convert_fusion) | data formatting | bytes 1990656
  (21 shorter events, 0.4 us)
Async XLA Ops:
  0.6 23.6 %copy-start.3 = (bf16[2592,96]{0,1:T(8,128)(2,1)S(1)}, bf16[2592,96]{0,1:T(8,128)(2,1)}, u32[]{:S(2)}) copy-start(bf16[2592,96]{0,1:T(8,128)(2,1)} %param.19) | copy-start | bytes 1492996
  3.1 25.7 %all-to-all-start = ((f32[32,8,256]{2,1,0:T(8,128)}), f32[32,8,256]{2,1,0:T(8,128)S(1)}, u32[]{:S(2)}, u32[]{:S(2)}) async-start(f32[32,8,256]{2,1,0:T(8,128)} %shard_map.146), calls=%async_computation | async-start | bytes 524288 | tf_op jit(solution)/shard_map/all_to_all | solution.py:327
  11.5 6.0 %collective-permute-start.1 = (bf16[8,2,1024]{2,1,0:T(2,128)(2,1)S(1)}, bf16[8,2,1024]{2,1,0:T(2,128)(2,1)S(1)}, u32[]{:S(2)}, u32[]{:S(2)}) collective-permute-start(bf16[8,2,1024]{2,1,0:T(2,128)(2,1)S(1)} %get-tuple-element.40), channel_id=1, source_target_pairs={{4,0},{8,4},{12,8},{16,12},{20,16},{24,20},{28,24},{5,1},{9,5},{13... | collective-permute-start | bytes 98312 | tf_op jit(solution)/shard_map/ppermute | solution.py:26
  12.8 12.8 %copy-start.2 = (bf16[2592,128]{1,0:T(8,128)(2,1)S(1)}, bf16[2592,128]{1,0:T(8,128)(2,1)}, u32[]{:S(2)}) copy-start(bf16[2592,128]{1,0:T(8,128)(2,1)} %param.20) | copy-start | bytes 1990660
  12.8 6.3 %collective-permute-start = (bf16[8,2,1024]{2,1,0:T(2,128)(2,1)S(1)}, bf16[8,2,1024]{2,1,0:T(2,128)(2,1)S(1)}, u32[]{:S(2)}, u32[]{:S(2)}) collective-permute-start(bf16[8,2,1024]{2,1,0:T(2,128)(2,1)S(1)} %get-tuple-element.39), channel_id=1, source_target_pairs={{0,4},{4,8},{8,12},{12,16},{16,20},{20,24},{24,28},{1,5},{5,9},{9,... | collective-permute-start | bytes 98312 | tf_op jit(solution)/shard_map/ppermute | solution.py:24
  19.9 8.0 %collective-permute-start.3 = (bf16[2,12,1024]{2,1,0:T(8,128)(2,1)S(1)}, bf16[2,12,1024]{2,1,0:T(8,128)(2,1)S(1)}, u32[]{:S(2)}, u32[]{:S(2)}) collective-permute-start(bf16[2,12,1024]{2,1,0:T(8,128)(2,1)S(1)} %get-tuple-element.36), channel_id=1, source_target_pairs={{1,0},{2,1},{3,2},{5,4},{6,5},{7,6},{9,8},{10,9},{11,10},{13,12},{... | collective-permute-start | bytes 147464 | tf_op jit(solution)/shard_map/ppermute | solution.py:26
  21.2 6.7 %collective-permute-start.2 = (bf16[2,12,1024]{2,1,0:T(8,128)(2,1)S(1)}, bf16[2,12,1024]{2,1,0:T(8,128)(2,1)S(1)}, u32[]{:S(2)}, u32[]{:S(2)}) collective-permute-start(bf16[2,12,1024]{2,1,0:T(8,128)(2,1)S(1)} %get-tuple-element.35), channel_id=1, source_target_pairs={{0,1},{1,2},{2,3},{4,5},{5,6},{6,7},{8,9},{9,10},{10,11},{12,13},{... | collective-permute-start | bytes 147464 | tf_op jit(solution)/shard_map/ppermute | solution.py:24
  24.6 1.9 %copy-start.4 = (f32[8,96]{1,0:T(8,128)S(1)}, f32[8,96]{1,0:T(8,128)}, u32[]{:S(2)}) copy-start(f32[8,96]{1,0:T(8,128)} %weight_ref.1) | copy-start | bytes 9220
  24.6 2.6 %copy-start.5 = (f32[96]{0:T(128)S(1)}, f32[96]{0:T(128)}, u32[]{:S(2)}) copy-start(f32[96]{0:T(128)} %param.18) | copy-start | bytes 1156
  24.6 3.3 %copy-start.1 = (bf16[8,8,1024]{2,1,0:T(8,128)(2,1)S(1)}, bf16[8,8,1024]{2,1,0:T(8,128)(2,1)}, u32[]{:S(2)}) copy-start(bf16[8,8,1024]{2,1,0:T(8,128)(2,1)} %param.21) | copy-start | bytes 393220
  28.8 0.7 copy-start
  43.5 3.2 %collective-permute-start.4 = (bf16[2688,128]{1,0:T(8,128)(2,1)S(1)}, bf16[2688,128]{1,0:T(8,128)(2,1)S(1)}, u32[]{:S(2)}, u32[]{:S(2)}) collective-permute-start(bf16[2688,128]{1,0:T(8,128)(2,1)S(1)} %fusion), channel_id=1, source_target_pairs={{0,1},{1,0},{2,3},{3,2},{4,5},{5,4},{6,7},{7,6},{8,9},{9,8},{10,11... | collective-permute-start | bytes 2064392 | tf_op jit(solution)/shard_map/ppermute | solution.py:57
  48.2 7.3 %collective-permute-start.5 = (bf16[1344,128]{1,0:T(8,128)(2,1)S(1)}, bf16[1344,128]{1,0:T(8,128)(2,1)S(1)}, u32[]{:S(2)}, u32[]{:S(2)}) collective-permute-start(bf16[1344,128]{1,0:T(8,128)(2,1)S(1)} %fusion.2), channel_id=1, source_target_pairs={{0,2},{1,5},{2,0},{3,7},{4,6},{5,1},{6,4},{7,3},{8,10},{9,13},{10,... | collective-permute-start | bytes 1032200 | tf_op jit(solution)/shard_map/ppermute | solution.py:57
  55.6 5.9 %collective-permute-start.6 = (bf16[672,128]{1,0:T(8,128)(2,1)S(1)}, bf16[672,128]{1,0:T(8,128)(2,1)S(1)}, u32[]{:S(2)}, u32[]{:S(2)}) collective-permute-start(bf16[672,128]{1,0:T(8,128)(2,1)S(1)} %fusion.3), channel_id=1, source_target_pairs={{0,4},{1,3},{2,6},{3,1},{4,0},{5,7},{6,2},{7,5},{8,12},{9,11},{10,... | collective-permute-start | bytes 516104 | tf_op jit(solution)/shard_map/ppermute | solution.py:57
  61.5 6.3 %collective-permute-start.7 = (bf16[336,128]{1,0:T(8,128)(2,1)S(1)}, bf16[336,128]{1,0:T(8,128)(2,1)S(1)}, u32[]{:S(2)}, u32[]{:S(2)}) collective-permute-start(bf16[336,128]{1,0:T(8,128)(2,1)S(1)} %fusion.4), channel_id=1, source_target_pairs={{0,8},{1,17},{2,10},{3,19},{4,12},{5,21},{6,14},{7,23},{8,0},{9,25... | collective-permute-start | bytes 258056 | tf_op jit(solution)/shard_map/ppermute | solution.py:57
  67.8 5.1 %collective-permute-start.8 = (bf16[168,128]{1,0:T(8,128)(2,1)S(1)}, bf16[168,128]{1,0:T(8,128)(2,1)S(1)}, u32[]{:S(2)}, u32[]{:S(2)}) collective-permute-start(bf16[168,128]{1,0:T(8,128)(2,1)S(1)} %fusion.6), channel_id=1, source_target_pairs={{0,16},{1,9},{2,18},{3,11},{4,20},{5,13},{6,22},{7,15},{8,24},{9,1... | collective-permute-start | bytes 129032 | tf_op jit(solution)/shard_map/ppermute | solution.py:57
  72.9 5.4 %collective-permute-start.9 = (bf16[168,128]{1,0:T(8,128)(2,1)S(1)}, bf16[168,128]{1,0:T(8,128)(2,1)S(1)}, u32[]{:S(2)}, u32[]{:S(2)}) collective-permute-start(bf16[168,128]{1,0:T(8,128)(2,1)S(1)} %fusion.5), channel_id=1, source_target_pairs={{0,16},{1,9},{2,18},{3,11},{4,20},{5,13},{6,22},{7,15},{8,24},{9,1... | collective-permute-start | bytes 129032 | tf_op jit(solution)/shard_map/ppermute | solution.py:61
  78.4 4.6 %collective-permute-start.10 = (bf16[336,128]{1,0:T(8,128)(2,1)S(1)}, bf16[336,128]{1,0:T(8,128)(2,1)S(1)}, u32[]{:S(2)}, u32[]{:S(2)}) collective-permute-start(bf16[336,128]{1,0:T(8,128)(2,1)S(1)} %pad_maximum_fusion.5), channel_id=1, source_target_pairs={{0,8},{1,17},{2,10},{3,19},{4,12},{5,21},{6,14},{7,23},{8,0},{9,25... | collective-permute-start | bytes 258056 | tf_op jit(solution)/shard_map/ppermute | solution.py:61
  83.0 7.3 %collective-permute-start.11 = (bf16[672,128]{1,0:T(8,128)(2,1)S(1)}, bf16[672,128]{1,0:T(8,128)(2,1)S(1)}, u32[]{:S(2)}, u32[]{:S(2)}) collective-permute-start(bf16[672,128]{1,0:T(8,128)(2,1)S(1)} %pad_maximum_fusion.4), channel_id=1, source_target_pairs={{0,4},{1,3},{2,6},{3,1},{4,0},{5,7},{6,2},{7,5},{8,12},{9,11},{10,... | collective-permute-start | bytes 516104 | tf_op jit(solution)/shard_map/ppermute | solution.py:61
  90.4 7.3 %collective-permute-start.12 = (bf16[1344,128]{1,0:T(8,128)(2,1)S(1)}, bf16[1344,128]{1,0:T(8,128)(2,1)S(1)}, u32[]{:S(2)}, u32[]{:S(2)}) collective-permute-start(bf16[1344,128]{1,0:T(8,128)(2,1)S(1)} %pad_maximum_fusion.3), channel_id=1, source_target_pairs={{0,2},{1,5},{2,0},{3,7},{4,6},{5,1},{6,4},{7,3},{8,10},{9,13},{10,... | collective-permute-start | bytes 1032200 | tf_op jit(solution)/shard_map/ppermute | solution.py:61
  98.0 22.1 %collective-permute-start.13 = (bf16[2688,128]{1,0:T(8,128)(2,1)S(1)}, bf16[2688,128]{1,0:T(8,128)(2,1)S(1)}, u32[]{:S(2)}, u32[]{:S(2)}) collective-permute-start(bf16[2688,128]{1,0:T(8,128)(2,1)S(1)} %pad_maximum_fusion), channel_id=1, source_target_pairs={{0,1},{1,0},{2,3},{3,2},{4,5},{5,4},{6,7},{7,6},{8,9},{9,8},{10,11... | collective-permute-start | bytes 2064392 | tf_op jit(solution)/shard_map/ppermute | solution.py:61
  105.1 12.4 %all-to-all-start.1 = ((f32[8,1,512]{2,1,0:T(1,128)}), f32[8,1,512]{2,1,0:T(1,128)S(1)}, u32[]{:S(2)}, u32[]{:S(2)}) async-start(f32[8,1,512]{2,1,0:T(1,128)} %reshape.62), calls=%async_computation.1 | async-start | bytes 32768 | tf_op jit(solution)/shard_map/all_to_all | solution.py:373

commit v3 on v2

v3 whole, which is shorter than its diff:
```python
import functools

import jax
import jax.numpy as jnp
from jax import lax
from jax.experimental import pallas as pl
from jax.experimental.pallas import tpu as pltpu
from jax.sharding import PartitionSpec as P

SLOT_CAP = 64
LANES = 128
TAPS = 27
GROUP = 8


def rims(cells, dim, width):
    head = lax.slice_in_dim(cells, 0, width, axis=dim)
    tail = lax.slice_in_dim(cells, cells.shape[dim] - width, cells.shape[dim], axis=dim)
    return head, tail


def neighbours(head, tail, axis):
    ends = lax.axis_size(axis) - 1
    return (
        lax.ppermute(tail, axis, [(i, i + 1) for i in range(ends)]),
        lax.ppermute(head, axis, [(i + 1, i) for i in range(ends)]),
    )


def slab_steps():
    count = lax.axis_size("rep")
    masks = [1 << k for k in range(count.bit_length() - 1)]
    return [[(i, i ^ mask) for i in range(count)] for mask in masks]


def silu_slope(value):
    sigmoid_v = jax.nn.sigmoid(value)
    return sigmoid_v * (1.0 + value * (1.0 - sigmoid_v))


def iota(shape, axis):
    return lax.broadcasted_iota(jnp.int32, shape, axis)


def pack_kernel(blocks, slabs, counts_ref, yaw_ref, jitter_ref, xyz_ref, attr_ref, vox_ref, sent_ref):
    cos_yaw = jnp.cos(yaw_ref[...])
    sin_yaw = jnp.sin(yaw_ref[...])
    x, y, z = (xyz_ref[k : k + 1, :] for k in range(3))
    jitter = jitter_ref[...]
    rotated_x = cos_yaw * x - sin_yaw * y + jitter[:, 0:1]
    rotated_y = sin_yaw * x + cos_yaw * y + jitter[:, 1:2]
    rotated_z = z + jitter[:, 2:3]
    values = jnp.concatenate([rotated_x, rotated_y, rotated_z, attr_ref[...]], axis=0)
    slot = iota((1, SLOT_CAP), 1)
    named = []
    for block in range(blocks):
        piece = vox_ref[:, block * SLOT_CAP : (block + 1) * SLOT_CAP]
        named.append(jnp.where(slot < counts_ref[0, block], piece + 1, 0).astype(jnp.float32))
    none = jnp.zeros((1, SLOT_CAP), jnp.float32)
    named = [none] + named + [none]
    blank = jnp.zeros((8, SLOT_CAP), jnp.float32)
    wide = jnp.concatenate([blank, values, blank], axis=1)
    for block in range(blocks):
        window = wide[:, block * SLOT_CAP : (block + 3) * SLOT_CAP]
        voxels = jnp.concatenate(named[block : block + 3] + [jnp.zeros((5, SLOT_CAP), jnp.float32)], axis=0)
        message = jnp.concatenate([window, voxels], axis=1)
        for slab in range(slabs):
            sent_ref[block * slabs + slab] = message


def fill_copies(copies, value):
    depth, rows, _ = value.shape
    cube = value.reshape(depth * rows // 8, 8, LANES)
    place = iota(cube.shape, 1)
    below = jnp.where(place == 0, 0.0, pltpu.roll(cube, 1, 1))
    above = jnp.where(place == 7, 0.0, pltpu.roll(cube, 7, 1))
    odd_rows = (rows - 8) // 16 * 16
    for s, moved in enumerate((below, cube, above)):
        moved = moved.reshape(depth, rows, LANES)
        copies[s, 0] = moved.astype(jnp.bfloat16)
        copies[s, 1, :, :odd_rows, :] = moved[:, 8 : 8 + odd_rows, :].astype(jnp.bfloat16)


def window(copies, tap, depth, rows, base=0):
    ix, iy, s = tap // 9 + base, tap // 3 % 3 + base, tap % 3
    start = iy // 2 * 16
    part = copies[s, iy % 2, ix : ix + depth, start : start + rows, :]
    return part.reshape(depth * rows, LANES)


def pairs_of_taps():
    return [[t for t in (tap, tap + 1) if t < TAPS] for tap in range(0, TAPS, 2)]


def conv_forward(copies, weight_ref, width, depth, rows):
    total = None
    for taps in pairs_of_taps():
        left = jnp.concatenate([window(copies, t, depth, rows) for t in taps], axis=1)
        if taps[-1] == TAPS - 1:
            left = left[:, : (len(taps) - 1) * LANES + width]
        right = jnp.concatenate(
            [
                weight_ref[t * width : min(t * width + LANES, TAPS * width), :]
                for t in taps
            ],
            axis=0,
        )
        part = jnp.dot(left, right, preferred_element_type=jnp.float32)
        total = part if total is None else total + part
    return widen(total)


def conv_back(copies, weight_ref, width, depth, rows):
    total = None
    for taps in pairs_of_taps():
        left = jnp.concatenate([window(copies, t, depth, rows) for t in taps], axis=1)
        right = jnp.concatenate(
            [
                widen(weight_ref[(TAPS - 1 - t) * width : (TAPS - t) * width, :])
                for t in taps
            ],
            axis=1,
        )
        part = lax.dot_general(
            left, right, (((1,), (1,)), ((), ())), preferred_element_type=jnp.float32
        )
        total = part if total is None else total + part
    return widen(total)


def grad_products(copies, base, partner, edge):
    turned = partner.astype(jnp.float32).T.astype(jnp.bfloat16)
    for taps in pairs_of_taps():
        right = jnp.concatenate([window(copies, t, edge, edge * 8, base) for t in taps], axis=1)
        part = jnp.dot(turned, right, preferred_element_type=jnp.float32)
        for k, t in enumerate(taps):
            yield t, part[:, k * LANES : (k + 1) * LANES]


def turned_grad(copies, base, partner, width, edge, out_ref):
    for t, block in grad_products(copies, base, partner, edge):
        out_ref[t * width : (t + 1) * width, :] = block.T[:width]


def packed_grad(copies, base, partner, width, edge, out_ref, first):
    lane = iota((width, LANES), 1)
    held = None
    for t, block in grad_products(copies, base, partner, edge):
        block = block[:width]
        start = t * width
        tile, shift = start // LANES, start % LANES
        moved = block if shift == 0 else pltpu.roll(block, shift, 1)
        held = moved if held is None else jnp.where(lane < shift, held, moved)
        if shift + width >= LANES:
            out_ref[first + tile * width : first + (tile + 1) * width, :] = held
            held = moved if shift + width > LANES else None
    if held is not None:
        tile = TAPS * width // LANES
        held = jnp.where(lane < TAPS * width % LANES, held, 0.0)
        out_ref[first + tile * width : first + (tile + 1) * width, :] = held


def layer_t(values, weight_t):
    depth = values.shape[0]
    total = weight_t[:, depth : depth + 1]
    for k in range(depth):
        total = total + weight_t[:, k : k + 1] * values[k : k + 1, :]
    return total


def widen(value):
    if value.shape[1] == LANES:
        return value
    return jnp.concatenate(
        [value, jnp.zeros((value.shape[0], LANES - value.shape[1]), value.dtype)], axis=1
    )


def turned_layer(weight_ref, bias_ref):
    rows = jnp.concatenate([weight_ref[...], bias_ref[...]], axis=0)
    rows = widen(rows)
    blank = jnp.zeros((LANES - rows.shape[0], LANES), jnp.float32)
    return jnp.concatenate([rows, blank], axis=0).T[: weight_ref.shape[1]]


def lay_out(target, piece, x0, y0, edge):
    depth, rows, _ = piece.shape
    for z in range(edge):
        target[x0 : x0 + depth, pl.ds(y0 * edge + z, rows, stride=edge), :] = piece[
            :, :, z * LANES : (z + 1) * LANES
        ].astype(jnp.float32)


def forward_kernel(
    blocks, slabs, edge, width,
    got_ref, og_ref, below_ref, above_ref, left_ref, right_ref, w1_ref, w2_ref, weight_ref, bias_ref,
    kept_ref, moving_ref, hidden_ref, ga_ref, occupied_ref, inverse_ref,
    pool_ref, occ_ref, pc_ref, gc_ref, grads_ref,
):
    here = lax.axis_index("rep")
    weight_t = turned_layer(weight_ref, bias_ref)
    scans = min(blocks, GROUP)
    lanes = scans * SLOT_CAP
    ones = (iota((LANES - width, lanes), 0) == 0).astype(jnp.bfloat16)
    lane = iota((1, LANES), 1)
    for sx in (-1, 0, 1):
        slab = jnp.clip(here + sx, 0, slabs - 1)
        exists = jnp.logical_and(here + sx >= 0, here + sx < slabs)
        for sy in (-1, 0, 1):
            xs = edge if sx == 0 else 2
            ys = edge if sy == 0 else 2
            cells = xs * ys * edge
            row = iota((cells, 1), 0)
            x0 = edge - 2 if sx < 0 else 0
            y0 = edge - 2 if sy < 0 else 0
            voxel = (row // (ys * edge) + x0) * edge * edge + y0 * edge + row % (ys * edge)
            voxel = (voxel + 1).astype(jnp.float32)
            total = jnp.zeros((cells, LANES), jnp.float32)
            for first in range(0, blocks, scans):
                low = (sy + 1) * SLOT_CAP
                got = [got_ref[first + k, slab] for k in range(scans)]
                values = jnp.concatenate([g[:, low : low + SLOT_CAP] for g in got], axis=1)
                names = jnp.concatenate(
                    [g[sy + 1 : sy + 2, 3 * SLOT_CAP :] for g in got], axis=1
                )
                names = jnp.where(exists, names, 0.0)
                pre = layer_t(values, weight_t)
                feat = (pre * jax.nn.sigmoid(pre)).astype(jnp.bfloat16)
                feat = jnp.concatenate([feat, ones], axis=0)
                chosen = (voxel == names).astype(jnp.bfloat16)
                total = total + lax.dot_general(
                    chosen, feat, (((1,), (1,)), ((), ())), preferred_element_type=jnp.float32
                )
            count = total[:, width : width + 1]
            divisor = jnp.maximum(count, 1.0)
            pooled = jnp.where(lane < width, total / divisor, 0.0)
            occupied = jnp.broadcast_to((count > 0).astype(jnp.float32), (cells, LANES))
            gx = 0 if sx < 0 else (2 if sx == 0 else edge + 2)
            gy = 0 if sy < 0 else (2 if sy == 0 else edge + 2)
            at = (slice(gx, gx + xs), slice(gy * edge, (gy + ys) * edge))
            pool_ref[at] = pooled.reshape(xs, ys * edge, LANES)
            occ_ref[at] = occupied.reshape(xs, ys * edge, LANES)
            if sx == 0 and sy == 0:
                inverse_ref[...] = jnp.broadcast_to(1.0 / divisor, (cells, LANES))
    fill_copies(pc_ref, pool_ref[...])
    one = edge + 2
    act = conv_forward(pc_ref, w1_ref, width, one, one * edge)
    occ_one = occ_ref[1 : one + 1, edge : edge + one * edge, :].reshape(-1, LANES)
    sigmoid_v = jax.nn.sigmoid(act)
    hidden = occ_one * (act * sigmoid_v)
    slope = occ_one * (sigmoid_v * (1.0 + act * (1.0 - sigmoid_v)))
    fill_copies(hidden_ref, hidden.reshape(one, one * edge, LANES))
    lay_out(pool_ref, og_ref[...], 2, 2, edge)
    lay_out(pool_ref, below_ref[...], 0, 2, edge)
    lay_out(pool_ref, above_ref[...], edge + 2, 2, edge)
    lay_out(pool_ref, left_ref[...], 0, 0, edge)
    lay_out(pool_ref, right_ref[...], 0, edge + 2, edge)
    grad_two = jnp.where(occ_ref[...] > 0, pool_ref[...], 0.0)
    fill_copies(gc_ref, grad_two)
    grad_hidden = conv_back(gc_ref, w2_ref, width, one, one * edge)
    fill_copies(ga_ref, (grad_hidden * slope).reshape(one, one * edge, LANES))
    own = gc_ref[1, 0, 2 : edge + 2, 2 * edge : (edge + 2) * edge, :].reshape(-1, LANES)
    turned_grad(hidden_ref, 0, own, width, edge, grads_ref)
    own = ga_ref[1, 1, 1 : edge + 1, : edge * edge, :].reshape(-1, LANES)
    packed_grad(pc_ref, 1, own, width, edge, grads_ref, TAPS * width)
    used = TAPS * width - (-TAPS * width // LANES) * width
    if used < grads_ref.shape[0]:
        grads_ref[used:, :] = jnp.zeros((grads_ref.shape[0] - used, LANES), jnp.float32)
    divide(grads_ref, 0, kept_ref, moving_ref)
    occupied_ref[...] = occ_ref[2 : edge + 2, 2 * edge : (edge + 2) * edge, :].reshape(-1, LANES)


def divide(total_ref, step, kept_ref, moving_ref):
    half = kept_ref.shape[0]
    upper = (lax.axis_index("rep") >> step) & 1
    kept_ref[...] = total_ref[pl.ds(pl.multiple_of(upper * half, 8), half), :]
    moving = total_ref[pl.ds(pl.multiple_of((1 - upper) * half, 8), half), :]
    moving_ref[...] = moving.astype(jnp.bfloat16)


def fold_kernel(step, own_ref, received_ref, kept_ref, moving_ref, total_ref):
    total_ref[...] = own_ref[...] + received_ref[...].astype(jnp.float32)
    divide(total_ref, step, kept_ref, moving_ref)


def message_kernel(blocks, own_ref, received_ref, back_ref, sent_ref):
    rows = own_ref.shape[0] // blocks
    for block in range(blocks):
        at = slice(block * rows, (block + 1) * rows)
        total = own_ref[at, :] + received_ref[at, :].astype(jnp.float32)
        back = back_ref[block].astype(jnp.float32)
        sent_ref[block] = jnp.concatenate([total, back], axis=0).astype(jnp.bfloat16)


def split_bits(value):
    high = value.astype(jnp.bfloat16)
    return high, (value - high.astype(jnp.float32)).astype(jnp.bfloat16)


def backward_kernel(
    blocks, edge, width,
    got_ref, hidden_ref, ga_ref, occupied_ref, inverse_ref, w1_ref, w2_ref, weight_ref, bias_ref,
    ret_ref, block_ref,
    out_ref,
):
    out_ref[...] = occupied_ref[...] * conv_forward(hidden_ref, w2_ref, width, edge, edge * edge)
    for z in range(edge):
        at = pl.ds(z, edge * edge, stride=edge)
        block_ref[:, z * LANES : (z + 1) * LANES] = out_ref[at, :].astype(jnp.bfloat16)
    grad_pooled = conv_back(ga_ref, w1_ref, width, edge, edge * edge)
    turned = jnp.concatenate(split_bits((grad_pooled * inverse_ref[...]).T), axis=0)
    weight_t = turned_layer(weight_ref, bias_ref)
    here = lax.axis_index("rep")
    scans = min(blocks, GROUP)
    voxel = (iota((edge**3, 1), 0) + 1).astype(jnp.float32)
    for first in range(0, blocks, scans):
        got = [got_ref[first + k, here] for k in range(scans)]
        values = jnp.concatenate([g[:, SLOT_CAP : 2 * SLOT_CAP] for g in got], axis=1)
        names = jnp.concatenate([g[1:2, 3 * SLOT_CAP :] for g in got], axis=1)
        pre = layer_t(values, weight_t)
        chosen = (voxel == names).astype(jnp.bfloat16)
        both = jnp.dot(turned, chosen, preferred_element_type=jnp.float32)
        grad_pre = (both[:width] + both[LANES : LANES + width]) * silu_slope(pre)
        back = jnp.dot(
            weight_ref[...], grad_pre,
            precision=lax.Precision.HIGHEST, preferred_element_type=jnp.float32,
        )
        for k in range(scans):
            piece = back[:, k * SLOT_CAP : (k + 1) * SLOT_CAP]
            ret_ref[first + k] = jnp.concatenate(split_bits(piece), axis=1)


def points_kernel(blocks, ret_ref, attr_ref, jitter_ref):
    pieces = []
    for block in range(blocks):
        both = ret_ref[block].astype(jnp.float32)
        pieces.append(both[:, :SLOT_CAP] + both[:, SLOT_CAP:])
    grad_in = jnp.concatenate(pieces, axis=1)
    attr_ref[...] = grad_in[3:]
    sums = jnp.broadcast_to(jnp.sum(grad_in, axis=1, keepdims=True), (8, LANES))
    row, lane = iota((8, LANES), 0), iota((8, LANES), 1)
    jitter_ref[...] = jnp.sum(jnp.where(row == lane, sums, 0.0), axis=0, keepdims=True)[:, :3]


def finish_kernel(blocks, rows, width, *refs):
    pieces = refs[:-3]
    one_ref, two_ref, flat_ref = refs[-3:]
    here, turned = lax.axis_index("rep"), 0
    count = len(pieces).bit_length() - 1
    for k in range(count):
        turned = turned + (((here >> k) & 1) << (count - 1 - k))
    for k, got_ref in enumerate(pieces):
        for block in range(blocks):
            at = pl.multiple_of(((turned ^ k) * blocks + block) * rows, 8)
            flat_ref[pl.ds(at, rows), :] = got_ref[block].astype(jnp.float32)
    first, lanes = two_ref.shape[0], one_ref.shape[1]
    two_ref[...] = flat_ref[:first, :]
    for tile in range(-(-lanes // LANES)):
        upto = min(LANES, lanes - tile * LANES)
        one_ref[:, tile * LANES : tile * LANES + upto] = flat_ref[
            first + tile * width : first + (tile + 1) * width, :upto
        ]


def cost(micros):
    return pl.CostEstimate(flops=int(micros * 4e8), bytes_accessed=0, transcendentals=0)


def call(kernel, operands, out_shape, scratch=(), scalars=0, micros=1, grant=24):
    vmem = pl.BlockSpec(memory_space=pltpu.VMEM)
    smem = pl.BlockSpec(memory_space=pltpu.SMEM)
    count = len(out_shape) if isinstance(out_shape, tuple) else 0
    return pl.pallas_call(
        kernel,
        out_shape=out_shape,
        in_specs=[smem] * scalars + [vmem] * (len(operands) - scalars),
        out_specs=(vmem,) * count if count else vmem,
        scratch_shapes=list(scratch),
        compiler_params=pltpu.CompilerParams(vmem_limit_bytes=grant * 1024 * 1024),
        cost_estimate=cost(micros),
    )(*operands)


def shards(
    point_xyz,
    point_attrs,
    scan_yaw,
    scan_jitter,
    slot_counts,
    voxel_ids,
    point_weight,
    point_bias,
    conv_one,
    conv_two,
    out_grad,
):
    blocks = lax.axis_size("blk")
    slabs = lax.axis_size("rep")
    edge = out_grad.shape[0]
    width = conv_one.shape[1]
    bf16, f32 = jnp.bfloat16, jnp.float32
    near, one = edge + 4, edge + 2
    cells = edge**3
    bias = point_bias.reshape(1, -1)
    taps_rows = conv_one.shape[0]
    unit = 8 * blocks * slabs
    used = taps_rows - (-taps_rows // LANES) * width
    rows = used + -used % unit
    copies = jax.ShapeDtypeStruct((3, 2, one, one * edge, LANES), bf16)
    shaped = lambda *shape: jax.ShapeDtypeStruct(shape, f32)
    tie = lax.optimization_barrier

    sent = call(
        functools.partial(pack_kernel, blocks, slabs),
        (slot_counts, scan_yaw.reshape(1, 1), scan_jitter, point_xyz, point_attrs, voxel_ids.reshape(1, -1)),
        shaped(blocks * slabs, 8, 4 * SLOT_CAP),
        scalars=1,
        micros=1,
        grant=60,
    )
    sent, out_late = tie((sent, out_grad))
    with jax.named_scope("points_out"):
        got = lax.all_to_all(sent, ("blk", "rep"), split_axis=0, concat_axis=0, tiled=True)
    got = got.reshape(blocks, slabs, 8, 4 * SLOT_CAP)
    with jax.named_scope("rim_rep"):
        below, above = neighbours(*rims(out_late, 0, 2), "rep")
    tall = jnp.concatenate([below, out_late, above], axis=0)
    with jax.named_scope("rim_blk"):
        left, right = neighbours(*rims(tall, 1, 2), "blk")

    halves = lambda step: (
        shaped(rows >> (step + 1), LANES),
        jax.ShapeDtypeStruct((rows >> (step + 1), LANES), bf16),
    )
    kept, moving, hidden, grad_act, occupied, inverse = call(
        functools.partial(forward_kernel, blocks, slabs, edge, width),
        (got, out_grad, below, above, left, right, conv_one, conv_two, point_weight, bias),
        (*halves(0), copies, copies, shaped(cells, LANES), shaped(cells, LANES)),
        scratch=[
            pltpu.VMEM((near, near * edge, LANES), f32),
            pltpu.VMEM((near, near * edge, LANES), f32),
            pltpu.VMEM((3, 2, near, near * edge, LANES), bf16),
            pltpu.VMEM((3, 2, near, near * edge, LANES), bf16),
            pltpu.VMEM((rows, LANES), f32),
        ],
        micros=9,
    )

    steps = slab_steps()
    for step, pairs in enumerate(steps):
        if step:
            kept, moving = call(
                functools.partial(fold_kernel, step),
                (kept, received),
                halves(step),
                scratch=[pltpu.VMEM((rows >> step, LANES), f32)],
                micros=0.5,
            )
        moving, inverse = tie((moving, inverse))
        with jax.named_scope("halve"):
            received = lax.ppermute(moving, "rep", pairs)

    back, block_out = call(
        functools.partial(backward_kernel, blocks, edge, width),
        (got, hidden, grad_act, occupied, inverse, conv_one, conv_two, point_weight, bias),
        (
            jax.ShapeDtypeStruct((blocks, 8, 2 * SLOT_CAP), bf16),
            jax.ShapeDtypeStruct((edge * edge, edge * LANES), bf16),
        ),
        scratch=[pltpu.VMEM((cells, LANES), f32)],
        micros=4,
    )
    message = call(
        functools.partial(message_kernel, blocks),
        (kept, received, back),
        jax.ShapeDtypeStruct((blocks, rows // (blocks * slabs) + 8, LANES), bf16),
        micros=0.5,
    )
    arrived = lax.all_to_all(message, "blk", split_axis=0, concat_axis=0, tiled=True)
    shared = arrived.shape[1] - 8
    summed = jnp.sum(arrived[:, :shared].astype(f32), axis=0).astype(bf16)
    spread = jnp.broadcast_to(summed[None], (blocks, shared, LANES))
    whole = lax.all_to_all(spread, "blk", split_axis=0, concat_axis=0, tiled=True)

    attr_grad, jitter_grad = call(
        functools.partial(points_kernel, blocks),
        (arrived[:, shared:],),
        (shaped(5, blocks * SLOT_CAP), shaped(1, 3)),
        micros=1,
    )

    pieces = [whole]
    for pairs in steps[::-1]:
        pieces = pieces + [lax.ppermute(piece, "rep", pairs) for piece in pieces]

    one_total, two_total = call(
        functools.partial(finish_kernel, blocks, shared, width),
        tuple(pieces),
        (shaped(width, taps_rows), shaped(taps_rows, LANES)),
        scratch=[pltpu.VMEM((rows, LANES), f32)],
        micros=1,
    )
    return (block_out.reshape(edge, edge, -1), attr_grad, jitter_grad, one_total.T, two_total)


def solution(mesh):
    in_specs = (
        P(None, ("blk", "rep")),
        P(None, ("blk", "rep")),
        P(("blk", "rep")),
        P(("blk", "rep"), None),
        P(("blk", "rep"), None),
        P(("blk", "rep")),
        P(),
        P(),
        P(),
        P(),
        P("rep", "blk", None),
    )
    out_specs = (P("rep", "blk", None), P(None, ("blk", "rep")), P(("blk", "rep"), None), P(), P())
    return jax.shard_map(shards, mesh=mesh, in_specs=in_specs, out_specs=out_specs, check_vma=False)
```

time: 124 us -> 83.7 us (0.68)
  blocking collectives: 0 us -> 30.1 us
  waiting for transfers between devices: 43 us -> 17.1 us
  starting transfers between devices: 41 us -> 20.2 us
  local copies, waits for them, and re-layouts: 11 us -> 0.48 us
  other arithmetic: 6.51 us -> 0.04 us
  Pallas kernels: 19.8 us -> 14 us
    all_to_all x0 -> x2, blocking collectives: none -> 30.1 us  [the longest x1 17.4 us: shards(): lax.all_to_all(message, 'blk', split_axis=0, concat_axis=0, tiled=True)]
    ppermute x14 -> x9, waiting for transfers between devices: 36.4 us -> 17.1 us  [the longest x2 6.97 us: shards(): received = lax.ppermute(moving, 'rep', pairs)]
    ppermute x14 -> x9, starting transfers between devices: 27.9 us -> 13.1 us  [the longest x2 7.08 us: neighbours(): lax.ppermute(tail, axis, [(i, i + 1) for i in range(ends)])]
    all_to_all x1 -> x0, waiting for transfers between devices: 6.58 us -> none  [shards(): lax.all_to_all(back, 'blk', split_axis=0, concat_axis=0, tiled=True)]
    all_to_all x1 -> x0, starting transfers between devices: 5.81 us -> none  [shards(): lax.all_to_all(back, 'blk', split_axis=0, concat_axis=0, tiled=True)]
    pallas_call x3 -> x7, Pallas kernels: 19.8 us -> 14 us  [call(): pl.pallas_call(kernel, out_shape=out_shape, in_specs=[smem] * scalars + [...]
    unnamed x17 -> x13, local copies, waits for them, and re-layouts: 4.69 us -> 0.36 us
    pad x2 -> x0, local copies, waits for them, and re-layouts: 1.87 us -> none  [the longest x1 0.97 us: shards(): w1 = jnp.pad(conv_one, ((0, 32), (0, LANES - width)))]
  transfers between devices with their start and end apart: 16 -> 10, of which waited for: 11 -> 6; matrix products, arithmetic and copies ran while one was open for 8% -> 0% of each run, Pallas kernels for 5% -> 5%
where the time goes in v3:
time: 83.7 us; the launch traced here: 83.3 us
  blocking collectives  30.1 us (36%)
  starting transfers between devices  20.2 us (24%)
  waiting for transfers between devices  17.1 us (20%)
  Pallas kernels  14 us (17%)
  between operations  1.47 us (2%)
    all_to_all x1, blocking collectives, shards(): lax.all_to_all(message, 'blk', split_axis=0, concat_axis=0, tiled=True)  17.4 us
    pallas_call x7, Pallas kernels, call(): pl.pallas_call(kernel, out_shape=out_shape, in_specs=[smem] * scalars + [...  14 us
    all_to_all x1, blocking collectives, shards(): lax.all_to_all(spread, 'blk', split_axis=0, concat_axis=0, tiled=True)  12.7 us
    all_to_all x1, starting transfers between devices, shards(): lax.all_to_all(sent, ('blk', 'rep'), split_axis=0, concat_axis=0, tiled=T...  7.13 us
    ppermute x2, starting transfers between devices, neighbours(): lax.ppermute(tail, axis, [(i, i + 1) for i in range(ends)])  7.08 us
    ppermute x2, waiting for transfers between devices, shards(): received = lax.ppermute(moving, 'rep', pairs)  6.97 us
    ppermute x3, waiting for transfers between devices, shards(): pieces = pieces + [lax.ppermute(piece, 'rep', pairs) for piece in pieces]  6.93 us
    ppermute x2, starting transfers between devices, shards(): received = lax.ppermute(moving, 'rep', pairs)  2.78 us
  transfers between devices with their start and end apart: 10, of which 6 were waited for; matrix products, arithmetic and copies ran while one was open for 0% of the time, Pallas kernels for 5%

profile of v3, /device:TPU:0, one launch (start us, length us, event | category | flops | bytes accessed | tf_op | source)
XLA Modules:
  0.0 83.3 jit_solution(5581446843915239742)
XLA Ops:
  0.6 0.0 copy-start
  1.3 0.0 copy-start.4
  1.3 1.8 %shard_map.146 = f32[32,8,256]{2,1,0:T(8,128)} custom-call(s32[1,8]{1,0:T(1,128)} %counts_ref.1, f32[1,1]{1,0:T(1,128)} %bitcast.6.yaw_ref, f32[1,3]{1,0:T(1,128)} %jitter_ref.1, f32[3,512]{1,0:T(4,128)} %xyz_ref.1, f32[5,512]{1,0:T(8,128)} %attr_ref.1, s32[1,512]{1,0:T(1,128)} %bitcast.11), custom_call_target="tpu_custom_call" | custom-call | flops 400000000 | tf_op jit(solution)/shard_map/pallas_call | solution.py:373
  3.1 0.0 copy-done
  3.1 0.0 copy-start.1
  3.1 0.0 copy-start.2
  3.1 0.0 copy-start.3
  3.2 2.5 %collective-permute-start = (bf16[2,8,1024]{2,1,0:T(8,128)(2,1)S(1)}, bf16[2,8,1024]{2,1,0:T(8,128)(2,1)S(1)}, u32[]{:S(2)}, u32[]{:S(2)}) collective-permute-start(bf16[2,8,1024]{2,1,0:T(8,128)(2,1)S(1)} %get-tuple-element.48), channel_id=1, source_target_pairs={{0,1},{1,2},{2,3},{4,5},{5,6},{6,7},{8,9},{9,10},{10,11},{12,13},{... | collective-permute-start | bytes 98312 | tf_op jit(solution)/shard_map/rim_rep/ppermute | solution.py:25
  5.7 7.1 %all-to-all-start = ((f32[32,8,256]{2,1,0:T(8,128)}), f32[32,8,256]{2,1,0:T(8,128)S(1)}, u32[]{:S(2)}, u32[]{:S(2)}) async-start(f32[32,8,256]{2,1,0:T(8,128)} %shard_map.146), calls=%async_computation | async-start | bytes 524288 | tf_op jit(solution)/shard_map/points_out/all_to_all | solution.py:423
  12.8 1.3 %collective-permute-start.1 = (bf16[2,8,1024]{2,1,0:T(8,128)(2,1)S(1)}, bf16[2,8,1024]{2,1,0:T(8,128)(2,1)S(1)}, u32[]{:S(2)}, u32[]{:S(2)}) collective-permute-start(bf16[2,8,1024]{2,1,0:T(8,128)(2,1)S(1)} %get-tuple-element.47), channel_id=1, source_target_pairs={{1,0},{2,1},{3,2},{5,4},{6,5},{7,6},{9,8},{10,9},{11,10},{13,12},{... | collective-permute-start | bytes 98312 | tf_op jit(solution)/shard_map/rim_rep/ppermute | solution.py:26
  14.1 0.0 collective-permute-done.below_ref
  14.2 1.8 %collective-permute-done.1.above_ref = bf16[2,8,1024]{2,1,0:T(8,128)(2,1)S(1)} collective-permute-done((bf16[2,8,1024]{2,1,0:T(8,128)(2,1)S(1)}, bf16[2,8,1024]{2,1,0:T(8,128)(2,1)S(1)}, u32[]{:S(2)}, u32[]{:S(2)}) %collective-permute-start.1) | collective-permute-done | bytes 32800 | tf_op jit(solution)/shard_map/rim_rep/ppermute | solution.py:26
  15.9 0.1 fusion
  16.0 1.3 %collective-permute-start.3 = (bf16[12,2,1024]{2,1,0:T(2,128)(2,1)S(1)}, bf16[12,2,1024]{2,1,0:T(2,128)(2,1)S(1)}, u32[]{:S(2)}, u32[]{:S(2)}) collective-permute-start(bf16[12,2,1024]{2,1,0:T(2,128)(2,1)S(1)} %get-tuple-element.45), channel_id=1, source_target_pairs={{4,0},{8,4},{12,8},{16,12},{20,16},{24,20},{28,24},{5,1},{9,5},{13... | collective-permute-start | bytes 147464 | tf_op jit(solution)/shard_map/rim_blk/ppermute | solution.py:26
  17.3 4.5 %collective-permute-start.2 = (bf16[12,2,1024]{2,1,0:T(2,128)(2,1)S(1)}, bf16[12,2,1024]{2,1,0:T(2,128)(2,1)S(1)}, u32[]{:S(2)}, u32[]{:S(2)}) collective-permute-start(bf16[12,2,1024]{2,1,0:T(2,128)(2,1)S(1)} %get-tuple-element.46), channel_id=1, source_target_pairs={{0,4},{4,8},{8,12},{12,16},{16,20},{20,24},{24,28},{1,5},{5,9},{9,... | collective-permute-start | bytes 147464 | tf_op jit(solution)/shard_map/rim_blk/ppermute | solution.py:25
  21.9 0.0 copy-done.4
  21.9 0.3 copy.16.w1_ref
  22.2 0.0 collective-permute-done.3.right_ref
  22.2 1.4 %collective-permute-done.2.left_ref = bf16[12,2,1024]{2,1,0:T(2,128)(2,1)S(1)} collective-permute-done((bf16[12,2,1024]{2,1,0:T(2,128)(2,1)S(1)}, bf16[12,2,1024]{2,1,0:T(2,128)(2,1)S(1)}, u32[]{:S(2)}, u32[]{:S(2)}) %collective-permute-start.2) | collective-permute-done | bytes 49184 | tf_op jit(solution)/shard_map/rim_blk/ppermute | solution.py:25
  23.6 0.0 all-to-all-done
  23.6 0.0 copy-done.1
  23.6 0.0 copy-done.2
  23.6 0.0 copy-done.3
  23.6 6.5 %shard_map.147 = (f32[2304,128]{1,0:T(8,128)S(1)}, bf16[2304,128]{1,0:T(8,128)(2,1)S(1)}, bf16[3,2,10,80,128]{4,3,2,1,0:T(8,128)(2,1)S(1)}, bf16[3,2,10,80,128]{...) custom-call(f32[8,4,8,256]{3,2,1,0:T(8,128)S(1)} %bitcast.7, ...), custom_call_target="tpu_custom_call" | custom-call | flops 3600000000 | tf_op jit(solution)/shard_map/pallas_call | solution.py:373
  30.1 1.8 %collective-permute-start.4 = (bf16[2304,128]{1,0:T(8,128)(2,1)S(1)}, bf16[2304,128]{1,0:T(8,128)(2,1)S(1)}, u32[]{:S(2)}, u32[]{:S(2)}) collective-permute-start(bf16[2304,128]{1,0:T(8,128)(2,1)S(1)} %get-tuple-element.33), channel_id=1, source_target_pairs={{0,1},{1,0},{2,3},{3,2},{4,5},{5,4},{6,7},{7,6},{8,9},{9,8},{10,11... | collective-permute-start | bytes 1769480 | tf_op jit(solution)/shard_map/halve/ppermute | solution.py:461
  31.9 1.6 %collective-permute-done.4.received_ref = bf16[2304,128]{1,0:T(8,128)(2,1)S(1)} collective-permute-done((bf16[2304,128]{1,0:T(8,128)(2,1)S(1)}, bf16[2304,128]{1,0:T(8,128)(2,1)S(1)}, u32[]{:S(2)}, u32[]{:S(2)}) %collective-permute-start.4) | collective-permute-done | bytes 589856 | tf_op jit(solution)/shard_map/halve/ppermute | solution.py:461
  33.6 0.3 shard_map.148
  33.8 1.0 %collective-permute-start.5 = (bf16[1152,128]{1,0:T(8,128)(2,1)S(1)}, bf16[1152,128]{1,0:T(8,128)(2,1)S(1)}, u32[]{:S(2)}, u32[]{:S(2)}) collective-permute-start(bf16[1152,128]{1,0:T(8,128)(2,1)S(1)} %get-tuple-element.39), channel_id=1, source_target_pairs={{0,2},{1,3},{2,0},{3,1},{4,6},{5,7},{6,4},{7,5},{8,10},{9,11},{10,... | collective-permute-start | bytes 884744 | tf_op jit(solution)/shard_map/halve/ppermute | solution.py:461
  34.8 3.0 %shard_map.149 = (bf16[8,8,128]{2,1,0:T(8,128)(2,1)S(1)}, bf16[64,1024]{1,0:T(8,128)(2,1)}) custom-call(f32[8,4,8,256]{3,2,1,0:T(8,128)S(1)} %bitcast.8, bf16[3,2,10,80,128]{4,3,2,1,0:T(8,128)(2,1)S(1)} %get-tuple-element.27.hidden_ref, bf16[3,2,10,80,128]{4,3,2,1,0:T(8,128)(2,1)S(1)} %get-tuple-element.28.ga_ref, ...), custom_call_target="tpu_custom_call" | custom-call | flops 1600000000 | tf_op jit(solution)/shard_map/pallas_call | solution.py:373
  37.8 5.3 %collective-permute-done.5.received_ref = bf16[1152,128]{1,0:T(8,128)(2,1)S(1)} collective-permute-done((bf16[1152,128]{1,0:T(8,128)(2,1)S(1)}, bf16[1152,128]{1,0:T(8,128)(2,1)S(1)}, u32[]{:S(2)}, u32[]{:S(2)}) %collective-permute-start.5) | collective-permute-done | bytes 294944 | tf_op jit(solution)/shard_map/halve/ppermute | solution.py:461
  43.2 0.1 shard_map.150
  43.2 17.4 %all_to_all.15 = bf16[8,152,128]{2,1,0:T(8,128)(2,1)S(1)} all-to-all(bf16[8,152,128]{2,1,0:T(8,128)(2,1)S(1)} %shard_map.150), channel_id=1, replica_groups=mesh['blk'=8,'rep'=4] {'blk'}, dimensions={0} | all-to-all | bytes 622592 | tf_op jit(solution)/shard_map/all_to_all | solution.py:479
  60.7 12.7 %all_to_all.16.refs_0_ = bf16[8,144,128]{2,1,0:T(8,128)(2,1)S(1)} all-to-all(bf16[8,144,128]{2,1,0:T(8,128)(2,1)S(1)} %broadcast_in_dim.2), channel_id=1, replica_groups=mesh['blk'=8,'rep'=4] {'blk'}, dimensions={0} | all-to-all | bytes 589824 | tf_op jit(solution)/shard_map/all_to_all | solution.py:483
  73.4 0.6 collective-permute-start.6
  74.0 0.0 collective-permute-start.7
  74.0 6.1 %collective-permute-done.6.refs_1_ = bf16[8,144,128]{2,1,0:T(8,128)(2,1)S(1)} collective-permute-done((bf16[8,144,128]{2,1,0:T(8,128)(2,1)S(1)}, bf16[8,144,128]{2,1,0:T(8,128)(2,1)S(1)}, u32[]{:S(2)}, u32[]{:S(2)}) %collective-permute-start.6) | collective-permute-done | bytes 294944 | tf_op jit(solution)/shard_map/ppermute | solution.py:494
  80.1 0.0 collective-permute-start.8
  80.1 0.8 shard_map.151
  80.9 0.0 collective-permute-done.7.refs_2_
  80.9 0.8 collective-permute-done.8.refs_3_
  81.7 1.6 %shard_map.152 = (f32[96,2592]{1,0:T(8,128)}, f32[2592,128]{1,0:T(8,128)}) custom-call(bf16[8,144,128]{2,1,0:T(8,128)(2,1)S(1)} %all_to_all.16.refs_0_, bf16[8,144,128]{2,1,0:T(8,128)(2,1)S(1)} %collective-permute-done.6.refs_1_, bf16[8,144,128]{2,1,0:T(8,128)(2,1)S(1)} %collective-permute-done.7.refs_2_, bf16[8,144,128]{2,1,0:T(8,128)(2,1)S(1)} %collective-permute-done.8.refs_3_), custom_call_target="tpu_custom_call" | custom-call | flops 400000000 | tf_op jit(solution)/shard_map/pallas_call | solution.py:373
  (7 shorter events, 0.1 us)
Async XLA Ops:
  0.6 2.5 %copy-start = (bf16[8,8,1024]{2,1,0:T(8,128)(2,1)S(1)}, bf16[8,8,1024]{2,1,0:T(8,128)(2,1)}, u32[]{:S(2)}) copy-start(bf16[8,8,1024]{2,1,0:T(8,128)(2,1)} %og_ref.1) | copy-start | bytes 393220
  1.3 20.5 %copy-start.4 = (bf16[2592,96]{0,1:T(8,128)(2,1)S(1)}, bf16[2592,96]{0,1:T(8,128)(2,1)}, u32[]{:S(2)}) copy-start(bf16[2592,96]{0,1:T(8,128)(2,1)} %param.19) | copy-start | bytes 1492996
  3.1 20.5 %copy-start.1 = (bf16[2592,128]{1,0:T(8,128)(2,1)S(1)}, bf16[2592,128]{1,0:T(8,128)(2,1)}, u32[]{:S(2)}) copy-start(bf16[2592,128]{1,0:T(8,128)(2,1)} %w2_ref.3) | copy-start | bytes 1990660
  3.1 20.5 %copy-start.2 = (f32[8,96]{1,0:T(8,128)S(1)}, f32[8,96]{1,0:T(8,128)}, u32[]{:S(2)}) copy-start(f32[8,96]{1,0:T(8,128)} %weight_ref.3) | copy-start | bytes 9220
  3.1 20.5 %copy-start.3 = (f32[96]{0:T(128)S(1)}, f32[96]{0:T(128)}, u32[]{:S(2)}) copy-start(f32[96]{0:T(128)} %param.18) | copy-start | bytes 1156
  3.2 11.0 %collective-permute-start = (bf16[2,8,1024]{2,1,0:T(8,128)(2,1)S(1)}, bf16[2,8,1024]{2,1,0:T(8,128)(2,1)S(1)}, u32[]{:S(2)}, u32[]{:S(2)}) collective-permute-start(bf16[2,8,1024]{2,1,0:T(8,128)(2,1)S(1)} %get-tuple-element.48), channel_id=1, source_target_pairs={{0,1},{1,2},{2,3},{4,5},{5,6},{6,7},{8,9},{9,10},{10,11},{12,13},{... | collective-permute-start | bytes 98312 | tf_op jit(solution)/shard_map/rim_rep/ppermute | solution.py:25
  5.7 17.9 %all-to-all-start = ((f32[32,8,256]{2,1,0:T(8,128)}), f32[32,8,256]{2,1,0:T(8,128)S(1)}, u32[]{:S(2)}, u32[]{:S(2)}) async-start(f32[32,8,256]{2,1,0:T(8,128)} %shard_map.146), calls=%async_computation | async-start | bytes 524288 | tf_op jit(solution)/shard_map/points_out/all_to_all | solution.py:423
  12.8 3.1 %collective-permute-start.1 = (bf16[2,8,1024]{2,1,0:T(8,128)(2,1)S(1)}, bf16[2,8,1024]{2,1,0:T(8,128)(2,1)S(1)}, u32[]{:S(2)}, u32[]{:S(2)}) collective-permute-start(bf16[2,8,1024]{2,1,0:T(8,128)(2,1)S(1)} %get-tuple-element.47), channel_id=1, source_target_pairs={{1,0},{2,1},{3,2},{5,4},{6,5},{7,6},{9,8},{10,9},{11,10},{13,12},{... | collective-permute-start | bytes 98312 | tf_op jit(solution)/shard_map/rim_rep/ppermute | solution.py:26
  16.0 6.2 %collective-permute-start.3 = (bf16[12,2,1024]{2,1,0:T(2,128)(2,1)S(1)}, bf16[12,2,1024]{2,1,0:T(2,128)(2,1)S(1)}, u32[]{:S(2)}, u32[]{:S(2)}) collective-permute-start(bf16[12,2,1024]{2,1,0:T(2,128)(2,1)S(1)} %get-tuple-element.45), channel_id=1, source_target_pairs={{4,0},{8,4},{12,8},{16,12},{20,16},{24,20},{28,24},{5,1},{9,5},{13... | collective-permute-start | bytes 147464 | tf_op jit(solution)/shard_map/rim_blk/ppermute | solution.py:26
  17.3 6.3 %collective-permute-start.2 = (bf16[12,2,1024]{2,1,0:T(2,128)(2,1)S(1)}, bf16[12,2,1024]{2,1,0:T(2,128)(2,1)S(1)}, u32[]{:S(2)}, u32[]{:S(2)}) collective-permute-start(bf16[12,2,1024]{2,1,0:T(2,128)(2,1)S(1)} %get-tuple-element.46), channel_id=1, source_target_pairs={{0,4},{4,8},{8,12},{12,16},{16,20},{20,24},{24,28},{1,5},{5,9},{9,... | collective-permute-start | bytes 147464 | tf_op jit(solution)/shard_map/rim_blk/ppermute | solution.py:25
  30.1 3.4 %collective-permute-start.4 = (bf16[2304,128]{1,0:T(8,128)(2,1)S(1)}, bf16[2304,128]{1,0:T(8,128)(2,1)S(1)}, u32[]{:S(2)}, u32[]{:S(2)}) collective-permute-start(bf16[2304,128]{1,0:T(8,128)(2,1)S(1)} %get-tuple-element.33), channel_id=1, source_target_pairs={{0,1},{1,0},{2,3},{3,2},{4,5},{5,4},{6,7},{7,6},{8,9},{9,8},{10,11... | collective-permute-start | bytes 1769480 | tf_op jit(solution)/shard_map/halve/ppermute | solution.py:461
  33.8 9.4 %collective-permute-start.5 = (bf16[1152,128]{1,0:T(8,128)(2,1)S(1)}, bf16[1152,128]{1,0:T(8,128)(2,1)S(1)}, u32[]{:S(2)}, u32[]{:S(2)}) collective-permute-start(bf16[1152,128]{1,0:T(8,128)(2,1)S(1)} %get-tuple-element.39), channel_id=1, source_target_pairs={{0,2},{1,3},{2,0},{3,1},{4,6},{5,7},{6,4},{7,5},{8,10},{9,11},{10,... | collective-permute-start | bytes 884744 | tf_op jit(solution)/shard_map/halve/ppermute | solution.py:461
  73.4 6.7 %collective-permute-start.6 = (bf16[8,144,128]{2,1,0:T(8,128)(2,1)S(1)}, bf16[8,144,128]{2,1,0:T(8,128)(2,1)S(1)}, u32[]{:S(2)}, u32[]{:S(2)}) collective-permute-start(bf16[8,144,128]{2,1,0:T(8,128)(2,1)S(1)} %all_to_all.16.refs_0_), channel_id=1, source_target_pairs={{0,2},{1,3},{2,0},{3,1},{4,6},{5,7},{6,4},{7,5},{8,10},{9,11},{10,... | collective-permute-start | bytes 884744 | tf_op jit(solution)/shard_map/ppermute | solution.py:494
  74.0 6.9 %collective-permute-start.7 = (bf16[8,144,128]{2,1,0:T(8,128)(2,1)S(1)}, bf16[8,144,128]{2,1,0:T(8,128)(2,1)S(1)}, u32[]{:S(2)}, u32[]{:S(2)}) collective-permute-start(bf16[8,144,128]{2,1,0:T(8,128)(2,1)S(1)} %all_to_all.16.refs_0_), channel_id=1, source_target_pairs={{0,1},{1,0},{2,3},{3,2},{4,5},{5,4},{6,7},{7,6},{8,9},{9,8},{10,11... | collective-permute-start | bytes 884744 | tf_op jit(solution)/shard_map/ppermute | solution.py:494
  80.1 1.6 %collective-permute-start.8 = (bf16[8,144,128]{2,1,0:T(8,128)(2,1)S(1)}, bf16[8,144,128]{2,1,0:T(8,128)(2,1)S(1)}, u32[]{:S(2)}, u32[]{:S(2)}) collective-permute-start(bf16[8,144,128]{2,1,0:T(8,128)(2,1)S(1)} %collective-permute-done.6.refs_1_), channel_id=1, source_target_pairs={{0,1},{1,0},{2,3},{3,2},{4,5},{5,4},{6,7},{7,6},{8,9},{9,8},{10,11... | collective-permute-start | bytes 884744 | tf_op jit(solution)/shard_map/ppermute | solution.py:494

commit v4 on v3

--- a/solution.py
+++ b/solution.py
@@ -7,24 +7,21 @@
 from jax.experimental.pallas import tpu as pltpu
 from jax.sharding import PartitionSpec as P
 
+
 SLOT_CAP = 64
 LANES = 128
 TAPS = 27
 GROUP = 8
 
 
-def rims(cells, dim, width):
-    head = lax.slice_in_dim(cells, 0, width, axis=dim)
-    tail = lax.slice_in_dim(cells, cells.shape[dim] - width, cells.shape[dim], axis=dim)
-    return head, tail
-
-
-def neighbours(head, tail, axis):
-    ends = lax.axis_size(axis) - 1
-    return (
-        lax.ppermute(tail, axis, [(i, i + 1) for i in range(ends)]),
-        lax.ppermute(head, axis, [(i + 1, i) for i in range(ends)]),
-    )
+def pair_swap(both, axis):
+    return lax.ppermute(both, axis, [(i, i ^ 1) for i in range(lax.axis_size(axis))])
+
+
+def pass_on(piece, axis):
+    count = lax.axis_size(axis)
+    pairs = [(i, i - 2 if i & 1 else i + 2) for i in range(count)]
+    return lax.ppermute(piece, axis, [pair for pair in pairs if 0 <= pair[1] < count])
 
 
 def slab_steps():
@@ -193,9 +190,9 @@
 
 def forward_kernel(
     blocks, slabs, edge, width,
-    got_ref, og_ref, below_ref, above_ref, left_ref, right_ref, w1_ref, w2_ref, weight_ref, bias_ref,
-    kept_ref, moving_ref, hidden_ref, ga_ref, occupied_ref, inverse_ref,
-    pool_ref, occ_ref, pc_ref, gc_ref, grads_ref,
+    got_ref, og_ref, w1_ref, weight_ref, bias_ref,
+    kept_ref, moving_ref, rest_ref, hidden_ref, pc_ref, occ_ref, slope_ref, occupied_ref, inverse_ref,
+    pool_ref, grads_ref,
 ):
     here = lax.axis_index("rep")
     weight_t = turned_layer(weight_ref, bias_ref)
@@ -248,26 +245,45 @@
     occ_one = occ_ref[1 : one + 1, edge : edge + one * edge, :].reshape(-1, LANES)
     sigmoid_v = jax.nn.sigmoid(act)
     hidden = occ_one * (act * sigmoid_v)
-    slope = occ_one * (sigmoid_v * (1.0 + act * (1.0 - sigmoid_v)))
+    slope_ref[...] = occ_one * (sigmoid_v * (1.0 + act * (1.0 - sigmoid_v)))
     fill_copies(hidden_ref, hidden.reshape(one, one * edge, LANES))
     lay_out(pool_ref, og_ref[...], 2, 2, edge)
-    lay_out(pool_ref, below_ref[...], 0, 2, edge)
-    lay_out(pool_ref, above_ref[...], edge + 2, 2, edge)
-    lay_out(pool_ref, left_ref[...], 0, 0, edge)
-    lay_out(pool_ref, right_ref[...], 0, edge + 2, edge)
-    grad_two = jnp.where(occ_ref[...] > 0, pool_ref[...], 0.0)
-    fill_copies(gc_ref, grad_two)
+    at = (slice(2, edge + 2), slice(2 * edge, (edge + 2) * edge))
+    occupied = occ_ref[at].reshape(-1, LANES)
+    occupied_ref[...] = occupied
+    own = jnp.where(occupied > 0, pool_ref[at].reshape(-1, LANES), 0.0)
+    turned_grad(hidden_ref, 0, own, width, edge, grads_ref)
+    first = 2 * kept_ref.shape[0]
+    divide(grads_ref, 0, kept_ref, moving_ref)
+    rest_ref[...] = grads_ref[first:, :]
+
+
+def middle_kernel(
+    edge, width,
+    og_ref, rep_both, rep_passed, blk_both, blk_passed, rest_ref, pc_ref, occ_ref, slope_ref, w2_ref,
+    kept_ref, moving_ref, ga_ref,
+    pool_ref, gc_ref, grads_ref,
+):
+    one = edge + 2
+    lay_out(pool_ref, og_ref[...], 2, 2, edge)
+    below, above = sides("rep", rep_both, rep_passed)
+    lay_out(pool_ref, below, 0, 2, edge)
+    lay_out(pool_ref, above, edge + 2, 2, edge)
+    left, right = sides("blk", blk_both, blk_passed)
+    lay_out(pool_ref, left, 0, 0, edge)
+    lay_out(pool_ref, right, 0, edge + 2, edge)
+    fill_copies(gc_ref, jnp.where(occ_ref[...] > 0, pool_ref[...], 0.0))
     grad_hidden = conv_back(gc_ref, w2_ref, width, one, one * edge)
-    fill_copies(ga_ref, (grad_hidden * slope).reshape(one, one * edge, LANES))
-    own = gc_ref[1, 0, 2 : edge + 2, 2 * edge : (edge + 2) * edge, :].reshape(-1, LANES)
-    turned_grad(hidden_ref, 0, own, width, edge, grads_ref)
+    fill_copies(ga_ref, (grad_hidden * slope_ref[...]).reshape(one, one * edge, LANES))
     own = ga_ref[1, 1, 1 : edge + 1, : edge * edge, :].reshape(-1, LANES)
-    packed_grad(pc_ref, 1, own, width, edge, grads_ref, TAPS * width)
-    used = TAPS * width - (-TAPS * width // LANES) * width
-    if used < grads_ref.shape[0]:
-        grads_ref[used:, :] = jnp.zeros((grads_ref.shape[0] - used, LANES), jnp.float32)
+    packed_grad(pc_ref, 1, own, width, edge, grads_ref, 0)
+    used = -(-TAPS * width // LANES) * width
+    rest = rest_ref.shape[0]
+    grads_ref[used : used + rest, :] = rest_ref[...]
+    if used + rest < grads_ref.shape[0]:
+        blank = grads_ref.shape[0] - used - rest
+        grads_ref[used + rest :, :] = jnp.zeros((blank, LANES), jnp.float32)
     divide(grads_ref, 0, kept_ref, moving_ref)
-    occupied_ref[...] = occ_ref[2 : edge + 2, 2 * edge : (edge + 2) * edge, :].reshape(-1, LANES)
 
 
 def divide(total_ref, step, kept_ref, moving_ref):
@@ -283,13 +299,38 @@
     divide(total_ref, step, kept_ref, moving_ref)
 
 
-def message_kernel(blocks, own_ref, received_ref, back_ref, sent_ref):
-    rows = own_ref.shape[0] // blocks
+def is_odd(axis):
+    return (lax.axis_index(axis) & 1) == 1
+
+
+def choose_kernel(axis, both_ref, sent_ref):
+    sent_ref[...] = jnp.where(is_odd(axis), both_ref[0], both_ref[1])
+
+
+def sides(axis, both_ref, passed_ref):
+    odd = is_odd(axis)
+    before = jnp.where(odd, both_ref[1], passed_ref[...])
+    after = jnp.where(odd, passed_ref[...], both_ref[0])
+    return before, after
+
+
+def tall_kernel(edge, og_ref, both_ref, passed_ref, rims_ref):
+    below, above = sides("rep", both_ref, passed_ref)
+    for k, at in enumerate((slice(0, 2), slice(edge - 2, edge))):
+        rims_ref[k, 2 : edge + 2] = og_ref[:, at, :]
+        rims_ref[k, :2] = below[:, at, :]
+        rims_ref[k, edge + 2 :] = above[:, at, :]
+
+
+def message_kernel(blocks, own_one, received_one, own_two, received_two, back_ref, sent_ref):
     for block in range(blocks):
-        at = slice(block * rows, (block + 1) * rows)
-        total = own_ref[at, :] + received_ref[at, :].astype(jnp.float32)
-        back = back_ref[block].astype(jnp.float32)
-        sent_ref[block] = jnp.concatenate([total, back], axis=0).astype(jnp.bfloat16)
+        parts = []
+        for own_ref, received_ref in ((own_one, received_one), (own_two, received_two)):
+            rows = own_ref.shape[0] // blocks
+            at = slice(block * rows, (block + 1) * rows)
+            parts.append(own_ref[at, :] + received_ref[at, :].astype(jnp.float32))
+        parts.append(back_ref[block].astype(jnp.float32))
+        sent_ref[block] = jnp.concatenate(parts, axis=0).astype(jnp.bfloat16)
 
 
 def split_bits(value):
@@ -342,23 +383,30 @@
     jitter_ref[...] = jnp.sum(jnp.where(row == lane, sums, 0.0), axis=0, keepdims=True)[:, :3]
 
 
-def finish_kernel(blocks, rows, width, *refs):
-    pieces = refs[:-3]
-    one_ref, two_ref, flat_ref = refs[-3:]
+def finish_kernel(blocks, rows_one, rows_two, width, *refs):
+    pieces = refs[:-4]
+    one_ref, two_ref, flat_one, flat_two = refs[-4:]
     here, turned = lax.axis_index("rep"), 0
     count = len(pieces).bit_length() - 1
     for k in range(count):
         turned = turned + (((here >> k) & 1) << (count - 1 - k))
     for k, got_ref in enumerate(pieces):
         for block in range(blocks):
-            at = pl.multiple_of(((turned ^ k) * blocks + block) * rows, 8)
-            flat_ref[pl.ds(at, rows), :] = got_ref[block].astype(jnp.float32)
-    first, lanes = two_ref.shape[0], one_ref.shape[1]
-    two_ref[...] = flat_ref[:first, :]
-    for tile in range(-(-lanes // LANES)):
+            piece = got_ref[block].astype(jnp.float32)
+            place = (turned ^ k) * blocks + block
+            at = pl.multiple_of(place * rows_one, 8)
+            flat_one[pl.ds(at, rows_one), :] = piece[:rows_one]
+            at = pl.multiple_of(place * rows_two, 8)
+            flat_two[pl.ds(at, rows_two), :] = piece[rows_one:]
+    lanes = one_ref.shape[1]
+    tiles = -(-lanes // LANES)
+    first = flat_two.shape[0]
+    two_ref[:first, :] = flat_two[...]
+    two_ref[first:, :] = flat_one[tiles * width : tiles * width + two_ref.shape[0] - first, :]
+    for tile in range(tiles):
         upto = min(LANES, lanes - tile * LANES)
-        one_ref[:, tile * LANES : tile * LANES + upto] = flat_ref[
-            first + tile * width : first + (tile + 1) * width, :upto
+        one_ref[:, tile * LANES : tile * LANES + upto] = flat_one[
+            tile * width : (tile + 1) * width, :upto
         ]
 
 
@@ -404,9 +452,11 @@
     bias = point_bias.reshape(1, -1)
     taps_rows = conv_one.shape[0]
     unit = 8 * blocks * slabs
-    used = taps_rows - (-taps_rows // LANES) * width
-    rows = used + -used % unit
-    copies = jax.ShapeDtypeStruct((3, 2, one, one * edge, LANES), bf16)
+    rows_two = max(taps_rows // unit * unit, 0)
+    rest = taps_rows - rows_two
+    used = -(-taps_rows // LANES) * width + rest
+    rows_one = used + -used % unit
+    copies = lambda size: jax.ShapeDtypeStruct((3, 2, size, size * edge, LANES), bf16)
     shaped = lambda *shape: jax.ShapeDtypeStruct(shape, f32)
     tie = lax.optimization_barrier
 
@@ -419,46 +469,77 @@
         grant=60,
     )
     sent, out_late = tie((sent, out_grad))
-    with jax.named_scope("points_out"):
-        got = lax.all_to_all(sent, ("blk", "rep"), split_axis=0, concat_axis=0, tiled=True)
+    got = lax.all_to_all(sent, ("blk", "rep"), split_axis=0, concat_axis=0, tiled=True)
     got = got.reshape(blocks, slabs, 8, 4 * SLOT_CAP)
-    with jax.named_scope("rim_rep"):
-        below, above = neighbours(*rims(out_late, 0, 2), "rep")
-    tall = jnp.concatenate([below, out_late, above], axis=0)
-    with jax.named_scope("rim_blk"):
-        left, right = neighbours(*rims(tall, 1, 2), "blk")
-
-    halves = lambda step: (
+    ends = jnp.concatenate([out_late[:2], out_late[edge - 2 :]], axis=0).reshape(2, 2, edge, -1)
+    rim = jax.ShapeDtypeStruct((2, edge, edge * LANES), bf16)
+    side = jax.ShapeDtypeStruct((near, 2, edge * LANES), bf16)
+    rep_both = pair_swap(ends, "rep")
+    passing = call(functools.partial(choose_kernel, "rep"), (rep_both,), rim, micros=0.2)
+    rep_passed = pass_on(passing, "rep")
+    blk_ends = call(
+        functools.partial(tall_kernel, edge),
+        (out_late, rep_both, rep_passed),
+        jax.ShapeDtypeStruct((2, near, 2, edge * LANES), bf16),
+        micros=0.2,
+    )
+    got, blk_ends = tie((got, blk_ends))
+    blk_both = pair_swap(blk_ends, "blk")
+
+    halves = lambda rows, step: (
         shaped(rows >> (step + 1), LANES),
         jax.ShapeDtypeStruct((rows >> (step + 1), LANES), bf16),
     )
-    kept, moving, hidden, grad_act, occupied, inverse = call(
+    steps = slab_steps()
+    wide = pltpu.VMEM((near, near * edge, LANES), f32)
+    kept_two, moving_two, rest_two, hidden, pooled, occ, slope, occupied, inverse = call(
         functools.partial(forward_kernel, blocks, slabs, edge, width),
-        (got, out_grad, below, above, left, right, conv_one, conv_two, point_weight, bias),
-        (*halves(0), copies, copies, shaped(cells, LANES), shaped(cells, LANES)),
+        (got, out_grad, conv_one, point_weight, bias),
+        (
+            *halves(rows_two, 0),
+            shaped(rest, LANES),
+            copies(one),
+            copies(near),
+            shaped(near, near * edge, LANES),
+            shaped(one * one * edge, LANES),
+            shaped(cells, LANES),
+            shaped(cells, LANES),
+        ),
+        scratch=[wide, pltpu.VMEM((taps_rows, LANES), f32)],
+        micros=5,
+    )
+
+    def spread_halves(kept, moving, rows, after):
+        for step, pairs in enumerate(steps):
+            if step:
+                kept, moving = call(
+                    functools.partial(fold_kernel, step),
+                    (kept, received),
+                    halves(rows, step),
+                    scratch=[pltpu.VMEM((rows >> step, LANES), f32)],
+                    micros=0.5,
+                )
+            moving, after = tie((moving, after))
+            received = lax.ppermute(moving, "rep", pairs)
+        return kept, received, after
+
+    blk_both, slope = tie((blk_both, slope))
+    passing = call(functools.partial(choose_kernel, "blk"), (blk_both,), side, micros=0.2)
+    blk_passed = pass_on(passing, "blk")
+    kept_two, received_two, slope = spread_halves(kept_two, moving_two, rows_two, slope)
+
+    kept_one, moving_one, grad_act = call(
+        functools.partial(middle_kernel, edge, width),
+        (out_grad, rep_both, rep_passed, blk_both, blk_passed, rest_two, pooled, occ, slope, conv_two),
+        (*halves(rows_one, 0), copies(one)),
         scratch=[
-            pltpu.VMEM((near, near * edge, LANES), f32),
-            pltpu.VMEM((near, near * edge, LANES), f32),
+            wide,
             pltpu.VMEM((3, 2, near, near * edge, LANES), bf16),
-            pltpu.VMEM((3, 2, near, near * edge, LANES), bf16),
-            pltpu.VMEM((rows, LANES), f32),
+            pltpu.VMEM((rows_one, LANES), f32),
         ],
-        micros=9,
-    )
-
-    steps = slab_steps()
-    for step, pairs in enumerate(steps):
-        if step:
-            kept, moving = call(
-                functools.partial(fold_kernel, step),
-                (kept, received),
-                halves(step),
-                scratch=[pltpu.VMEM((rows >> step, LANES), f32)],
-                micros=0.5,
-            )
-        moving, inverse = tie((moving, inverse))
-        with jax.named_scope("halve"):
-            received = lax.ppermute(moving, "rep", pairs)
+        micros=4,
+    )
+    kept_one, received_one, inverse = spread_halves(kept_one, moving_one, rows_one, inverse)
 
     back, block_out = call(
         functools.partial(backward_kernel, blocks, edge, width),
@@ -472,8 +553,8 @@
     )
     message = call(
         functools.partial(message_kernel, blocks),
-        (kept, received, back),
-        jax.ShapeDtypeStruct((blocks, rows // (blocks * slabs) + 8, LANES), bf16),
+        (kept_one, received_one, kept_two, received_two, back),
+        jax.ShapeDtypeStruct((blocks, (rows_one + rows_two) // (blocks * slabs) + 8, LANES), bf16),
         micros=0.5,
     )
     arrived = lax.all_to_all(message, "blk", split_axis=0, concat_axis=0, tiled=True)
@@ -494,10 +575,12 @@
         pieces = pieces + [lax.ppermute(piece, "rep", pairs) for piece in pieces]
 
     one_total, two_total = call(
-        functools.partial(finish_kernel, blocks, shared, width),
+        functools.partial(
+            finish_kernel, blocks, rows_one // (blocks * slabs), rows_two // (blocks * slabs), width
+        ),
         tuple(pieces),
         (shaped(width, taps_rows), shaped(taps_rows, LANES)),
-        scratch=[pltpu.VMEM((rows, LANES), f32)],
+        scratch=[pltpu.VMEM((rows_one, LANES), f32), pltpu.VMEM((rows_two, LANES), f32)],
         micros=1,
     )
     return (block_out.reshape(edge, edge, -1), attr_grad, jitter_grad, one_total.T, two_total)

time: 83.7 us -> 82.2 us (0.982)
  starting transfers between devices: 20.2 us -> 17.1 us
  blocking collectives: 30.1 us -> 27.4 us
  waiting for transfers between devices: 17.1 us -> 19.3 us
  Pallas kernels: 14 us -> 16.1 us
    all_to_all x1, waiting for transfers between devices: 0.01 us -> 3.9 us  [shards(): lax.all_to_all(sent, ('blk', 'rep'), split_axis=0, concat_axis=0, tiled=T...]
    ppermute x6 -> x8, starting transfers between devices: 12.4 us -> 8.86 us  [the longest x2 6.23 us: pass_on(): lax.ppermute(piece, axis, [pair for pair in pairs if 0 <= pair[1] < count])]
    all_to_all x1, blocking collectives: 17.4 us -> 14.7 us  [shards(): lax.all_to_all(message, 'blk', split_axis=0, concat_axis=0, tiled=True)]
    pallas_call x7 -> x12, Pallas kernels: 14 us -> 16.1 us  [call(): pl.pallas_call(kernel, out_shape=out_shape, in_specs=[smem] * scalars + [...]
    ppermute x6 -> x8, waiting for transfers between devices: 10.1 us -> 8.78 us  [the longest x4 4.96 us: spread_halves(): received = lax.ppermute(moving, 'rep', pairs)]
  transfers between devices with their start and end apart: 10 -> 12, of which waited for: 6 -> 9; matrix products, arithmetic and copies ran while one was open for 0% -> 0% of each run, Pallas kernels for 5% -> 11%
where the time goes in v4:
time: 82.2 us; the launch traced here: 81.9 us
  blocking collectives  27.4 us (33%)
  waiting for transfers between devices  19.3 us (23%)
  starting transfers between devices  17.1 us (21%)
  Pallas kernels  16.1 us (20%)
  between operations  1.51 us (2%)
    pallas_call x12, Pallas kernels, call(): pl.pallas_call(kernel, out_shape=out_shape, in_specs=[smem] * scalars + [...  16.1 us
    all_to_all x1, blocking collectives, shards(): lax.all_to_all(message, 'blk', split_axis=0, concat_axis=0, tiled=True)  14.7 us
    all_to_all x1, blocking collectives, shards(): lax.all_to_all(spread, 'blk', split_axis=0, concat_axis=0, tiled=True)  12.7 us
    all_to_all x1, starting transfers between devices, shards(): lax.all_to_all(sent, ('blk', 'rep'), split_axis=0, concat_axis=0, tiled=T...  7.33 us
    ppermute x3, waiting for transfers between devices, shards(): pieces = pieces + [lax.ppermute(piece, 'rep', pairs) for piece in pieces]  6.6 us
    ppermute x2, starting transfers between devices, pass_on(): lax.ppermute(piece, axis, [pair for pair in pairs if 0 <= pair[1] < count])  6.23 us
    ppermute x4, waiting for transfers between devices, spread_halves(): received = lax.ppermute(moving, 'rep', pairs)  4.96 us
    all_to_all x1, waiting for transfers between devices, shards(): lax.all_to_all(sent, ('blk', 'rep'), split_axis=0, concat_axis=0, tiled=T...  3.9 us
  transfers between devices with their start and end apart: 12, of which 9 were waited for; matrix products, arithmetic and copies ran while one was open for 0% of the time, Pallas kernels for 11%

profile of v4, /device:TPU:0, one launch (start us, length us, event | category | flops | bytes accessed | tf_op | source)
XLA Modules:
  0.0 81.9 jit_solution(9405169833649223589)
XLA Ops:
  0.6 0.0 copy-start
  0.6 0.0 copy-start.4
  1.4 1.8 %shard_map.146 = f32[32,8,256]{2,1,0:T(8,128)} custom-call(s32[1,8]{1,0:T(1,128)} %counts_ref.1, f32[1,1]{1,0:T(1,128)} %bitcast.7.yaw_ref, f32[1,3]{1,0:T(1,128)} %jitter_ref.1, f32[3,512]{1,0:T(4,128)} %xyz_ref.1, f32[5,512]{1,0:T(8,128)} %attr_ref.1, s32[1,512]{1,0:T(1,128)} %bitcast.13), custom_call_target="tpu_custom_call" | custom-call | flops 400000000 | tf_op jit(solution)/shard_map/pallas_call | solution.py:421
  3.1 0.0 copy-start.2
  3.1 0.0 copy-start.3
  3.1 7.3 %all-to-all-start = ((f32[32,8,256]{2,1,0:T(8,128)}), f32[32,8,256]{2,1,0:T(8,128)S(1)}, u32[]{:S(2)}, u32[]{:S(2)}) async-start(f32[32,8,256]{2,1,0:T(8,128)} %shard_map.146), calls=%async_computation | async-start | bytes 524288 | tf_op jit(solution)/shard_map/all_to_all | solution.py:472
  10.5 0.0 copy-done
  10.5 0.3 collective-permute-start
  10.8 1.0 %collective-permute-done.both_ref.rep_both = bf16[2,2,8,1024]{3,2,1,0:T(8,128)(2,1)S(1)} collective-permute-done((bf16[2,2,8,1024]{3,2,1,0:T(8,128)(2,1)S(1)}, bf16[2,2,8,1024]{3,2,1,0:T(8,128)(2,1)S(1)}, u32[]{:S(2)}, u32[]{:S(2)}) %collective-permute-start) | collective-permute-done | bytes 65568 | tf_op jit(solution)/shard_map/ppermute | solution.py:18
  11.8 3.7 %collective-permute-start.1 = (bf16[2,8,1024]{2,1,0:T(8,128)(2,1)S(1)}, bf16[2,8,1024]{2,1,0:T(8,128)(2,1)S(1)}, u32[]{:S(2)}, u32[]{:S(2)}) collective-permute-start(bf16[2,8,1024]{2,1,0:T(8,128)(2,1)S(1)} %shard_map.147), channel_id=1, source_target_pairs={{0,2},{3,1},{4,6},{7,5},{8,10},{11,9},{12,14},{15,13},{16,18},{19,... | collective-permute-start | bytes 98312 | tf_op jit(solution)/shard_map/ppermute | solution.py:24
  15.5 0.0 copy-done.4
  15.5 0.3 copy.16.w1_ref
  15.9 1.2 %collective-permute-done.1.passed_ref.rep_passed = bf16[2,8,1024]{2,1,0:T(8,128)(2,1)S(1)} collective-permute-done((bf16[2,8,1024]{2,1,0:T(8,128)(2,1)S(1)}, bf16[2,8,1024]{2,1,0:T(8,128)(2,1)S(1)}, u32[]{:S(2)}, u32[]{:S(2)}) %collective-permute-start.1) | collective-permute-done | bytes 32800 | tf_op jit(solution)/shard_map/ppermute | solution.py:24
  17.1 3.9 %all-to-all-done = f32[32,8,256]{2,1,0:T(8,128)S(1)} async-done(((f32[32,8,256]{2,1,0:T(8,128)}), f32[32,8,256]{2,1,0:T(8,128)S(1)}, u32[]{:S(2)}, u32[]{:S(2)}) %all-to-all-start) | async-done | bytes 262176 | tf_op jit(solution)/shard_map/all_to_all | solution.py:472
  21.0 0.9 %collective-permute-start.2 = (bf16[2,12,2,1024]{3,2,1,0:T(2,128)(2,1)S(1)}, bf16[2,12,2,1024]{3,2,1,0:T(2,128)(2,1)S(1)}, u32[]{:S(2)}, u32[]{:S(2)}) collective-permute-start(bf16[2,12,2,1024]{3,2,1,0:T(2,128)(2,1)S(1)} %shard_map.148), channel_id=1, source_target_pairs={{0,4},{4,0},{8,12},{12,8},{16,20},{20,16},{24,28},{28,24},{1,5},{5... | collective-permute-start | bytes 294920 | tf_op jit(solution)/shard_map/ppermute | solution.py:18
  21.9 0.0 copy-done.2
  21.9 0.0 copy-done.3
  21.9 0.0 copy-start.1
  21.9 5.0 %shard_map.149 = (f32[1280,128]{1,0:T(8,128)S(1)}, bf16[1280,128]{1,0:T(8,128)(2,1)S(1)}, f32[32,128]{1,0:T(8,128)S(1)}, bf16[3,2,10,80,128]{4,3,2,1,0:T(8,128)(...) custom-call(f32[8,4,8,256]{3,2,1,0:T(8,128)S(1)} %bitcast.8, ...), custom_call_target="tpu_custom_call" | custom-call | flops 2000000000 | tf_op jit(solution)/shard_map/pallas_call | solution.py:421
  27.0 0.0 collective-permute-done.2.both_ref.blk_both
  27.0 0.1 collective-permute-start.4
  27.1 2.6 %collective-permute-start.3 = (bf16[12,2,1024]{2,1,0:T(2,128)(2,1)S(1)}, bf16[12,2,1024]{2,1,0:T(2,128)(2,1)S(1)}, u32[]{:S(2)}, u32[]{:S(2)}) collective-permute-start(bf16[12,2,1024]{2,1,0:T(2,128)(2,1)S(1)} %shard_map.150), channel_id=1, source_target_pairs={{0,8},{8,16},{12,4},{16,24},{20,12},{28,20},{1,9},{9,17},{13,5},{1... | collective-permute-start | bytes 147464 | tf_op jit(solution)/shard_map/ppermute | solution.py:24
  29.7 0.0 collective-permute-done.4.received_ref
  29.7 0.1 shard_map.151
  29.8 1.6 %collective-permute-done.3.blk_passed = bf16[12,2,1024]{2,1,0:T(2,128)(2,1)S(1)} collective-permute-done((bf16[12,2,1024]{2,1,0:T(2,128)(2,1)S(1)}, bf16[12,2,1024]{2,1,0:T(2,128)(2,1)S(1)}, u32[]{:S(2)}, u32[]{:S(2)}) %collective-permute-start.3) | collective-permute-done | bytes 49184 | tf_op jit(solution)/shard_map/ppermute | solution.py:24
  31.4 0.0 copy-done.1
  31.4 3.5 %shard_map.152 = (f32[1024,128]{1,0:T(8,128)S(1)}, bf16[1024,128]{1,0:T(8,128)(2,1)S(1)}, bf16[3,2,10,80,128]{4,3,2,1,0:T(8,128)(2,1)S(1)}) custom-call(bf16[8,8,1024]{2,1,0:T(8,128)(2,1)S(1)} %copy-done, bf16[2,2,8,1024]{3,2,1,0:T(8,128)(2,1)S(1)} %collective-permute-done.both_ref.rep_both, ...), custom_call_target="tpu_custom_call" | custom-call | flops 1600000000 | tf_op jit(solution)/shard_map/pallas_call | solution.py:421
  34.8 0.1 collective-permute-start.5
  34.9 0.6 collective-permute-start.7
  35.6 0.9 %collective-permute-done.5.received_ref = bf16[1024,128]{1,0:T(8,128)(2,1)S(1)} collective-permute-done((bf16[1024,128]{1,0:T(8,128)(2,1)S(1)}, bf16[1024,128]{1,0:T(8,128)(2,1)S(1)}, u32[]{:S(2)}, u32[]{:S(2)}) %collective-permute-start.5) | collective-permute-done | bytes 262176 | tf_op jit(solution)/shard_map/ppermute | solution.py:523
  36.4 0.1 shard_map.153
  36.6 0.6 collective-permute-start.6
  37.2 3.0 %shard_map.154 = (bf16[8,8,128]{2,1,0:T(8,128)(2,1)S(1)}, bf16[64,1024]{1,0:T(8,128)(2,1)}) custom-call(f32[8,4,8,256]{3,2,1,0:T(8,128)S(1)} %bitcast.9, bf16[3,2,10,80,128]{4,3,2,1,0:T(8,128)(2,1)S(1)} %get-tuple-element.44.hidden_ref, bf16[3,2,10,80,128]{4,3,2,1,0:T(8,128)(2,1)S(1)} %get-tuple-element.58.ga_ref, ...), custom_call_target="tpu_custom_call" | custom-call | flops 1600000000 | tf_op jit(solution)/shard_map/pallas_call | solution.py:421
  40.3 1.8 %collective-permute-done.7.received_two = bf16[640,128]{1,0:T(8,128)(2,1)S(1)} collective-permute-done((bf16[640,128]{1,0:T(8,128)(2,1)S(1)}, bf16[640,128]{1,0:T(8,128)(2,1)S(1)}, u32[]{:S(2)}, u32[]{:S(2)}) %collective-permute-start.7) | collective-permute-done | bytes 163872 | tf_op jit(solution)/shard_map/ppermute | solution.py:523
  42.1 2.3 %collective-permute-done.6.received_one = bf16[512,128]{1,0:T(8,128)(2,1)S(1)} collective-permute-done((bf16[512,128]{1,0:T(8,128)(2,1)S(1)}, bf16[512,128]{1,0:T(8,128)(2,1)S(1)}, u32[]{:S(2)}, u32[]{:S(2)}) %collective-permute-start.6) | collective-permute-done | bytes 131104 | tf_op jit(solution)/shard_map/ppermute | solution.py:523
  44.3 0.1 shard_map.155
  44.4 14.7 %all_to_all.15 = bf16[8,152,128]{2,1,0:T(8,128)(2,1)S(1)} all-to-all(bf16[8,152,128]{2,1,0:T(8,128)(2,1)S(1)} %shard_map.155), channel_id=1, replica_groups=mesh['blk'=8,'rep'=4] {'blk'}, dimensions={0} | all-to-all | bytes 622592 | tf_op jit(solution)/shard_map/all_to_all | solution.py:560
  59.2 12.7 %all_to_all.16.refs_0_ = bf16[8,144,128]{2,1,0:T(8,128)(2,1)S(1)} all-to-all(bf16[8,144,128]{2,1,0:T(8,128)(2,1)S(1)} %broadcast_in_dim.2), channel_id=1, replica_groups=mesh['blk'=8,'rep'=4] {'blk'}, dimensions={0} | all-to-all | bytes 589824 | tf_op jit(solution)/shard_map/all_to_all | solution.py:564
  71.9 0.9 %collective-permute-start.8 = (bf16[8,144,128]{2,1,0:T(8,128)(2,1)S(1)}, bf16[8,144,128]{2,1,0:T(8,128)(2,1)S(1)}, u32[]{:S(2)}, u32[]{:S(2)}) collective-permute-start(bf16[8,144,128]{2,1,0:T(8,128)(2,1)S(1)} %all_to_all.16.refs_0_), channel_id=1, source_target_pairs={{0,2},{1,3},{2,0},{3,1},{4,6},{5,7},{6,4},{7,5},{8,10},{9,11},{10,... | collective-permute-start | bytes 884744 | tf_op jit(solution)/shard_map/ppermute | solution.py:575
  72.9 0.0 collective-permute-start.9
  72.9 5.8 %collective-permute-done.8.refs_1_ = bf16[8,144,128]{2,1,0:T(8,128)(2,1)S(1)} collective-permute-done((bf16[8,144,128]{2,1,0:T(8,128)(2,1)S(1)}, bf16[8,144,128]{2,1,0:T(8,128)(2,1)S(1)}, u32[]{:S(2)}, u32[]{:S(2)}) %collective-permute-start.8) | collective-permute-done | bytes 294944 | tf_op jit(solution)/shard_map/ppermute | solution.py:575
  78.7 0.0 collective-permute-start.10
  78.7 0.8 shard_map.156
  79.4 0.0 collective-permute-done.9.refs_2_
  79.4 0.8 %collective-permute-done.10.refs_3_ = bf16[8,144,128]{2,1,0:T(8,128)(2,1)S(1)} collective-permute-done((bf16[8,144,128]{2,1,0:T(8,128)(2,1)S(1)}, bf16[8,144,128]{2,1,0:T(8,128)(2,1)S(1)}, u32[]{:S(2)}, u32[]{:S(2)}) %collective-permute-start.10) | collective-permute-done | bytes 294944 | tf_op jit(solution)/shard_map/ppermute | solution.py:575
  80.2 1.6 %shard_map.157 = (f32[96,2592]{1,0:T(8,128)}, f32[2592,128]{1,0:T(8,128)}) custom-call(bf16[8,144,128]{2,1,0:T(8,128)(2,1)S(1)} %all_to_all.16.refs_0_, bf16[8,144,128]{2,1,0:T(8,128)(2,1)S(1)} %collective-permute-done.8.refs_1_, bf16[8,144,128]{2,1,0:T(8,128)(2,1)S(1)} %collective-permute-done.9.refs_2_, ...), custom_call_target="tpu_custom_call" | custom-call | flops 400000000 | tf_op jit(solution)/shard_map/pallas_call | solution.py:421
  (8 shorter events, 0.2 us)
Async XLA Ops:
  0.6 9.8 %copy-start = (bf16[8,8,1024]{2,1,0:T(8,128)(2,1)S(1)}, bf16[8,8,1024]{2,1,0:T(8,128)(2,1)}, u32[]{:S(2)}) copy-start(bf16[8,8,1024]{2,1,0:T(8,128)(2,1)} %og_ref.4) | copy-start | bytes 393220
  0.6 14.9 %copy-start.4 = (bf16[2592,96]{0,1:T(8,128)(2,1)S(1)}, bf16[2592,96]{0,1:T(8,128)(2,1)}, u32[]{:S(2)}) copy-start(bf16[2592,96]{0,1:T(8,128)(2,1)} %param.19) | copy-start | bytes 1492996
  3.1 18.8 %copy-start.2 = (f32[8,96]{1,0:T(8,128)S(1)}, f32[8,96]{1,0:T(8,128)}, u32[]{:S(2)}) copy-start(f32[8,96]{1,0:T(8,128)} %weight_ref.3) | copy-start | bytes 9220
  3.1 18.8 %copy-start.3 = (f32[96]{0:T(128)S(1)}, f32[96]{0:T(128)}, u32[]{:S(2)}) copy-start(f32[96]{0:T(128)} %param.18) | copy-start | bytes 1156
  3.1 17.9 %all-to-all-start = ((f32[32,8,256]{2,1,0:T(8,128)}), f32[32,8,256]{2,1,0:T(8,128)S(1)}, u32[]{:S(2)}, u32[]{:S(2)}) async-start(f32[32,8,256]{2,1,0:T(8,128)} %shard_map.146), calls=%async_computation | async-start | bytes 524288 | tf_op jit(solution)/shard_map/all_to_all | solution.py:472
  10.5 1.3 %collective-permute-start = (bf16[2,2,8,1024]{3,2,1,0:T(8,128)(2,1)S(1)}, bf16[2,2,8,1024]{3,2,1,0:T(8,128)(2,1)S(1)}, u32[]{:S(2)}, u32[]{:S(2)}) collective-permute-start(bf16[2,2,8,1024]{3,2,1,0:T(8,128)(2,1)S(1)} %bitcast.12), channel_id=1, source_target_pairs={{0,1},{1,0},{2,3},{3,2},{4,5},{5,4},{6,7},{7,6},{8,9},{9,8},{10,11... | collective-permute-start | bytes 196616 | tf_op jit(solution)/shard_map/ppermute | solution.py:18
  11.8 5.3 %collective-permute-start.1 = (bf16[2,8,1024]{2,1,0:T(8,128)(2,1)S(1)}, bf16[2,8,1024]{2,1,0:T(8,128)(2,1)S(1)}, u32[]{:S(2)}, u32[]{:S(2)}) collective-permute-start(bf16[2,8,1024]{2,1,0:T(8,128)(2,1)S(1)} %shard_map.147), channel_id=1, source_target_pairs={{0,2},{3,1},{4,6},{7,5},{8,10},{11,9},{12,14},{15,13},{16,18},{19,... | collective-permute-start | bytes 98312 | tf_op jit(solution)/shard_map/ppermute | solution.py:24
  21.0 5.9 %collective-permute-start.2 = (bf16[2,12,2,1024]{3,2,1,0:T(2,128)(2,1)S(1)}, bf16[2,12,2,1024]{3,2,1,0:T(2,128)(2,1)S(1)}, u32[]{:S(2)}, u32[]{:S(2)}) collective-permute-start(bf16[2,12,2,1024]{3,2,1,0:T(2,128)(2,1)S(1)} %shard_map.148), channel_id=1, source_target_pairs={{0,4},{4,0},{8,12},{12,8},{16,20},{20,16},{24,28},{28,24},{1,5},{5... | collective-permute-start | bytes 294920 | tf_op jit(solution)/shard_map/ppermute | solution.py:18
  21.9 9.5 %copy-start.1 = (bf16[2592,128]{1,0:T(8,128)(2,1)S(1)}, bf16[2592,128]{1,0:T(8,128)(2,1)}, u32[]{:S(2)}) copy-start(bf16[2592,128]{1,0:T(8,128)(2,1)} %w2_ref.3) | copy-start | bytes 1990660
  27.0 2.7 %collective-permute-start.4 = (bf16[1280,128]{1,0:T(8,128)(2,1)S(1)}, bf16[1280,128]{1,0:T(8,128)(2,1)S(1)}, u32[]{:S(2)}, u32[]{:S(2)}) collective-permute-start(bf16[1280,128]{1,0:T(8,128)(2,1)S(1)} %get-tuple-element.54), channel_id=1, source_target_pairs={{0,1},{1,0},{2,3},{3,2},{4,5},{5,4},{6,7},{7,6},{8,9},{9,8},{10,11... | collective-permute-start | bytes 983048 | tf_op jit(solution)/shard_map/ppermute | solution.py:523
  27.1 4.3 %collective-permute-start.3 = (bf16[12,2,1024]{2,1,0:T(2,128)(2,1)S(1)}, bf16[12,2,1024]{2,1,0:T(2,128)(2,1)S(1)}, u32[]{:S(2)}, u32[]{:S(2)}) collective-permute-start(bf16[12,2,1024]{2,1,0:T(2,128)(2,1)S(1)} %shard_map.150), channel_id=1, source_target_pairs={{0,8},{8,16},{12,4},{16,24},{20,12},{28,20},{1,9},{9,17},{13,5},{1... | collective-permute-start | bytes 147464 | tf_op jit(solution)/shard_map/ppermute | solution.py:24
  34.8 1.6 %collective-permute-start.5 = (bf16[1024,128]{1,0:T(8,128)(2,1)S(1)}, bf16[1024,128]{1,0:T(8,128)(2,1)S(1)}, u32[]{:S(2)}, u32[]{:S(2)}) collective-permute-start(bf16[1024,128]{1,0:T(8,128)(2,1)S(1)} %get-tuple-element.63), channel_id=1, source_target_pairs={{0,1},{1,0},{2,3},{3,2},{4,5},{5,4},{6,7},{7,6},{8,9},{9,8},{10,11... | collective-permute-start | bytes 786440 | tf_op jit(solution)/shard_map/ppermute | solution.py:523
  34.9 7.1 %collective-permute-start.7 = (bf16[640,128]{1,0:T(8,128)(2,1)S(1)}, bf16[640,128]{1,0:T(8,128)(2,1)S(1)}, u32[]{:S(2)}, u32[]{:S(2)}) collective-permute-start(bf16[640,128]{1,0:T(8,128)(2,1)S(1)} %get-tuple-element.71), channel_id=1, source_target_pairs={{0,2},{1,3},{2,0},{3,1},{4,6},{5,7},{6,4},{7,5},{8,10},{9,11},{10,... | collective-permute-start | bytes 491528 | tf_op jit(solution)/shard_map/ppermute | solution.py:523
  36.6 7.8 %collective-permute-start.6 = (bf16[512,128]{1,0:T(8,128)(2,1)S(1)}, bf16[512,128]{1,0:T(8,128)(2,1)S(1)}, u32[]{:S(2)}, u32[]{:S(2)}) collective-permute-start(bf16[512,128]{1,0:T(8,128)(2,1)S(1)} %get-tuple-element.69), channel_id=1, source_target_pairs={{0,2},{1,3},{2,0},{3,1},{4,6},{5,7},{6,4},{7,5},{8,10},{9,11},{10,... | collective-permute-start | bytes 393224 | tf_op jit(solution)/shard_map/ppermute | solution.py:523
  71.9 6.7 %collective-permute-start.8 = (bf16[8,144,128]{2,1,0:T(8,128)(2,1)S(1)}, bf16[8,144,128]{2,1,0:T(8,128)(2,1)S(1)}, u32[]{:S(2)}, u32[]{:S(2)}) collective-permute-start(bf16[8,144,128]{2,1,0:T(8,128)(2,1)S(1)} %all_to_all.16.refs_0_), channel_id=1, source_target_pairs={{0,2},{1,3},{2,0},{3,1},{4,6},{5,7},{6,4},{7,5},{8,10},{9,11},{10,... | collective-permute-start | bytes 884744 | tf_op jit(solution)/shard_map/ppermute | solution.py:575
  72.9 6.5 %collective-permute-start.9 = (bf16[8,144,128]{2,1,0:T(8,128)(2,1)S(1)}, bf16[8,144,128]{2,1,0:T(8,128)(2,1)S(1)}, u32[]{:S(2)}, u32[]{:S(2)}) collective-permute-start(bf16[8,144,128]{2,1,0:T(8,128)(2,1)S(1)} %all_to_all.16.refs_0_), channel_id=1, source_target_pairs={{0,1},{1,0},{2,3},{3,2},{4,5},{5,4},{6,7},{7,6},{8,9},{9,8},{10,11... | collective-permute-start | bytes 884744 | tf_op jit(solution)/shard_map/ppermute | solution.py:575
  78.7 1.6 %collective-permute-start.10 = (bf16[8,144,128]{2,1,0:T(8,128)(2,1)S(1)}, bf16[8,144,128]{2,1,0:T(8,128)(2,1)S(1)}, u32[]{:S(2)}, u32[]{:S(2)}) collective-permute-start(bf16[8,144,128]{2,1,0:T(8,128)(2,1)S(1)} %collective-permute-done.8.refs_1_), channel_id=1, source_target_pairs={{0,1},{1,0},{2,3},{3,2},{4,5},{5,4},{6,7},{7,6},{8,9},{9,8},{10,11... | collective-permute-start | bytes 884744 | tf_op jit(solution)/shard_map/ppermute | solution.py:575

commit v5 on v4

--- a/solution.py
+++ b/solution.py
@@ -39,20 +39,22 @@
     return lax.broadcasted_iota(jnp.int32, shape, axis)
 
 
-def pack_kernel(blocks, slabs, counts_ref, yaw_ref, jitter_ref, xyz_ref, attr_ref, vox_ref, sent_ref):
-    cos_yaw = jnp.cos(yaw_ref[...])
-    sin_yaw = jnp.sin(yaw_ref[...])
+def pack_kernel(blocks, slabs, counts_ref, jitter_ref, yaw_ref, xyz_ref, attr_ref, vox_ref, sent_ref):
+    yaw = yaw_ref[...].reshape(1, 1)
+    jitter = jitter_ref[...]
+    cos_yaw, sin_yaw = jnp.cos(yaw), jnp.sin(yaw)
     x, y, z = (xyz_ref[k : k + 1, :] for k in range(3))
-    jitter = jitter_ref[...]
     rotated_x = cos_yaw * x - sin_yaw * y + jitter[:, 0:1]
     rotated_y = sin_yaw * x + cos_yaw * y + jitter[:, 1:2]
     rotated_z = z + jitter[:, 2:3]
     values = jnp.concatenate([rotated_x, rotated_y, rotated_z, attr_ref[...]], axis=0)
     slot = iota((1, SLOT_CAP), 1)
+    counts = counts_ref[...]
     named = []
     for block in range(blocks):
         piece = vox_ref[:, block * SLOT_CAP : (block + 1) * SLOT_CAP]
-        named.append(jnp.where(slot < counts_ref[0, block], piece + 1, 0).astype(jnp.float32))
+        used = slot < counts[:, block : block + 1]
+        named.append(jnp.where(used, piece + 1, 0).astype(jnp.float32))
     none = jnp.zeros((1, SLOT_CAP), jnp.float32)
     named = [none] + named + [none]
     blank = jnp.zeros((8, SLOT_CAP), jnp.float32)
@@ -127,7 +129,8 @@
 
 def grad_products(copies, base, partner, edge):
     turned = partner.astype(jnp.float32).T.astype(jnp.bfloat16)
-    for taps in pairs_of_taps():
+    for tap in range(0, TAPS, 4):
+        taps = range(tap, min(tap + 4, TAPS))
         right = jnp.concatenate([window(copies, t, edge, edge * 8, base) for t in taps], axis=1)
         part = jnp.dot(turned, right, preferred_element_type=jnp.float32)
         for k, t in enumerate(taps):
@@ -157,12 +160,19 @@
         out_ref[first + tile * width : first + (tile + 1) * width, :] = held
 
 
+def split_three(value):
+    high = value.astype(jnp.bfloat16).astype(jnp.float32)
+    rest = value - high
+    middle = rest.astype(jnp.bfloat16).astype(jnp.float32)
+    return high, middle, rest - middle
+
+
 def layer_t(values, weight_t):
-    depth = values.shape[0]
-    total = weight_t[:, depth : depth + 1]
-    for k in range(depth):
-        total = total + weight_t[:, k : k + 1] * values[k : k + 1, :]
-    return total
+    high, middle, low = split_three(values)
+    unit = (iota(values.shape, 0) < 3).astype(jnp.float32)
+    blocks = [high, middle, high, middle, low, high, unit, jnp.zeros_like(unit)]
+    right = jnp.concatenate(blocks, axis=0).astype(jnp.bfloat16)
+    return jnp.dot(weight_t, right, preferred_element_type=jnp.float32)
 
 
 def widen(value):
@@ -174,10 +184,12 @@
 
 
 def turned_layer(weight_ref, bias_ref):
-    rows = jnp.concatenate([weight_ref[...], bias_ref[...]], axis=0)
-    rows = widen(rows)
-    blank = jnp.zeros((LANES - rows.shape[0], LANES), jnp.float32)
-    return jnp.concatenate([rows, blank], axis=0).T[: weight_ref.shape[1]]
+    high, middle, low = split_three(weight_ref[...])
+    width = high.shape[1]
+    bias = jnp.concatenate(list(split_three(bias_ref[...])) + [jnp.zeros((5, width), jnp.float32)], axis=0)
+    blank = jnp.zeros((LANES - 7 * 8, width), jnp.float32)
+    rows = jnp.concatenate([high, high, middle, middle, high, low, bias, blank], axis=0)
+    return widen(rows).T[:width, :64].astype(jnp.bfloat16)
 
 
 def lay_out(target, piece, x0, y0, edge):
@@ -462,9 +474,8 @@
 
     sent = call(
         functools.partial(pack_kernel, blocks, slabs),
-        (slot_counts, scan_yaw.reshape(1, 1), scan_jitter, point_xyz, point_attrs, voxel_ids.reshape(1, -1)),
+        (slot_counts, scan_jitter, scan_yaw, point_xyz, point_attrs, voxel_ids.reshape(1, -1)),
         shaped(blocks * slabs, 8, 4 * SLOT_CAP),
-        scalars=1,
         micros=1,
         grant=60,
     )

time: 82.2 us -> 82.1 us (level)
  no operation moved by 1% of the time
where the time goes in v5:
time: 82.1 us; the launch traced here: 81.7 us
  blocking collectives  27.4 us (33%)
  waiting for transfers between devices  19.5 us (24%)
  starting transfers between devices  17.1 us (21%)
  Pallas kernels  15.7 us (19%)
  between operations  1.51 us (2%)
    pallas_call x12, Pallas kernels, call(): pl.pallas_call(kernel, out_shape=out_shape, in_specs=[smem] * scalars + [...  15.7 us
    all_to_all x1, blocking collectives, shards(): lax.all_to_all(message, 'blk', split_axis=0, concat_axis=0, tiled=True)  14.7 us
    all_to_all x1, blocking collectives, shards(): lax.all_to_all(spread, 'blk', split_axis=0, concat_axis=0, tiled=True)  12.7 us
    all_to_all x1, starting transfers between devices, shards(): lax.all_to_all(sent, ('blk', 'rep'), split_axis=0, concat_axis=0, tiled=T...  7.33 us
    ppermute x3, waiting for transfers between devices, shards(): pieces = pieces + [lax.ppermute(piece, 'rep', pairs) for piece in pieces]  6.6 us
    ppermute x2, starting transfers between devices, pass_on(): lax.ppermute(piece, axis, [pair for pair in pairs if 0 <= pair[1] < count])  6.23 us
    ppermute x4, waiting for transfers between devices, spread_halves(): received = lax.ppermute(moving, 'rep', pairs)  5.19 us
    all_to_all x1, waiting for transfers between devices, shards(): lax.all_to_all(sent, ('blk', 'rep'), split_axis=0, concat_axis=0, tiled=T...  3.9 us
  transfers between devices with their start and end apart: 12, of which 9 were waited for; matrix products, arithmetic and copies ran while one was open for 0% of the time, Pallas kernels for 11%

profile of v5, /device:TPU:0, one launch (start us, length us, event | category | flops | bytes accessed | tf_op | source)
XLA Modules:
  0.0 81.7 jit_solution(14640999903969702672)
XLA Ops:
  0.6 0.0 copy-start
  0.6 0.0 copy-start.4
  1.4 1.7 %shard_map.146 = f32[32,8,256]{2,1,0:T(8,128)} custom-call(s32[1,8]{1,0:T(1,128)} %counts_ref.1, f32[1,3]{1,0:T(1,128)} %jitter_ref.1, f32[1]{0:T(128)S(6)} %copy.18.yaw_ref, f32[3,512]{1,0:T(4,128)} %xyz_ref.1, f32[5,512]{1,0:T(8,128)} %attr_ref.1, s32[1,512]{1,0:T(1,128)} %bitcast.11), custom_call_target="tpu_custom_call" | custom-call | flops 400000000 | tf_op jit(solution)/shard_map/pallas_call | solution.py:433
  3.1 0.0 copy-start.2
  3.1 0.0 copy-start.3
  3.1 7.3 %all-to-all-start = ((f32[32,8,256]{2,1,0:T(8,128)}), f32[32,8,256]{2,1,0:T(8,128)S(1)}, u32[]{:S(2)}, u32[]{:S(2)}) async-start(f32[32,8,256]{2,1,0:T(8,128)} %shard_map.146), calls=%async_computation | async-start | bytes 524288 | tf_op jit(solution)/shard_map/all_to_all | solution.py:483
  10.4 0.0 copy-done
  10.5 0.3 collective-permute-start
  10.8 1.0 %collective-permute-done.both_ref.rep_both = bf16[2,2,8,1024]{3,2,1,0:T(8,128)(2,1)S(1)} collective-permute-done((bf16[2,2,8,1024]{3,2,1,0:T(8,128)(2,1)S(1)}, bf16[2,2,8,1024]{3,2,1,0:T(8,128)(2,1)S(1)}, u32[]{:S(2)}, u32[]{:S(2)}) %collective-permute-start) | collective-permute-done | bytes 65568 | tf_op jit(solution)/shard_map/ppermute | solution.py:18
  11.8 3.7 %collective-permute-start.1 = (bf16[2,8,1024]{2,1,0:T(8,128)(2,1)S(1)}, bf16[2,8,1024]{2,1,0:T(8,128)(2,1)S(1)}, u32[]{:S(2)}, u32[]{:S(2)}) collective-permute-start(bf16[2,8,1024]{2,1,0:T(8,128)(2,1)S(1)} %shard_map.147), channel_id=1, source_target_pairs={{0,2},{3,1},{4,6},{7,5},{8,10},{11,9},{12,14},{15,13},{16,18},{19,... | collective-permute-start | bytes 98312 | tf_op jit(solution)/shard_map/ppermute | solution.py:24
  15.5 0.0 copy-done.4
  15.5 0.3 copy.16.w1_ref
  15.8 1.2 %collective-permute-done.1.passed_ref.rep_passed = bf16[2,8,1024]{2,1,0:T(8,128)(2,1)S(1)} collective-permute-done((bf16[2,8,1024]{2,1,0:T(8,128)(2,1)S(1)}, bf16[2,8,1024]{2,1,0:T(8,128)(2,1)S(1)}, u32[]{:S(2)}, u32[]{:S(2)}) %collective-permute-start.1) | collective-permute-done | bytes 32800 | tf_op jit(solution)/shard_map/ppermute | solution.py:24
  17.1 3.9 %all-to-all-done = f32[32,8,256]{2,1,0:T(8,128)S(1)} async-done(((f32[32,8,256]{2,1,0:T(8,128)}), f32[32,8,256]{2,1,0:T(8,128)S(1)}, u32[]{:S(2)}, u32[]{:S(2)}) %all-to-all-start) | async-done | bytes 262176 | tf_op jit(solution)/shard_map/all_to_all | solution.py:483
  21.0 0.9 %collective-permute-start.2 = (bf16[2,12,2,1024]{3,2,1,0:T(2,128)(2,1)S(1)}, bf16[2,12,2,1024]{3,2,1,0:T(2,128)(2,1)S(1)}, u32[]{:S(2)}, u32[]{:S(2)}) collective-permute-start(bf16[2,12,2,1024]{3,2,1,0:T(2,128)(2,1)S(1)} %shard_map.148), channel_id=1, source_target_pairs={{0,4},{4,0},{8,12},{12,8},{16,20},{20,16},{24,28},{28,24},{1,5},{5... | collective-permute-start | bytes 294920 | tf_op jit(solution)/shard_map/ppermute | solution.py:18
  21.9 0.0 copy-done.2
  21.9 0.0 copy-done.3
  21.9 0.0 copy-start.1
  21.9 4.9 %shard_map.149 = (f32[1280,128]{1,0:T(8,128)S(1)}, bf16[1280,128]{1,0:T(8,128)(2,1)S(1)}, f32[32,128]{1,0:T(8,128)S(1)}, bf16[3,2,10,80,128]{4,3,2,1,0:T(8,128)(...) custom-call(f32[8,4,8,256]{3,2,1,0:T(8,128)S(1)} %bitcast.6, ...), custom_call_target="tpu_custom_call" | custom-call | flops 2000000000 | tf_op jit(solution)/shard_map/pallas_call | solution.py:433
  26.8 0.0 collective-permute-done.2.both_ref.blk_both
  26.8 0.1 collective-permute-start.4
  26.9 2.6 %collective-permute-start.3 = (bf16[12,2,1024]{2,1,0:T(2,128)(2,1)S(1)}, bf16[12,2,1024]{2,1,0:T(2,128)(2,1)S(1)}, u32[]{:S(2)}, u32[]{:S(2)}) collective-permute-start(bf16[12,2,1024]{2,1,0:T(2,128)(2,1)S(1)} %shard_map.150), channel_id=1, source_target_pairs={{0,8},{8,16},{12,4},{16,24},{20,12},{28,20},{1,9},{9,17},{13,5},{1... | collective-permute-start | bytes 147464 | tf_op jit(solution)/shard_map/ppermute | solution.py:24
  29.5 0.0 collective-permute-done.4.received_ref
  29.5 0.1 shard_map.151
  29.6 1.6 %collective-permute-done.3.blk_passed = bf16[12,2,1024]{2,1,0:T(2,128)(2,1)S(1)} collective-permute-done((bf16[12,2,1024]{2,1,0:T(2,128)(2,1)S(1)}, bf16[12,2,1024]{2,1,0:T(2,128)(2,1)S(1)}, u32[]{:S(2)}, u32[]{:S(2)}) %collective-permute-start.3) | collective-permute-done | bytes 49184 | tf_op jit(solution)/shard_map/ppermute | solution.py:24
  31.2 0.0 copy-done.1
  31.2 3.5 %shard_map.152 = (f32[1024,128]{1,0:T(8,128)S(1)}, bf16[1024,128]{1,0:T(8,128)(2,1)S(1)}, bf16[3,2,10,80,128]{4,3,2,1,0:T(8,128)(2,1)S(1)}) custom-call(bf16[8,8,1024]{2,1,0:T(8,128)(2,1)S(1)} %copy-done, bf16[2,2,8,1024]{3,2,1,0:T(8,128)(2,1)S(1)} %collective-permute-done.both_ref.rep_both, ...), custom_call_target="tpu_custom_call" | custom-call | flops 1600000000 | tf_op jit(solution)/shard_map/pallas_call | solution.py:433
  34.7 0.1 collective-permute-start.5
  34.8 0.6 collective-permute-start.7
  35.4 0.9 %collective-permute-done.5.received_ref = bf16[1024,128]{1,0:T(8,128)(2,1)S(1)} collective-permute-done((bf16[1024,128]{1,0:T(8,128)(2,1)S(1)}, bf16[1024,128]{1,0:T(8,128)(2,1)S(1)}, u32[]{:S(2)}, u32[]{:S(2)}) %collective-permute-start.5) | collective-permute-done | bytes 262176 | tf_op jit(solution)/shard_map/ppermute | solution.py:534
  36.3 0.1 shard_map.153
  36.4 0.6 collective-permute-start.6
  37.0 2.8 %shard_map.154 = (bf16[8,8,128]{2,1,0:T(8,128)(2,1)S(1)}, bf16[64,1024]{1,0:T(8,128)(2,1)}) custom-call(f32[8,4,8,256]{3,2,1,0:T(8,128)S(1)} %bitcast.7, bf16[3,2,10,80,128]{4,3,2,1,0:T(8,128)(2,1)S(1)} %get-tuple-element.44.hidden_ref, bf16[3,2,10,80,128]{4,3,2,1,0:T(8,128)(2,1)S(1)} %get-tuple-element.58.ga_ref, ...), custom_call_target="tpu_custom_call" | custom-call | flops 1600000000 | tf_op jit(solution)/shard_map/pallas_call | solution.py:433
  39.9 2.0 %collective-permute-done.7.received_two = bf16[640,128]{1,0:T(8,128)(2,1)S(1)} collective-permute-done((bf16[640,128]{1,0:T(8,128)(2,1)S(1)}, bf16[640,128]{1,0:T(8,128)(2,1)S(1)}, u32[]{:S(2)}, u32[]{:S(2)}) %collective-permute-start.7) | collective-permute-done | bytes 163872 | tf_op jit(solution)/shard_map/ppermute | solution.py:534
  41.9 2.3 %collective-permute-done.6.received_one = bf16[512,128]{1,0:T(8,128)(2,1)S(1)} collective-permute-done((bf16[512,128]{1,0:T(8,128)(2,1)S(1)}, bf16[512,128]{1,0:T(8,128)(2,1)S(1)}, u32[]{:S(2)}, u32[]{:S(2)}) %collective-permute-start.6) | collective-permute-done | bytes 131104 | tf_op jit(solution)/shard_map/ppermute | solution.py:534
  44.2 0.1 shard_map.155
  44.2 14.7 %all_to_all.15 = bf16[8,152,128]{2,1,0:T(8,128)(2,1)S(1)} all-to-all(bf16[8,152,128]{2,1,0:T(8,128)(2,1)S(1)} %shard_map.155), channel_id=1, replica_groups=mesh['blk'=8,'rep'=4] {'blk'}, dimensions={0} | all-to-all | bytes 622592 | tf_op jit(solution)/shard_map/all_to_all | solution.py:571
  59.0 12.7 %all_to_all.16.refs_0_ = bf16[8,144,128]{2,1,0:T(8,128)(2,1)S(1)} all-to-all(bf16[8,144,128]{2,1,0:T(8,128)(2,1)S(1)} %broadcast_in_dim.2), channel_id=1, replica_groups=mesh['blk'=8,'rep'=4] {'blk'}, dimensions={0} | all-to-all | bytes 589824 | tf_op jit(solution)/shard_map/all_to_all | solution.py:575
  71.8 0.9 %collective-permute-start.8 = (bf16[8,144,128]{2,1,0:T(8,128)(2,1)S(1)}, bf16[8,144,128]{2,1,0:T(8,128)(2,1)S(1)}, u32[]{:S(2)}, u32[]{:S(2)}) collective-permute-start(bf16[8,144,128]{2,1,0:T(8,128)(2,1)S(1)} %all_to_all.16.refs_0_), channel_id=1, source_target_pairs={{0,2},{1,3},{2,0},{3,1},{4,6},{5,7},{6,4},{7,5},{8,10},{9,11},{10,... | collective-permute-start | bytes 884744 | tf_op jit(solution)/shard_map/ppermute | solution.py:586
  72.7 0.0 collective-permute-start.9
  72.7 5.8 %collective-permute-done.8.refs_1_ = bf16[8,144,128]{2,1,0:T(8,128)(2,1)S(1)} collective-permute-done((bf16[8,144,128]{2,1,0:T(8,128)(2,1)S(1)}, bf16[8,144,128]{2,1,0:T(8,128)(2,1)S(1)}, u32[]{:S(2)}, u32[]{:S(2)}) %collective-permute-start.8) | collective-permute-done | bytes 294944 | tf_op jit(solution)/shard_map/ppermute | solution.py:586
  78.5 0.0 collective-permute-start.10
  78.5 0.8 shard_map.156
  79.2 0.0 collective-permute-done.9.refs_2_
  79.2 0.8 %collective-permute-done.10.refs_3_ = bf16[8,144,128]{2,1,0:T(8,128)(2,1)S(1)} collective-permute-done((bf16[8,144,128]{2,1,0:T(8,128)(2,1)S(1)}, bf16[8,144,128]{2,1,0:T(8,128)(2,1)S(1)}, u32[]{:S(2)}, u32[]{:S(2)}) %collective-permute-start.10) | collective-permute-done | bytes 294944 | tf_op jit(solution)/shard_map/ppermute | solution.py:586
  80.1 1.6 %shard_map.157 = (f32[96,2592]{1,0:T(8,128)}, f32[2592,128]{1,0:T(8,128)}) custom-call(bf16[8,144,128]{2,1,0:T(8,128)(2,1)S(1)} %all_to_all.16.refs_0_, bf16[8,144,128]{2,1,0:T(8,128)(2,1)S(1)} %collective-permute-done.8.refs_1_, bf16[8,144,128]{2,1,0:T(8,128)(2,1)S(1)} %collective-permute-done.9.refs_2_, ...), custom_call_target="tpu_custom_call" | custom-call | flops 400000000 | tf_op jit(solution)/shard_map/pallas_call | solution.py:433
  (8 shorter events, 0.2 us)
Async XLA Ops:
  0.6 9.8 %copy-start = (bf16[8,8,1024]{2,1,0:T(8,128)(2,1)S(1)}, bf16[8,8,1024]{2,1,0:T(8,128)(2,1)}, u32[]{:S(2)}) copy-start(bf16[8,8,1024]{2,1,0:T(8,128)(2,1)} %og_ref.4) | copy-start | bytes 393220
  0.6 14.8 %copy-start.4 = (bf16[2592,96]{0,1:T(8,128)(2,1)S(1)}, bf16[2592,96]{0,1:T(8,128)(2,1)}, u32[]{:S(2)}) copy-start(bf16[2592,96]{0,1:T(8,128)(2,1)} %param.19) | copy-start | bytes 1492996
  3.1 18.8 %copy-start.2 = (f32[8,96]{1,0:T(8,128)S(1)}, f32[8,96]{1,0:T(8,128)}, u32[]{:S(2)}) copy-start(f32[8,96]{1,0:T(8,128)} %weight_ref.3) | copy-start | bytes 9220
  3.1 18.8 %copy-start.3 = (f32[96]{0:T(128)S(1)}, f32[96]{0:T(128)}, u32[]{:S(2)}) copy-start(f32[96]{0:T(128)} %param.18) | copy-start | bytes 1156
  3.1 17.9 %all-to-all-start = ((f32[32,8,256]{2,1,0:T(8,128)}), f32[32,8,256]{2,1,0:T(8,128)S(1)}, u32[]{:S(2)}, u32[]{:S(2)}) async-start(f32[32,8,256]{2,1,0:T(8,128)} %shard_map.146), calls=%async_computation | async-start | bytes 524288 | tf_op jit(solution)/shard_map/all_to_all | solution.py:483
  10.5 1.3 %collective-permute-start = (bf16[2,2,8,1024]{3,2,1,0:T(8,128)(2,1)S(1)}, bf16[2,2,8,1024]{3,2,1,0:T(8,128)(2,1)S(1)}, u32[]{:S(2)}, u32[]{:S(2)}) collective-permute-start(bf16[2,2,8,1024]{3,2,1,0:T(8,128)(2,1)S(1)} %bitcast.10), channel_id=1, source_target_pairs={{0,1},{1,0},{2,3},{3,2},{4,5},{5,4},{6,7},{7,6},{8,9},{9,8},{10,11... | collective-permute-start | bytes 196616 | tf_op jit(solution)/shard_map/ppermute | solution.py:18
  11.8 5.3 %collective-permute-start.1 = (bf16[2,8,1024]{2,1,0:T(8,128)(2,1)S(1)}, bf16[2,8,1024]{2,1,0:T(8,128)(2,1)S(1)}, u32[]{:S(2)}, u32[]{:S(2)}) collective-permute-start(bf16[2,8,1024]{2,1,0:T(8,128)(2,1)S(1)} %shard_map.147), channel_id=1, source_target_pairs={{0,2},{3,1},{4,6},{7,5},{8,10},{11,9},{12,14},{15,13},{16,18},{19,... | collective-permute-start | bytes 98312 | tf_op jit(solution)/shard_map/ppermute | solution.py:24
  21.0 5.8 %collective-permute-start.2 = (bf16[2,12,2,1024]{3,2,1,0:T(2,128)(2,1)S(1)}, bf16[2,12,2,1024]{3,2,1,0:T(2,128)(2,1)S(1)}, u32[]{:S(2)}, u32[]{:S(2)}) collective-permute-start(bf16[2,12,2,1024]{3,2,1,0:T(2,128)(2,1)S(1)} %shard_map.148), channel_id=1, source_target_pairs={{0,4},{4,0},{8,12},{12,8},{16,20},{20,16},{24,28},{28,24},{1,5},{5... | collective-permute-start | bytes 294920 | tf_op jit(solution)/shard_map/ppermute | solution.py:18
  21.9 9.3 %copy-start.1 = (bf16[2592,128]{1,0:T(8,128)(2,1)S(1)}, bf16[2592,128]{1,0:T(8,128)(2,1)}, u32[]{:S(2)}) copy-start(bf16[2592,128]{1,0:T(8,128)(2,1)} %w2_ref.3) | copy-start | bytes 1990660
  26.8 2.7 %collective-permute-start.4 = (bf16[1280,128]{1,0:T(8,128)(2,1)S(1)}, bf16[1280,128]{1,0:T(8,128)(2,1)S(1)}, u32[]{:S(2)}, u32[]{:S(2)}) collective-permute-start(bf16[1280,128]{1,0:T(8,128)(2,1)S(1)} %get-tuple-element.54), channel_id=1, source_target_pairs={{0,1},{1,0},{2,3},{3,2},{4,5},{5,4},{6,7},{7,6},{8,9},{9,8},{10,11... | collective-permute-start | bytes 983048 | tf_op jit(solution)/shard_map/ppermute | solution.py:534
  26.9 4.3 %collective-permute-start.3 = (bf16[12,2,1024]{2,1,0:T(2,128)(2,1)S(1)}, bf16[12,2,1024]{2,1,0:T(2,128)(2,1)S(1)}, u32[]{:S(2)}, u32[]{:S(2)}) collective-permute-start(bf16[12,2,1024]{2,1,0:T(2,128)(2,1)S(1)} %shard_map.150), channel_id=1, source_target_pairs={{0,8},{8,16},{12,4},{16,24},{20,12},{28,20},{1,9},{9,17},{13,5},{1... | collective-permute-start | bytes 147464 | tf_op jit(solution)/shard_map/ppermute | solution.py:24
  34.7 1.6 %collective-permute-start.5 = (bf16[1024,128]{1,0:T(8,128)(2,1)S(1)}, bf16[1024,128]{1,0:T(8,128)(2,1)S(1)}, u32[]{:S(2)}, u32[]{:S(2)}) collective-permute-start(bf16[1024,128]{1,0:T(8,128)(2,1)S(1)} %get-tuple-element.63), channel_id=1, source_target_pairs={{0,1},{1,0},{2,3},{3,2},{4,5},{5,4},{6,7},{7,6},{8,9},{9,8},{10,11... | collective-permute-start | bytes 786440 | tf_op jit(solution)/shard_map/ppermute | solution.py:534
  34.8 7.1 %collective-permute-start.7 = (bf16[640,128]{1,0:T(8,128)(2,1)S(1)}, bf16[640,128]{1,0:T(8,128)(2,1)S(1)}, u32[]{:S(2)}, u32[]{:S(2)}) collective-permute-start(bf16[640,128]{1,0:T(8,128)(2,1)S(1)} %get-tuple-element.71), channel_id=1, source_target_pairs={{0,2},{1,3},{2,0},{3,1},{4,6},{5,7},{6,4},{7,5},{8,10},{9,11},{10,... | collective-permute-start | bytes 491528 | tf_op jit(solution)/shard_map/ppermute | solution.py:534
  36.4 7.8 %collective-permute-start.6 = (bf16[512,128]{1,0:T(8,128)(2,1)S(1)}, bf16[512,128]{1,0:T(8,128)(2,1)S(1)}, u32[]{:S(2)}, u32[]{:S(2)}) collective-permute-start(bf16[512,128]{1,0:T(8,128)(2,1)S(1)} %get-tuple-element.69), channel_id=1, source_target_pairs={{0,2},{1,3},{2,0},{3,1},{4,6},{5,7},{6,4},{7,5},{8,10},{9,11},{10,... | collective-permute-start | bytes 393224 | tf_op jit(solution)/shard_map/ppermute | solution.py:534
  71.8 6.7 %collective-permute-start.8 = (bf16[8,144,128]{2,1,0:T(8,128)(2,1)S(1)}, bf16[8,144,128]{2,1,0:T(8,128)(2,1)S(1)}, u32[]{:S(2)}, u32[]{:S(2)}) collective-permute-start(bf16[8,144,128]{2,1,0:T(8,128)(2,1)S(1)} %all_to_all.16.refs_0_), channel_id=1, source_target_pairs={{0,2},{1,3},{2,0},{3,1},{4,6},{5,7},{6,4},{7,5},{8,10},{9,11},{10,... | collective-permute-start | bytes 884744 | tf_op jit(solution)/shard_map/ppermute | solution.py:586
  72.7 6.5 %collective-permute-start.9 = (bf16[8,144,128]{2,1,0:T(8,128)(2,1)S(1)}, bf16[8,144,128]{2,1,0:T(8,128)(2,1)S(1)}, u32[]{:S(2)}, u32[]{:S(2)}) collective-permute-start(bf16[8,144,128]{2,1,0:T(8,128)(2,1)S(1)} %all_to_all.16.refs_0_), channel_id=1, source_target_pairs={{0,1},{1,0},{2,3},{3,2},{4,5},{5,4},{6,7},{7,6},{8,9},{9,8},{10,11... | collective-permute-start | bytes 884744 | tf_op jit(solution)/shard_map/ppermute | solution.py:586
  78.5 1.6 %collective-permute-start.10 = (bf16[8,144,128]{2,1,0:T(8,128)(2,1)S(1)}, bf16[8,144,128]{2,1,0:T(8,128)(2,1)S(1)}, u32[]{:S(2)}, u32[]{:S(2)}) collective-permute-start(bf16[8,144,128]{2,1,0:T(8,128)(2,1)S(1)} %collective-permute-done.8.refs_1_), channel_id=1, source_target_pairs={{0,1},{1,0},{2,3},{3,2},{4,5},{5,4},{6,7},{7,6},{8,9},{9,8},{10,11... | collective-permute-start | bytes 884744 | tf_op jit(solution)/shard_map/ppermute | solution.py:586

commit v6 on v5

--- a/solution.py
+++ b/solution.py
@@ -396,8 +396,8 @@
 
 
 def finish_kernel(blocks, rows_one, rows_two, width, *refs):
-    pieces = refs[:-4]
-    one_ref, two_ref, flat_one, flat_two = refs[-4:]
+    pieces = refs[:-3]
+    one_ref, two_ref, flat_one = refs[-3:]
     here, turned = lax.axis_index("rep"), 0
     count = len(pieces).bit_length() - 1
     for k in range(count):
@@ -409,11 +409,10 @@
             at = pl.multiple_of(place * rows_one, 8)
             flat_one[pl.ds(at, rows_one), :] = piece[:rows_one]
             at = pl.multiple_of(place * rows_two, 8)
-            flat_two[pl.ds(at, rows_two), :] = piece[rows_one:]
+            two_ref[pl.ds(at, rows_two), :] = piece[rows_one:]
     lanes = one_ref.shape[1]
     tiles = -(-lanes // LANES)
-    first = flat_two.shape[0]
-    two_ref[:first, :] = flat_two[...]
+    first = rows_two * blocks * len(pieces)
     two_ref[first:, :] = flat_one[tiles * width : tiles * width + two_ref.shape[0] - first, :]
     for tile in range(tiles):
         upto = min(LANES, lanes - tile * LANES)
@@ -591,7 +590,7 @@
         ),
         tuple(pieces),
         (shaped(width, taps_rows), shaped(taps_rows, LANES)),
-        scratch=[pltpu.VMEM((rows_one, LANES), f32), pltpu.VMEM((rows_two, LANES), f32)],
+        scratch=[pltpu.VMEM((rows_one, LANES), f32)],
         micros=1,
     )
     return (block_out.reshape(edge, edge, -1), attr_grad, jitter_grad, one_total.T, two_total)

time: 82.1 us -> 82 us (level)
  no operation moved by 1% of the time
where the time goes in v6:
time: 82 us; the launch traced here: 81.6 us
  blocking collectives  27.4 us (33%)
  waiting for transfers between devices  19.5 us (24%)
  starting transfers between devices  17.1 us (21%)
  Pallas kernels  15.6 us (19%)
  between operations  1.51 us (2%)
    pallas_call x12, Pallas kernels, call(): pl.pallas_call(kernel, out_shape=out_shape, in_specs=[smem] * scalars + [...  15.6 us
    all_to_all x1, blocking collectives, shards(): lax.all_to_all(message, 'blk', split_axis=0, concat_axis=0, tiled=True)  14.7 us
    all_to_all x1, blocking collectives, shards(): lax.all_to_all(spread, 'blk', split_axis=0, concat_axis=0, tiled=True)  12.7 us
    all_to_all x1, starting transfers between devices, shards(): lax.all_to_all(sent, ('blk', 'rep'), split_axis=0, concat_axis=0, tiled=T...  7.33 us
    ppermute x3, waiting for transfers between devices, shards(): pieces = pieces + [lax.ppermute(piece, 'rep', pairs) for piece in pieces]  6.6 us
    ppermute x2, starting transfers between devices, pass_on(): lax.ppermute(piece, axis, [pair for pair in pairs if 0 <= pair[1] < count])  6.23 us
    ppermute x4, waiting for transfers between devices, spread_halves(): received = lax.ppermute(moving, 'rep', pairs)  5.19 us
    all_to_all x1, waiting for transfers between devices, shards(): lax.all_to_all(sent, ('blk', 'rep'), split_axis=0, concat_axis=0, tiled=T...  3.9 us
  transfers between devices with their start and end apart: 12, of which 9 were waited for; matrix products, arithmetic and copies ran while one was open for 0% of the time, Pallas kernels for 11%

profile of v6, /device:TPU:0, one launch (start us, length us, event | category | flops | bytes accessed | tf_op | source)
XLA Modules:
  0.0 81.6 jit_solution(12541204297644030955)
XLA Ops:
  0.6 0.0 copy-start
  0.6 0.0 copy-start.4
  1.4 1.7 %shard_map.146 = f32[32,8,256]{2,1,0:T(8,128)} custom-call(s32[1,8]{1,0:T(1,128)} %counts_ref.1, f32[1,3]{1,0:T(1,128)} %jitter_ref.1, f32[1]{0:T(128)S(6)} %copy.18.yaw_ref, f32[3,512]{1,0:T(4,128)} %xyz_ref.1, f32[5,512]{1,0:T(8,128)} %attr_ref.1, s32[1,512]{1,0:T(1,128)} %bitcast.11), custom_call_target="tpu_custom_call" | custom-call | flops 400000000 | tf_op jit(solution)/shard_map/pallas_call | solution.py:432
  3.1 0.0 copy-start.2
  3.1 0.0 copy-start.3
  3.1 7.3 %all-to-all-start = ((f32[32,8,256]{2,1,0:T(8,128)}), f32[32,8,256]{2,1,0:T(8,128)S(1)}, u32[]{:S(2)}, u32[]{:S(2)}) async-start(f32[32,8,256]{2,1,0:T(8,128)} %shard_map.146), calls=%async_computation | async-start | bytes 524288 | tf_op jit(solution)/shard_map/all_to_all | solution.py:482
  10.4 0.0 copy-done
  10.5 0.3 collective-permute-start
  10.8 1.0 %collective-permute-done.both_ref.rep_both = bf16[2,2,8,1024]{3,2,1,0:T(8,128)(2,1)S(1)} collective-permute-done((bf16[2,2,8,1024]{3,2,1,0:T(8,128)(2,1)S(1)}, bf16[2,2,8,1024]{3,2,1,0:T(8,128)(2,1)S(1)}, u32[]{:S(2)}, u32[]{:S(2)}) %collective-permute-start) | collective-permute-done | bytes 65568 | tf_op jit(solution)/shard_map/ppermute | solution.py:18
  11.8 3.7 %collective-permute-start.1 = (bf16[2,8,1024]{2,1,0:T(8,128)(2,1)S(1)}, bf16[2,8,1024]{2,1,0:T(8,128)(2,1)S(1)}, u32[]{:S(2)}, u32[]{:S(2)}) collective-permute-start(bf16[2,8,1024]{2,1,0:T(8,128)(2,1)S(1)} %shard_map.147), channel_id=1, source_target_pairs={{0,2},{3,1},{4,6},{7,5},{8,10},{11,9},{12,14},{15,13},{16,18},{19,... | collective-permute-start | bytes 98312 | tf_op jit(solution)/shard_map/ppermute | solution.py:24
  15.5 0.0 copy-done.4
  15.5 0.3 copy.16.w1_ref
  15.8 1.2 %collective-permute-done.1.passed_ref.rep_passed = bf16[2,8,1024]{2,1,0:T(8,128)(2,1)S(1)} collective-permute-done((bf16[2,8,1024]{2,1,0:T(8,128)(2,1)S(1)}, bf16[2,8,1024]{2,1,0:T(8,128)(2,1)S(1)}, u32[]{:S(2)}, u32[]{:S(2)}) %collective-permute-start.1) | collective-permute-done | bytes 32800 | tf_op jit(solution)/shard_map/ppermute | solution.py:24
  17.1 3.9 %all-to-all-done = f32[32,8,256]{2,1,0:T(8,128)S(1)} async-done(((f32[32,8,256]{2,1,0:T(8,128)}), f32[32,8,256]{2,1,0:T(8,128)S(1)}, u32[]{:S(2)}, u32[]{:S(2)}) %all-to-all-start) | async-done | bytes 262176 | tf_op jit(solution)/shard_map/all_to_all | solution.py:482
  21.0 0.9 %collective-permute-start.2 = (bf16[2,12,2,1024]{3,2,1,0:T(2,128)(2,1)S(1)}, bf16[2,12,2,1024]{3,2,1,0:T(2,128)(2,1)S(1)}, u32[]{:S(2)}, u32[]{:S(2)}) collective-permute-start(bf16[2,12,2,1024]{3,2,1,0:T(2,128)(2,1)S(1)} %shard_map.148), channel_id=1, source_target_pairs={{0,4},{4,0},{8,12},{12,8},{16,20},{20,16},{24,28},{28,24},{1,5},{5... | collective-permute-start | bytes 294920 | tf_op jit(solution)/shard_map/ppermute | solution.py:18
  21.9 0.0 copy-done.2
  21.9 0.0 copy-done.3
  21.9 0.0 copy-start.1
  21.9 4.9 %shard_map.149 = (f32[1280,128]{1,0:T(8,128)S(1)}, bf16[1280,128]{1,0:T(8,128)(2,1)S(1)}, f32[32,128]{1,0:T(8,128)S(1)}, bf16[3,2,10,80,128]{4,3,2,1,0:T(8,128)(...) custom-call(f32[8,4,8,256]{3,2,1,0:T(8,128)S(1)} %bitcast.6, ...), custom_call_target="tpu_custom_call" | custom-call | flops 2000000000 | tf_op jit(solution)/shard_map/pallas_call | solution.py:432
  26.8 0.0 collective-permute-done.2.both_ref.blk_both
  26.8 0.1 collective-permute-start.4
  26.9 2.6 %collective-permute-start.3 = (bf16[12,2,1024]{2,1,0:T(2,128)(2,1)S(1)}, bf16[12,2,1024]{2,1,0:T(2,128)(2,1)S(1)}, u32[]{:S(2)}, u32[]{:S(2)}) collective-permute-start(bf16[12,2,1024]{2,1,0:T(2,128)(2,1)S(1)} %shard_map.150), channel_id=1, source_target_pairs={{0,8},{8,16},{12,4},{16,24},{20,12},{28,20},{1,9},{9,17},{13,5},{1... | collective-permute-start | bytes 147464 | tf_op jit(solution)/shard_map/ppermute | solution.py:24
  29.5 0.0 collective-permute-done.4.received_ref
  29.5 0.1 shard_map.151
  29.6 1.6 %collective-permute-done.3.blk_passed = bf16[12,2,1024]{2,1,0:T(2,128)(2,1)S(1)} collective-permute-done((bf16[12,2,1024]{2,1,0:T(2,128)(2,1)S(1)}, bf16[12,2,1024]{2,1,0:T(2,128)(2,1)S(1)}, u32[]{:S(2)}, u32[]{:S(2)}) %collective-permute-start.3) | collective-permute-done | bytes 49184 | tf_op jit(solution)/shard_map/ppermute | solution.py:24
  31.2 0.0 copy-done.1
  31.2 3.5 %shard_map.152 = (f32[1024,128]{1,0:T(8,128)S(1)}, bf16[1024,128]{1,0:T(8,128)(2,1)S(1)}, bf16[3,2,10,80,128]{4,3,2,1,0:T(8,128)(2,1)S(1)}) custom-call(bf16[8,8,1024]{2,1,0:T(8,128)(2,1)S(1)} %copy-done, bf16[2,2,8,1024]{3,2,1,0:T(8,128)(2,1)S(1)} %collective-permute-done.both_ref.rep_both, ...), custom_call_target="tpu_custom_call" | custom-call | flops 1600000000 | tf_op jit(solution)/shard_map/pallas_call | solution.py:432
  34.7 0.1 collective-permute-start.5
  34.8 0.6 collective-permute-start.7
  35.4 0.9 %collective-permute-done.5.received_ref = bf16[1024,128]{1,0:T(8,128)(2,1)S(1)} collective-permute-done((bf16[1024,128]{1,0:T(8,128)(2,1)S(1)}, bf16[1024,128]{1,0:T(8,128)(2,1)S(1)}, u32[]{:S(2)}, u32[]{:S(2)}) %collective-permute-start.5) | collective-permute-done | bytes 262176 | tf_op jit(solution)/shard_map/ppermute | solution.py:533
  36.3 0.1 shard_map.153
  36.4 0.6 collective-permute-start.6
  37.0 2.8 %shard_map.154 = (bf16[8,8,128]{2,1,0:T(8,128)(2,1)S(1)}, bf16[64,1024]{1,0:T(8,128)(2,1)}) custom-call(f32[8,4,8,256]{3,2,1,0:T(8,128)S(1)} %bitcast.7, bf16[3,2,10,80,128]{4,3,2,1,0:T(8,128)(2,1)S(1)} %get-tuple-element.44.hidden_ref, bf16[3,2,10,80,128]{4,3,2,1,0:T(8,128)(2,1)S(1)} %get-tuple-element.58.ga_ref, ...), custom_call_target="tpu_custom_call" | custom-call | flops 1600000000 | tf_op jit(solution)/shard_map/pallas_call | solution.py:432
  39.9 2.0 %collective-permute-done.7.received_two = bf16[640,128]{1,0:T(8,128)(2,1)S(1)} collective-permute-done((bf16[640,128]{1,0:T(8,128)(2,1)S(1)}, bf16[640,128]{1,0:T(8,128)(2,1)S(1)}, u32[]{:S(2)}, u32[]{:S(2)}) %collective-permute-start.7) | collective-permute-done | bytes 163872 | tf_op jit(solution)/shard_map/ppermute | solution.py:533
  41.9 2.3 %collective-permute-done.6.received_one = bf16[512,128]{1,0:T(8,128)(2,1)S(1)} collective-permute-done((bf16[512,128]{1,0:T(8,128)(2,1)S(1)}, bf16[512,128]{1,0:T(8,128)(2,1)S(1)}, u32[]{:S(2)}, u32[]{:S(2)}) %collective-permute-start.6) | collective-permute-done | bytes 131104 | tf_op jit(solution)/shard_map/ppermute | solution.py:533
  44.2 0.1 shard_map.155
  44.2 14.7 %all_to_all.15 = bf16[8,152,128]{2,1,0:T(8,128)(2,1)S(1)} all-to-all(bf16[8,152,128]{2,1,0:T(8,128)(2,1)S(1)} %shard_map.155), channel_id=1, replica_groups=mesh['blk'=8,'rep'=4] {'blk'}, dimensions={0} | all-to-all | bytes 622592 | tf_op jit(solution)/shard_map/all_to_all | solution.py:570
  59.0 12.7 %all_to_all.16.refs_0_ = bf16[8,144,128]{2,1,0:T(8,128)(2,1)S(1)} all-to-all(bf16[8,144,128]{2,1,0:T(8,128)(2,1)S(1)} %broadcast_in_dim.2), channel_id=1, replica_groups=mesh['blk'=8,'rep'=4] {'blk'}, dimensions={0} | all-to-all | bytes 589824 | tf_op jit(solution)/shard_map/all_to_all | solution.py:574
  71.8 0.9 %collective-permute-start.8 = (bf16[8,144,128]{2,1,0:T(8,128)(2,1)S(1)}, bf16[8,144,128]{2,1,0:T(8,128)(2,1)S(1)}, u32[]{:S(2)}, u32[]{:S(2)}) collective-permute-start(bf16[8,144,128]{2,1,0:T(8,128)(2,1)S(1)} %all_to_all.16.refs_0_), channel_id=1, source_target_pairs={{0,2},{1,3},{2,0},{3,1},{4,6},{5,7},{6,4},{7,5},{8,10},{9,11},{10,... | collective-permute-start | bytes 884744 | tf_op jit(solution)/shard_map/ppermute | solution.py:585
  72.7 0.0 collective-permute-start.9
  72.7 5.8 %collective-permute-done.8.refs_1_ = bf16[8,144,128]{2,1,0:T(8,128)(2,1)S(1)} collective-permute-done((bf16[8,144,128]{2,1,0:T(8,128)(2,1)S(1)}, bf16[8,144,128]{2,1,0:T(8,128)(2,1)S(1)}, u32[]{:S(2)}, u32[]{:S(2)}) %collective-permute-start.8) | collective-permute-done | bytes 294944 | tf_op jit(solution)/shard_map/ppermute | solution.py:585
  78.5 0.0 collective-permute-start.10
  78.5 0.8 shard_map.156
  79.2 0.0 collective-permute-done.9.refs_2_
  79.2 0.8 %collective-permute-done.10.refs_3_ = bf16[8,144,128]{2,1,0:T(8,128)(2,1)S(1)} collective-permute-done((bf16[8,144,128]{2,1,0:T(8,128)(2,1)S(1)}, bf16[8,144,128]{2,1,0:T(8,128)(2,1)S(1)}, u32[]{:S(2)}, u32[]{:S(2)}) %collective-permute-start.10) | collective-permute-done | bytes 294944 | tf_op jit(solution)/shard_map/ppermute | solution.py:585
  80.1 1.6 %shard_map.157 = (f32[96,2592]{1,0:T(8,128)}, f32[2592,128]{1,0:T(8,128)}) custom-call(bf16[8,144,128]{2,1,0:T(8,128)(2,1)S(1)} %all_to_all.16.refs_0_, bf16[8,144,128]{2,1,0:T(8,128)(2,1)S(1)} %collective-permute-done.8.refs_1_, bf16[8,144,128]{2,1,0:T(8,128)(2,1)S(1)} %collective-permute-done.9.refs_2_, ...), custom_call_target="tpu_custom_call" | custom-call | flops 400000000 | tf_op jit(solution)/shard_map/pallas_call | solution.py:432
  (8 shorter events, 0.2 us)
Async XLA Ops:
  0.6 9.8 %copy-start = (bf16[8,8,1024]{2,1,0:T(8,128)(2,1)S(1)}, bf16[8,8,1024]{2,1,0:T(8,128)(2,1)}, u32[]{:S(2)}) copy-start(bf16[8,8,1024]{2,1,0:T(8,128)(2,1)} %og_ref.4) | copy-start | bytes 393220
  0.6 14.8 %copy-start.4 = (bf16[2592,96]{0,1:T(8,128)(2,1)S(1)}, bf16[2592,96]{0,1:T(8,128)(2,1)}, u32[]{:S(2)}) copy-start(bf16[2592,96]{0,1:T(8,128)(2,1)} %param.19) | copy-start | bytes 1492996
  3.1 18.8 %copy-start.2 = (f32[8,96]{1,0:T(8,128)S(1)}, f32[8,96]{1,0:T(8,128)}, u32[]{:S(2)}) copy-start(f32[8,96]{1,0:T(8,128)} %weight_ref.3) | copy-start | bytes 9220
  3.1 18.8 %copy-start.3 = (f32[96]{0:T(128)S(1)}, f32[96]{0:T(128)}, u32[]{:S(2)}) copy-start(f32[96]{0:T(128)} %param.18) | copy-start | bytes 1156
  3.1 17.9 %all-to-all-start = ((f32[32,8,256]{2,1,0:T(8,128)}), f32[32,8,256]{2,1,0:T(8,128)S(1)}, u32[]{:S(2)}, u32[]{:S(2)}) async-start(f32[32,8,256]{2,1,0:T(8,128)} %shard_map.146), calls=%async_computation | async-start | bytes 524288 | tf_op jit(solution)/shard_map/all_to_all | solution.py:482
  10.5 1.3 %collective-permute-start = (bf16[2,2,8,1024]{3,2,1,0:T(8,128)(2,1)S(1)}, bf16[2,2,8,1024]{3,2,1,0:T(8,128)(2,1)S(1)}, u32[]{:S(2)}, u32[]{:S(2)}) collective-permute-start(bf16[2,2,8,1024]{3,2,1,0:T(8,128)(2,1)S(1)} %bitcast.10), channel_id=1, source_target_pairs={{0,1},{1,0},{2,3},{3,2},{4,5},{5,4},{6,7},{7,6},{8,9},{9,8},{10,11... | collective-permute-start | bytes 196616 | tf_op jit(solution)/shard_map/ppermute | solution.py:18
  11.8 5.3 %collective-permute-start.1 = (bf16[2,8,1024]{2,1,0:T(8,128)(2,1)S(1)}, bf16[2,8,1024]{2,1,0:T(8,128)(2,1)S(1)}, u32[]{:S(2)}, u32[]{:S(2)}) collective-permute-start(bf16[2,8,1024]{2,1,0:T(8,128)(2,1)S(1)} %shard_map.147), channel_id=1, source_target_pairs={{0,2},{3,1},{4,6},{7,5},{8,10},{11,9},{12,14},{15,13},{16,18},{19,... | collective-permute-start | bytes 98312 | tf_op jit(solution)/shard_map/ppermute | solution.py:24
  21.0 5.8 %collective-permute-start.2 = (bf16[2,12,2,1024]{3,2,1,0:T(2,128)(2,1)S(1)}, bf16[2,12,2,1024]{3,2,1,0:T(2,128)(2,1)S(1)}, u32[]{:S(2)}, u32[]{:S(2)}) collective-permute-start(bf16[2,12,2,1024]{3,2,1,0:T(2,128)(2,1)S(1)} %shard_map.148), channel_id=1, source_target_pairs={{0,4},{4,0},{8,12},{12,8},{16,20},{20,16},{24,28},{28,24},{1,5},{5... | collective-permute-start | bytes 294920 | tf_op jit(solution)/shard_map/ppermute | solution.py:18
  21.9 9.3 %copy-start.1 = (bf16[2592,128]{1,0:T(8,128)(2,1)S(1)}, bf16[2592,128]{1,0:T(8,128)(2,1)}, u32[]{:S(2)}) copy-start(bf16[2592,128]{1,0:T(8,128)(2,1)} %w2_ref.3) | copy-start | bytes 1990660
  26.8 2.7 %collective-permute-start.4 = (bf16[1280,128]{1,0:T(8,128)(2,1)S(1)}, bf16[1280,128]{1,0:T(8,128)(2,1)S(1)}, u32[]{:S(2)}, u32[]{:S(2)}) collective-permute-start(bf16[1280,128]{1,0:T(8,128)(2,1)S(1)} %get-tuple-element.54), channel_id=1, source_target_pairs={{0,1},{1,0},{2,3},{3,2},{4,5},{5,4},{6,7},{7,6},{8,9},{9,8},{10,11... | collective-permute-start | bytes 983048 | tf_op jit(solution)/shard_map/ppermute | solution.py:533
  26.9 4.3 %collective-permute-start.3 = (bf16[12,2,1024]{2,1,0:T(2,128)(2,1)S(1)}, bf16[12,2,1024]{2,1,0:T(2,128)(2,1)S(1)}, u32[]{:S(2)}, u32[]{:S(2)}) collective-permute-start(bf16[12,2,1024]{2,1,0:T(2,128)(2,1)S(1)} %shard_map.150), channel_id=1, source_target_pairs={{0,8},{8,16},{12,4},{16,24},{20,12},{28,20},{1,9},{9,17},{13,5},{1... | collective-permute-start | bytes 147464 | tf_op jit(solution)/shard_map/ppermute | solution.py:24
  34.7 1.6 %collective-permute-start.5 = (bf16[1024,128]{1,0:T(8,128)(2,1)S(1)}, bf16[1024,128]{1,0:T(8,128)(2,1)S(1)}, u32[]{:S(2)}, u32[]{:S(2)}) collective-permute-start(bf16[1024,128]{1,0:T(8,128)(2,1)S(1)} %get-tuple-element.63), channel_id=1, source_target_pairs={{0,1},{1,0},{2,3},{3,2},{4,5},{5,4},{6,7},{7,6},{8,9},{9,8},{10,11... | collective-permute-start | bytes 786440 | tf_op jit(solution)/shard_map/ppermute | solution.py:533
  34.8 7.1 %collective-permute-start.7 = (bf16[640,128]{1,0:T(8,128)(2,1)S(1)}, bf16[640,128]{1,0:T(8,128)(2,1)S(1)}, u32[]{:S(2)}, u32[]{:S(2)}) collective-permute-start(bf16[640,128]{1,0:T(8,128)(2,1)S(1)} %get-tuple-element.71), channel_id=1, source_target_pairs={{0,2},{1,3},{2,0},{3,1},{4,6},{5,7},{6,4},{7,5},{8,10},{9,11},{10,... | collective-permute-start | bytes 491528 | tf_op jit(solution)/shard_map/ppermute | solution.py:533
  36.4 7.8 %collective-permute-start.6 = (bf16[512,128]{1,0:T(8,128)(2,1)S(1)}, bf16[512,128]{1,0:T(8,128)(2,1)S(1)}, u32[]{:S(2)}, u32[]{:S(2)}) collective-permute-start(bf16[512,128]{1,0:T(8,128)(2,1)S(1)} %get-tuple-element.69), channel_id=1, source_target_pairs={{0,2},{1,3},{2,0},{3,1},{4,6},{5,7},{6,4},{7,5},{8,10},{9,11},{10,... | collective-permute-start | bytes 393224 | tf_op jit(solution)/shard_map/ppermute | solution.py:533
  71.8 6.7 %collective-permute-start.8 = (bf16[8,144,128]{2,1,0:T(8,128)(2,1)S(1)}, bf16[8,144,128]{2,1,0:T(8,128)(2,1)S(1)}, u32[]{:S(2)}, u32[]{:S(2)}) collective-permute-start(bf16[8,144,128]{2,1,0:T(8,128)(2,1)S(1)} %all_to_all.16.refs_0_), channel_id=1, source_target_pairs={{0,2},{1,3},{2,0},{3,1},{4,6},{5,7},{6,4},{7,5},{8,10},{9,11},{10,... | collective-permute-start | bytes 884744 | tf_op jit(solution)/shard_map/ppermute | solution.py:585
  72.7 6.5 %collective-permute-start.9 = (bf16[8,144,128]{2,1,0:T(8,128)(2,1)S(1)}, bf16[8,144,128]{2,1,0:T(8,128)(2,1)S(1)}, u32[]{:S(2)}, u32[]{:S(2)}) collective-permute-start(bf16[8,144,128]{2,1,0:T(8,128)(2,1)S(1)} %all_to_all.16.refs_0_), channel_id=1, source_target_pairs={{0,1},{1,0},{2,3},{3,2},{4,5},{5,4},{6,7},{7,6},{8,9},{9,8},{10,11... | collective-permute-start | bytes 884744 | tf_op jit(solution)/shard_map/ppermute | solution.py:585
  78.5 1.6 %collective-permute-start.10 = (bf16[8,144,128]{2,1,0:T(8,128)(2,1)S(1)}, bf16[8,144,128]{2,1,0:T(8,128)(2,1)S(1)}, u32[]{:S(2)}, u32[]{:S(2)}) collective-permute-start(bf16[8,144,128]{2,1,0:T(8,128)(2,1)S(1)} %collective-permute-done.8.refs_1_), channel_id=1, source_target_pairs={{0,1},{1,0},{2,3},{3,2},{4,5},{5,4},{6,7},{7,6},{8,9},{9,8},{10,11... | collective-permute-start | bytes 884744 | tf_op jit(solution)/shard_map/ppermute | solution.py:585
